TPU v7x, 32 devices: a whole 2x2x4 slice. The times are simulated.
32 devices in a mesh: gx: 4 (over y, core), gy: 2 (over x), gz: 4 (over z).
Axes of the slice: x: 2, y: 2, z: 4, core: 2. Of those that a mesh axis runs over, the one named last changes fastest.
Arguments:
- charges: float32 [16, 8, 32, 128], P('gx', 'gy', 'gz'), may hold values from -6 to 6
- offset_x: float32 [16, 8, 32, 128], P('gx', 'gy', 'gz'), may hold values from 0 to 4
- offset_y: float32 [16, 8, 32, 128], P('gx', 'gy', 'gz'), may hold values from 0 to 4
- offset_z: float32 [16, 8, 32, 128], P('gx', 'gy', 'gz'), may hold values from 0 to 2
- counts: int32 [16, 8, 32], P('gx', 'gy', 'gz'), may hold values from 32 to 128
Outputs:
- fine_potential: float32 [64, 32, 64], P('gx', 'gy', 'gz')
- atom_potential: float32 [16, 8, 32, 128], P('gx', 'gy', 'gz')
Inputs may be any that keep to these rules, and one draw needn't show every extreme that they name: `counts`: slots at or beyond a bin's count are padding and hold no atom.
All inputs are finite; a program needn't handle non-finite values.
Results may differ from a plain program's by a relative error of at most 0.0003.
Values sent between devices are 32-bit elements; how exact they have to be, the bound alone decides.
No kernel may reach another device: no remote copies, remote signals or barrier semaphores. Data moves between devices by JAX's collectives and lax.ppermute only.
A program may use at most 64 MiB of HBM per device.

v0:
```python
import math

import jax
import jax.numpy as jnp
from jax import lax
from jax.sharding import PartitionSpec as P

R = 8


highest = lax.Precision.HIGHEST
restrict_taps = (-0.0625, 0.0, 0.5625, 1.0, 0.5625, 0.0, -0.0625)


def with_halo(block, sides, width):
    for axis, dim in sides:
        count = lax.axis_size(axis)
        forward = [(i, i + 1) for i in range(count - 1)]
        backward = [(target, source) for source, target in forward]
        low = lax.ppermute(
            lax.slice_in_dim(block, block.shape[dim] - width, None, axis=dim), axis, forward
        )
        high = lax.ppermute(lax.slice_in_dim(block, 0, width, axis=dim), axis, backward)
        block = jnp.concatenate([low, block, high], axis=dim)
    return block


def profile_value(family, offset, reach):
    if family == 0:
        return math.exp(-((offset / (0.4 * reach)) ** 2))
    if family == 1:
        return math.exp(-((offset / (0.8 * reach)) ** 2))
    return 1.0 / (1.0 + (offset / reach) ** 2)


def profile_array(family, offset, reach):
    if family == 0:
        return jnp.exp(-((offset / (0.4 * reach)) ** 2))
    if family == 1:
        return jnp.exp(-((offset / (0.8 * reach)) ** 2))
    return 1.0 / (1.0 + (offset / reach) ** 2)


def norm_factor(family, reach):
    return (
        sum(
            (
                profile_value(family, float(offset), reach) ** 2
                for offset in range(-reach, reach + 1)
            )
        )
        ** 1.5
    )


def bspline(spacing):
    magnitude = jnp.abs(spacing)
    inner = 2.0 / 3.0 - magnitude * magnitude + 0.5 * magnitude * magnitude * magnitude
    outer = (2.0 - magnitude) ** 3 / 6.0
    return jnp.where(magnitude < 1.0, inner, jnp.where(magnitude < 2.0, outer, 0.0))


def spline_weights(along_x, along_y, along_z):
    weight_x = bspline(along_x[..., None] + 2.0 - jnp.arange(8).astype(jnp.float32))
    weight_y = bspline(along_y[..., None] + 2.0 - jnp.arange(8).astype(jnp.float32))
    weight_z = bspline(along_z[..., None] + 2.0 - jnp.arange(6).astype(jnp.float32))
    return (weight_x, weight_y, weight_z)


def spread_patches(weighted, offset_x, offset_y, offset_z):

    def spread_one_slab(items):
        slab_charge, slab_x, slab_y, slab_z = items
        weight_x, weight_y, weight_z = spline_weights(slab_x, slab_y, slab_z)
        outer = (slab_charge[..., None] * weight_x)[..., :, None] * weight_y[..., None, :]
        return jnp.einsum("bcsxy,bcsz->bcxyz", outer, weight_z, precision=highest)

    return lax.map(spread_one_slab, (weighted, offset_x, offset_y, offset_z))


def place_patches(patches):
    nbins_x, nbins_y, nbins_z = patches.shape[:3]
    summed = jnp.zeros((4 * nbins_x + 4, 4 * nbins_y + 4, 2 * nbins_z + 4), jnp.float32)
    for shift_x in range(2):
        for shift_y in range(2):
            for shift_z in range(3):
                portion = patches[
                    :,
                    :,
                    :,
                    4 * shift_x : 4 * shift_x + 4,
                    4 * shift_y : 4 * shift_y + 4,
                    2 * shift_z : 2 * shift_z + 2,
                ]
                portion = jnp.transpose(portion, (0, 3, 1, 4, 2, 5)).reshape(
                    4 * nbins_x, 4 * nbins_y, 2 * nbins_z
                )
                summed = summed + jnp.pad(
                    portion,
                    (
                        (4 * shift_x, 4 - 4 * shift_x),
                        (4 * shift_y, 4 - 4 * shift_y),
                        (2 * shift_z, 4 - 2 * shift_z),
                    ),
                )
    return summed


def collect_patches(padded, nbins_x, nbins_y, nbins_z):
    blocks = padded.reshape(nbins_x + 1, 4, nbins_y + 1, 4, nbins_z + 2, 2)
    rows_x = []
    for shift_x in range(2):
        rows_y = []
        for shift_y in range(2):
            rows_z = []
            for shift_z in range(3):
                piece = blocks[
                    shift_x : shift_x + nbins_x,
                    :,
                    shift_y : shift_y + nbins_y,
                    :,
                    shift_z : shift_z + nbins_z,
                    :,
                ]
                rows_z.append(jnp.transpose(piece, (0, 2, 4, 1, 3, 5)))
            rows_y.append(jnp.concatenate(rows_z, axis=5))
        rows_x.append(jnp.concatenate(rows_y, axis=4))
    return jnp.concatenate(rows_x, axis=3)


def interpolate(patches, offset_x, offset_y, offset_z):

    def interpolate_one_slab(items):
        slab_values, slab_x, slab_y, slab_z = items
        weight_x, weight_y, weight_z = spline_weights(slab_x, slab_y, slab_z)
        partial_sum = jnp.einsum("bcxyz,bcsz->bcsxy", slab_values, weight_z, precision=highest)
        return jnp.einsum(
            "bcsxy,bcsx,bcsy->bcs", partial_sum, weight_x, weight_y, precision=highest
        )

    return lax.map(interpolate_one_slab, (patches, offset_x, offset_y, offset_z))


def fold_axis(values, axis_index, length):
    inside = lax.slice_in_dim(values, 6, 6 + length, axis=axis_index)
    from_low = lax.slice_in_dim(values, 2, 4, axis=axis_index)
    from_high = lax.slice_in_dim(values, length + 8, length + 10, axis=axis_index)
    front = lax.slice_in_dim(inside, 0, 2, axis=axis_index) + from_low
    middle = lax.slice_in_dim(inside, 2, length - 2, axis=axis_index)
    back = lax.slice_in_dim(inside, length - 2, length, axis=axis_index) + from_high
    return jnp.concatenate([front, middle, back], axis=axis_index)


def ghost_cells(field, width):
    return with_halo(field, (("gx", 0), ("gy", 1), ("gz", 2)), width)


def stencil_matrix(length, width, family):
    rows = jnp.arange(length)[:, None]
    columns = jnp.arange(length + 2 * width)[None, :]
    offset = columns - width - rows
    return jnp.where(
        jnp.abs(offset) <= R, profile_array(family, offset.astype(jnp.float32), R), 0.0
    )


def restrict_matrix(length_out, length_in, width):
    rows = jnp.arange(length_out)[:, None]
    columns = jnp.arange(length_in)[None, :]
    taps = columns - width - 2 * rows + 3
    matrix = jnp.zeros((length_out, length_in), jnp.float32)
    for position, weight in enumerate(restrict_taps):
        matrix = matrix + jnp.where(taps == position, weight, 0.0)
    return matrix


def prolong_matrix(length_out, length_in, width):
    rows = jnp.arange(length_out)[:, None]
    columns = jnp.arange(length_in)[None, :]
    taps = rows - 2 * (columns - width) + 3
    matrix = jnp.zeros((length_out, length_in), jnp.float32)
    for position, weight in enumerate(restrict_taps):
        matrix = matrix + jnp.where(taps == position, weight, 0.0)
    return matrix


def coarse_matrix(length_out, length_in, start):
    rows = jnp.arange(length_out)[:, None]
    columns = jnp.arange(length_in)[None, :]
    return profile_array(2, (columns - start - rows).astype(jnp.float32), R)


def apply_three(values, along_x, along_y, along_z):
    values = jnp.einsum("ia,abc->ibc", along_x, values, precision=highest)
    values = jnp.einsum("jb,ibc->ijc", along_y, values, precision=highest)
    return jnp.einsum("kc,ijc->ijk", along_z, values, precision=highest)


def level_stencil(extended, shape, width, scale):
    result = jnp.zeros(shape, jnp.float32)
    for family in (0, 1):
        term = apply_three(
            extended,
            stencil_matrix(shape[0], width, family),
            stencil_matrix(shape[1], width, family),
            stencil_matrix(shape[2], width, family),
        )
        result = result + scale / norm_factor(family, R) * term
    return result


def restrict_level(extended, shape, width):
    return apply_three(
        extended,
        restrict_matrix(shape[0] // 2, shape[0] + 2 * width, width),
        restrict_matrix(shape[1] // 2, shape[1] + 2 * width, width),
        restrict_matrix(shape[2] // 2, shape[2] + 2 * width, width),
    )


def prolong_level(extended, shape_coarse):
    return apply_three(
        extended,
        prolong_matrix(2 * shape_coarse[0], shape_coarse[0] + 4, 2),
        prolong_matrix(2 * shape_coarse[1], shape_coarse[1] + 4, 2),
        prolong_matrix(2 * shape_coarse[2], shape_coarse[2] + 4, 2),
    )


def body(charges, offset_x, offset_y, offset_z, counts):
    nbins_x, nbins_y, nbins_z, slot_count = charges.shape
    shape_one = (4 * nbins_x, 4 * nbins_y, 2 * nbins_z)
    present = jnp.arange(slot_count)[None, None, None, :] < counts[..., None]
    weighted = jnp.where(present, charges, 0.0)
    spread = place_patches(spread_patches(weighted, offset_x, offset_y, offset_z))
    rims = with_halo(spread, (("gx", 0), ("gy", 1), ("gz", 2)), 4)
    charge_one = fold_axis(
        fold_axis(fold_axis(rims, 0, shape_one[0]), 1, shape_one[1]), 2, shape_one[2]
    )
    width = max(R, 3)
    extended_one = ghost_cells(charge_one, width)
    direct_one = level_stencil(extended_one, shape_one, width, 1.0)
    charge_two = restrict_level(extended_one, shape_one, width)
    shape_two = charge_two.shape
    extended_two = ghost_cells(charge_two, width)
    direct_two = level_stencil(extended_two, shape_two, width, 0.5)
    charge_three = restrict_level(extended_two, shape_two, width)
    size_a, size_b, size_c = charge_three.shape
    devices_x, devices_y, devices_z = (
        lax.axis_size("gx"),
        lax.axis_size("gy"),
        lax.axis_size("gz"),
    )
    matrix_x = coarse_matrix(size_a, size_a * devices_x, lax.axis_index("gx") * size_a)
    matrix_y = coarse_matrix(size_b, size_b * devices_y, lax.axis_index("gy") * size_b)
    matrix_z = coarse_matrix(size_c, size_c * devices_z, lax.axis_index("gz") * size_c)
    zeros_block = jnp.zeros((size_a, size_b, size_c), jnp.float32)

    def along_z(carry, piece, start):
        return jnp.einsum("kc,abc->abk", matrix_z, piece, precision=highest)

    def along_y(carry, piece, start):
        return jnp.einsum("jb,abk->ajk", matrix_y, piece, precision=highest)

    def along_x(carry, piece, start):
        return jnp.einsum("ia,ajk->ijk", matrix_x, piece, precision=highest)

    section_one = along_z(
        zeros_block, lax.all_gather(charge_three, "gz", axis=2, tiled=True), jnp.int32(0)
    )
    section_two = along_y(
        zeros_block, lax.all_gather(section_one, "gy", axis=1, tiled=True), jnp.int32(0)
    )
    far = along_x(zeros_block, lax.all_gather(section_two, "gx", axis=0, tiled=True), jnp.int32(0))
    far = far * (0.5 / norm_factor(2, R))
    potential_two = direct_two + prolong_level(ghost_cells(far, 2), far.shape)
    fine_potential = direct_one + prolong_level(ghost_cells(potential_two, 2), shape_two)
    padded = ghost_cells(fine_potential, 2)
    patches = collect_patches(padded, nbins_x, nbins_y, nbins_z)
    atom_potential = jnp.where(present, interpolate(patches, offset_x, offset_y, offset_z), 0.0)
    return (fine_potential, atom_potential)


def solution(mesh):
    in_specs = (
        P("gx", "gy", "gz", None),
        P("gx", "gy", "gz", None),
        P("gx", "gy", "gz", None),
        P("gx", "gy", "gz", None),
        P("gx", "gy", "gz"),
    )
    out_specs = (P("gx", "gy", "gz"), P("gx", "gy", "gz", None))
    return jax.shard_map(body, mesh=mesh, in_specs=in_specs, out_specs=out_specs, check_vma=False)
```

profile of v0, /device:TPU:0, one launch (start us, length us, event | category | flops | bytes accessed | tf_op | source)
XLA Modules:
  0.0 346.2 jit_solution(17432847150455806383)
XLA Ops:
  1.6 15.2 %while.22 = (s32[]{:T(128)}, f32[4,4,8,8,8,6]{5,4,3,2,1,0:T(8,128)}, f32[4,4,8,128]{3,2,1,0:T(8,128)S(1)}, f32[4,4,8,128]{3,2,1,0:T(8,128)}, f32[4,4,8,128]{3,2,1,0:T(8,128)}, /*index=5*/f32[4,4,8,128]{3,2,1,0:T(8,128)}) while((s32[]{:T(128)}, f32[4,4,8,8,8,6]{5,4,3,2,1,0:T(8,128)}, f32[4,4,8,128]{3,2,1,0:T(8,128)S(1)}, ...), condition=%wide.region_1.2_spmd.clone, body=%wide.region_0.1_spmd.sunk.clone | while | flops 20623376 | bytes 1770173 | solution.py:78
  16.8 14.4 %slice_bitcast_fusion.11 = (f32[4,4,4,4,8,2]{5,3,1,4,2,0:T(4,128)}, f32[4,4,4,4,8,2]{5,3,1,4,2,0:T(4,128)S(1)}, f32[4,4,4,4,8,2]{5,3,1,4,2,0:T(4,128)S(1)}, f32[...) fusion(f32[4,4,8,8,8,6]{5,4,3,2,1,0:T(8,128)} %get-tuple-element.66), kind=kLoop, calls=%fused_computation.156 | loop fusion | bytes 393216 | tf_op jit(solution)/shard_map/transpose | solution.py:95
  31.2 5.1 %copy.180 = f32[4,4,4,4,8,2]{3,2,5,4,1,0:T(4,128)} copy(f32[4,4,4,4,8,2]{5,3,1,4,2,0:T(4,128)} %get-tuple-element.130) | data formatting | bytes 32768 | tf_op jit(solution)/shard_map/transpose | solution.py:95
  37.8 5.1 %copy.182 = f32[4,4,4,4,8,2]{3,2,5,4,1,0:T(4,128)} copy(f32[4,4,4,4,8,2]{5,3,1,4,2,0:T(4,128)} %get-tuple-element.141) | data formatting | bytes 32768 | tf_op jit(solution)/shard_map/transpose | solution.py:95
  44.3 5.1 %copy.184 = f32[4,4,4,4,8,2]{3,2,5,4,1,0:T(4,128)} copy(f32[4,4,4,4,8,2]{5,3,1,4,2,0:T(4,128)} %get-tuple-element.140) | data formatting | bytes 32768 | tf_op jit(solution)/shard_map/transpose | solution.py:95
  52.4 5.1 %copy.186 = f32[4,4,4,4,8,2]{3,2,5,4,1,0:T(4,128)} copy(f32[4,4,4,4,8,2]{5,3,1,4,2,0:T(4,128)} %get-tuple-element.139) | data formatting | bytes 32768 | tf_op jit(solution)/shard_map/transpose | solution.py:95
  61.2 5.1 %copy.188 = f32[4,4,4,4,8,2]{3,2,5,4,1,0:T(4,128)} copy(f32[4,4,4,4,8,2]{5,3,1,4,2,0:T(4,128)} %get-tuple-element.138) | data formatting | bytes 32768 | tf_op jit(solution)/shard_map/transpose | solution.py:95
  69.9 5.1 %copy.190 = f32[4,4,4,4,8,2]{3,2,5,4,1,0:T(4,128)} copy(f32[4,4,4,4,8,2]{5,3,1,4,2,0:T(4,128)} %get-tuple-element.137) | data formatting | bytes 32768 | tf_op jit(solution)/shard_map/transpose | solution.py:95
  78.7 5.1 %copy.192 = f32[4,4,4,4,8,2]{3,2,5,4,1,0:T(4,128)} copy(f32[4,4,4,4,8,2]{5,3,1,4,2,0:T(4,128)} %get-tuple-element.136) | data formatting | bytes 32768 | tf_op jit(solution)/shard_map/transpose | solution.py:95
  87.4 5.1 %copy.194 = f32[4,4,4,4,8,2]{3,2,5,4,1,0:T(4,128)} copy(f32[4,4,4,4,8,2]{5,3,1,4,2,0:T(4,128)} %get-tuple-element.135) | data formatting | bytes 32768 | tf_op jit(solution)/shard_map/transpose | solution.py:95
  96.2 5.1 %copy.196 = f32[4,4,4,4,8,2]{3,2,5,4,1,0:T(4,128)} copy(f32[4,4,4,4,8,2]{5,3,1,4,2,0:T(4,128)} %get-tuple-element.134) | data formatting | bytes 32768 | tf_op jit(solution)/shard_map/transpose | solution.py:95
  104.9 4.1 %copy.198 = f32[4,4,4,4,8,2]{3,2,5,4,1,0:T(4,128)} copy(f32[4,4,4,4,8,2]{5,3,1,4,2,0:T(4,128)S(1)} %get-tuple-element.133) | data formatting | bytes 32768 | tf_op jit(solution)/shard_map/transpose | solution.py:95
  131.7 4.3 %collective-permute-done.3 = f32[28,4,20]{2,0,1:T(8,128)S(1)} collective-permute-done((f32[28,4,20]{2,0,1:T(8,128)S(1)}, f32[28,4,20]{2,0,1:T(8,128)S(1)}, u32[]{:S(2)}, u32[]{:S(2)}) %collective-permute-start.3) | collective-permute-done | bytes 8992 | tf_op jit(solution)/shard_map/ppermute | solution.py:23
  141.1 9.2 %collective-permute-done.4 = f32[28,28,4]{2,0,1:T(8,128)S(1)} collective-permute-done((f32[28,28,4]{2,0,1:T(8,128)S(1)}, f32[28,28,4]{2,0,1:T(8,128)S(1)}, u32[]{:S(2)}, u32[]{:S(2)}) %collective-permute-start.4) | collective-permute-done | bytes 12576 | tf_op jit(solution)/shard_map/ppermute | solution.py:20
  150.3 4.7 %collective-permute-done.5 = f32[28,28,4]{2,0,1:T(8,128)S(1)} collective-permute-done((f32[28,28,4]{2,0,1:T(8,128)S(1)}, f32[28,28,4]{2,0,1:T(8,128)S(1)}, u32[]{:S(2)}, u32[]{:S(2)}) %collective-permute-start.5) | collective-permute-done | bytes 12576 | tf_op jit(solution)/shard_map/ppermute | solution.py:23
  165.7 4.4 %collective-permute-done.9 = f32[32,8,16]{2,0,1:T(8,128)S(1)} collective-permute-done((f32[32,8,16]{2,0,1:T(8,128)S(1)}, f32[32,8,16]{2,0,1:T(8,128)S(1)}, u32[]{:S(2)}, u32[]{:S(2)}) %collective-permute-start.9) | collective-permute-done | bytes 16416 | tf_op jit(solution)/shard_map/ppermute | solution.py:23
  175.2 10.6 %collective-permute-done.10 = f32[32,32,8]{2,0,1:T(8,128)S(1)} collective-permute-done((f32[32,32,8]{2,0,1:T(8,128)S(1)}, f32[32,32,8]{2,0,1:T(8,128)S(1)}, u32[]{:S(2)}, u32[]{:S(2)}) %collective-permute-start.10) | collective-permute-done | bytes 32800 | tf_op jit(solution)/shard_map/ppermute | solution.py:20
  185.8 4.7 %collective-permute-done.11 = f32[32,32,8]{2,0,1:T(8,128)S(1)} collective-permute-done((f32[32,32,8]{2,0,1:T(8,128)S(1)}, f32[32,32,8]{2,0,1:T(8,128)S(1)}, u32[]{:S(2)}, u32[]{:S(2)}) %collective-permute-start.11) | collective-permute-done | bytes 32800 | tf_op jit(solution)/shard_map/ppermute | solution.py:23
  200.8 4.3 %collective-permute-done.15 = f32[24,8,8]{1,2,0:T(8,128)S(1)} collective-permute-done((f32[24,8,8]{1,2,0:T(8,128)S(1)}, f32[24,8,8]{1,2,0:T(8,128)S(1)}, u32[]{:S(2)}, u32[]{:S(2)}) %collective-permute-start.15) | collective-permute-done | bytes 6176 | tf_op jit(solution)/shard_map/ppermute | solution.py:23
  211.9 4.2 %collective-permute-done.17 = f32[24,24,8]{1,2,0:T(8,128)S(1)} collective-permute-done((f32[24,24,8]{1,2,0:T(8,128)S(1)}, f32[24,24,8]{1,2,0:T(8,128)S(1)}, u32[]{:S(2)}, u32[]{:S(2)}) %collective-permute-start.17) | collective-permute-done | bytes 18464 | tf_op jit(solution)/shard_map/ppermute | solution.py:23
  217.8 13.1 %all_gather.9 = f32[4,4,16]{1,0,2:T(4,128)S(1)} all-gather(f32[4,4,4]{1,0,2:T(4,128)S(1)} %copy.213), channel_id=1, replica_groups=mesh['gx'=4,'gy'=2,'gz'=4] {'gz'}, dimensions={2}, use_global_device_ids=true | all-gather | bytes 1280 | tf_op jit(solution)/shard_map/all_gather | solution.py:269
  231.2 4.4 %all_gather.10 = f32[4,8,4]{2,0,1:T(4,128)S(1)} all-gather(f32[4,4,4]{2,0,1:T(4,128)S(1)} %fusion.192), channel_id=1, replica_groups=mesh['gx'=4,'gy'=2,'gz'=4] {'gy'}, dimensions={1}, use_global_device_ids=true | all-gather | bytes 768 | tf_op jit(solution)/shard_map/all_gather | solution.py:272
  235.9 5.2 %all_gather.11 = f32[16,4,4]{2,1,0:T(4,128)S(1)} all-gather(f32[4,4,4]{2,1,0:T(4,128)S(1)} %copy.217), channel_id=1, replica_groups=mesh['gx'=4,'gy'=2,'gz'=4] {'gx'}, dimensions={0}, use_global_device_ids=true | all-gather | bytes 1280 | tf_op jit(solution)/shard_map/all_gather | solution.py:274
  250.7 4.1 %collective-permute-done.21 = f32[8,2,4]{2,0,1:T(8,128)S(1)} collective-permute-done((f32[8,2,4]{2,0,1:T(8,128)S(1)}, f32[8,2,4]{2,0,1:T(8,128)S(1)}, u32[]{:S(2)}, u32[]{:S(2)}) %collective-permute-start.21) | collective-permute-done | bytes 288 | tf_op jit(solution)/shard_map/ppermute | solution.py:23
  257.8 4.5 %collective-permute-done.23 = f32[8,8,2]{2,0,1:T(8,128)S(1)} collective-permute-done((f32[8,8,2]{2,0,1:T(8,128)S(1)}, f32[8,8,2]{2,0,1:T(8,128)S(1)}, u32[]{:S(2)}, u32[]{:S(2)}) %collective-permute-start.23) | collective-permute-done | bytes 544 | tf_op jit(solution)/shard_map/ppermute | solution.py:23
  272.9 4.0 %collective-permute-done.27 = f32[12,2,8]{2,1,0:T(2,128)S(1)} collective-permute-done((f32[12,2,8]{2,1,0:T(2,128)S(1)}, f32[12,2,8]{2,1,0:T(2,128)S(1)}, u32[]{:S(2)}, u32[]{:S(2)}) %collective-permute-start.27) | collective-permute-done | bytes 800 | tf_op jit(solution)/shard_map/ppermute | solution.py:23
  283.8 4.1 %collective-permute-done.29 = f32[12,12,2]{2,1,0:T(8,128)S(1)} collective-permute-done((f32[12,12,2]{2,1,0:T(8,128)S(1)}, f32[12,12,2]{2,1,0:T(8,128)S(1)}, u32[]{:S(2)}, u32[]{:S(2)}) %collective-permute-start.29) | collective-permute-done | bytes 1184 | tf_op jit(solution)/shard_map/ppermute | solution.py:23
  298.5 4.2 %collective-permute-done.33 = f32[20,2,16]{2,1,0:T(2,128)S(1)} collective-permute-done((f32[20,2,16]{2,1,0:T(2,128)S(1)}, f32[20,2,16]{2,1,0:T(2,128)S(1)}, u32[]{:S(2)}, u32[]{:S(2)}) %collective-permute-start.33) | collective-permute-done | bytes 2592 | tf_op jit(solution)/shard_map/ppermute | solution.py:23
  306.1 4.9 %collective-permute-done.34 = f32[20,20,2]{2,1,0:T(8,128)S(1)} collective-permute-done((f32[20,20,2]{2,1,0:T(8,128)S(1)}, f32[20,20,2]{2,1,0:T(8,128)S(1)}, u32[]{:S(2)}, u32[]{:S(2)}) %collective-permute-start.34) | collective-permute-done | bytes 3232 | tf_op jit(solution)/shard_map/ppermute | solution.py:20
  311.0 4.3 %collective-permute-done.35 = f32[20,20,2]{2,1,0:T(8,128)S(1)} collective-permute-done((f32[20,20,2]{2,1,0:T(8,128)S(1)}, f32[20,20,2]{2,1,0:T(8,128)S(1)}, u32[]{:S(2)}, u32[]{:S(2)}) %collective-permute-start.35) | collective-permute-done | bytes 3232 | tf_op jit(solution)/shard_map/ppermute | solution.py:23
  317.8 4.5 %maximum_maximum_fusion = f32[4,4,8,8,8,6]{4,1,5,2,3,0:T(4,128)} fusion(f32[4,4,8,4,4,2]{4,1,5,2,3,0:T(4,128)S(1)} %get-tuple-element.143, f32[4,4,8,4,4,2]{4,1,5,2,3,0:T(4,128)S(1)} %get-tuple-element.144, f32[4,4,8,4,4,2]{4,1,5,2,3,0:T(4,128)S(1)} %get-tuple-element.145, f32[4,4,8,4,4,2]{4,1,5,2,3,0:T(4,128)S(1)} %get-tuple-element.146, ...), kind=kLoop, calls=%fused_computation.126 | loop fusion | flops 540672 | bytes 393216 | tf_op jit(solution)/shard_map/concatenate | solution.py:128
  322.3 22.8 %while.23 = (s32[]{:T(128)}, f32[4,4,8,128]{3,2,1,0:T(8,128)S(1)}, f32[4,4,8,128]{3,2,1,0:T(8,128)}, f32[4,4,8,128]{3,2,1,0:T(8,128)}, f32[4,4,8,8,8,6]{4,1,5,2,3,0:T(4,128)}, /*index=5*/f32[4,4,8,128]{3,2,1,0:T(8,128)}) while((s32[]{:T(128)}, f32[4,4,8,128]{3,2,1,0:T(8,128)S(1)}, f32[4,4,8,128]{3,2,1,0:T(8,128)}, ...), condition=%wide.region_3.4_spmd.clone, body=%wide.region_2.3_spmd.sunk.clone | while | flops 20881424 | bytes 966885 | solution.py:141
  (252 shorter events, 175.4 us)
Async XLA Ops:
  118.8 3.8 %collective-permute-start = (f32[4,20,20]{2,0,1:T(4,128)S(1)}, f32[4,20,20]{2,0,1:T(4,128)S(1)}, u32[]{:S(2)}, u32[]{:S(2)}) collective-permute-start(f32[4,20,20]{2,0,1:T(4,128)S(1)} %get-tuple-element.166), channel_id=1, source_target_pairs={{0,8},{8,16},{16,24},{1,9},{9,17},{17,25},{2,10},{10,18},{18,26},{... | collective-permute-start | bytes 19208 | tf_op jit(solution)/shard_map/ppermute | solution.py:20
  121.2 5.2 %collective-permute-start.1 = (f32[4,20,20]{2,0,1:T(4,128)S(1)}, f32[4,20,20]{2,0,1:T(4,128)S(1)}, u32[]{:S(2)}, u32[]{:S(2)}) collective-permute-start(f32[4,20,20]{2,0,1:T(4,128)S(1)} %get-tuple-element.167), channel_id=1, source_target_pairs={{8,0},{16,8},{24,16},{9,1},{17,9},{25,17},{10,2},{18,10},{26,18},{... | collective-permute-start | bytes 19208 | tf_op jit(solution)/shard_map/ppermute | solution.py:23
  126.4 5.3 %collective-permute-start.2 = (f32[28,4,20]{2,0,1:T(8,128)S(1)}, f32[28,4,20]{2,0,1:T(8,128)S(1)}, u32[]{:S(2)}, u32[]{:S(2)}) collective-permute-start(f32[28,4,20]{2,0,1:T(8,128)S(1)} %get-tuple-element.158), channel_id=1, source_target_pairs={{0,4},{1,5},{2,6},{3,7},{8,12},{9,13},{10,14},{11,15},{16,20},{17,... | collective-permute-start | bytes 26888 | tf_op jit(solution)/shard_map/ppermute | solution.py:20
  129.8 6.2 %collective-permute-start.3 = (f32[28,4,20]{2,0,1:T(8,128)S(1)}, f32[28,4,20]{2,0,1:T(8,128)S(1)}, u32[]{:S(2)}, u32[]{:S(2)}) collective-permute-start(f32[28,4,20]{2,0,1:T(8,128)S(1)} %get-tuple-element.159), channel_id=1, source_target_pairs={{4,0},{5,1},{6,2},{7,3},{12,8},{13,9},{14,10},{15,11},{20,16},{21,... | collective-permute-start | bytes 26888 | tf_op jit(solution)/shard_map/ppermute | solution.py:23
  136.3 14.1 %collective-permute-start.4 = (f32[28,28,4]{2,0,1:T(8,128)S(1)}, f32[28,28,4]{2,0,1:T(8,128)S(1)}, u32[]{:S(2)}, u32[]{:S(2)}) collective-permute-start(f32[28,28,4]{2,0,1:T(8,128)S(1)} %get-tuple-element.156), channel_id=1, source_target_pairs={{0,1},{1,2},{2,3},{4,5},{5,6},{6,7},{8,9},{9,10},{10,11},{12,13},{... | collective-permute-start | bytes 37640 | tf_op jit(solution)/shard_map/ppermute | solution.py:20
  139.8 15.3 %collective-permute-start.5 = (f32[28,28,4]{2,0,1:T(8,128)S(1)}, f32[28,28,4]{2,0,1:T(8,128)S(1)}, u32[]{:S(2)}, u32[]{:S(2)}) collective-permute-start(f32[28,28,4]{2,0,1:T(8,128)S(1)} %get-tuple-element.157), channel_id=1, source_target_pairs={{1,0},{2,1},{3,2},{5,4},{6,5},{7,6},{9,8},{10,9},{11,10},{13,12},{... | collective-permute-start | bytes 37640 | tf_op jit(solution)/shard_map/ppermute | solution.py:23
  156.5 3.3 collective-permute-start.6
  158.5 3.1 collective-permute-start.7
  161.8 3.8 %collective-permute-start.8 = (f32[32,8,16]{2,0,1:T(8,128)S(1)}, f32[32,8,16]{2,0,1:T(8,128)S(1)}, u32[]{:S(2)}, u32[]{:S(2)}) collective-permute-start(f32[32,8,16]{2,0,1:T(8,128)S(1)} %get-tuple-element.162), channel_id=1, source_target_pairs={{0,4},{1,5},{2,6},{3,7},{8,12},{9,13},{10,14},{11,15},{16,20},{17,... | collective-permute-start | bytes 49160 | tf_op jit(solution)/shard_map/ppermute | solution.py:20
  163.2 6.9 %collective-permute-start.9 = (f32[32,8,16]{2,0,1:T(8,128)S(1)}, f32[32,8,16]{2,0,1:T(8,128)S(1)}, u32[]{:S(2)}, u32[]{:S(2)}) collective-permute-start(f32[32,8,16]{2,0,1:T(8,128)S(1)} %get-tuple-element.163), channel_id=1, source_target_pairs={{4,0},{5,1},{6,2},{7,3},{12,8},{13,9},{14,10},{15,11},{20,16},{21,... | collective-permute-start | bytes 49160 | tf_op jit(solution)/shard_map/ppermute | solution.py:23
  170.4 15.4 %collective-permute-start.10 = (f32[32,32,8]{2,0,1:T(8,128)S(1)}, f32[32,32,8]{2,0,1:T(8,128)S(1)}, u32[]{:S(2)}, u32[]{:S(2)}) collective-permute-start(f32[32,32,8]{2,0,1:T(8,128)S(1)} %get-tuple-element.154), channel_id=1, source_target_pairs={{0,1},{1,2},{2,3},{4,5},{5,6},{6,7},{8,9},{9,10},{10,11},{12,13},{... | collective-permute-start | bytes 98312 | tf_op jit(solution)/shard_map/ppermute | solution.py:20
  173.9 16.7 %collective-permute-start.11 = (f32[32,32,8]{2,0,1:T(8,128)S(1)}, f32[32,32,8]{2,0,1:T(8,128)S(1)}, u32[]{:S(2)}, u32[]{:S(2)}) collective-permute-start(f32[32,32,8]{2,0,1:T(8,128)S(1)} %get-tuple-element.155), channel_id=1, source_target_pairs={{1,0},{2,1},{3,2},{5,4},{6,5},{7,6},{9,8},{10,9},{11,10},{13,12},{... | collective-permute-start | bytes 98312 | tf_op jit(solution)/shard_map/ppermute | solution.py:23
  192.2 3.7 %collective-permute-start.12 = (f32[8,8,8]{1,2,0:T(8,128)S(1)}, f32[8,8,8]{1,2,0:T(8,128)S(1)}, u32[]{:S(2)}, u32[]{:S(2)}) collective-permute-start(f32[8,8,8]{1,2,0:T(8,128)S(1)} %fusion.148), channel_id=1, source_target_pairs={{0,8},{8,16},{16,24},{1,9},{9,17},{17,25},{2,10},{10,18},{18,26},{... | collective-permute-start | bytes 6152 | tf_op jit(solution)/shard_map/ppermute | solution.py:20
  197.3 3.5 %collective-permute-start.14 = (f32[24,8,8]{1,2,0:T(8,128)S(1)}, f32[24,8,8]{1,2,0:T(8,128)S(1)}, u32[]{:S(2)}, u32[]{:S(2)}) collective-permute-start(f32[24,8,8]{1,2,0:T(8,128)S(1)} %pad_maximum_fusion.11), channel_id=1, source_target_pairs={{0,4},{1,5},{2,6},{3,7},{8,12},{9,13},{10,14},{11,15},{16,20},{17,... | collective-permute-start | bytes 18440 | tf_op jit(solution)/shard_map/ppermute | solution.py:20
  198.6 6.5 %collective-permute-start.15 = (f32[24,8,8]{1,2,0:T(8,128)S(1)}, f32[24,8,8]{1,2,0:T(8,128)S(1)}, u32[]{:S(2)}, u32[]{:S(2)}) collective-permute-start(f32[24,8,8]{1,2,0:T(8,128)S(1)} %pad_maximum_fusion.11), channel_id=1, source_target_pairs={{4,0},{5,1},{6,2},{7,3},{12,8},{13,9},{14,10},{15,11},{20,16},{21,... | collective-permute-start | bytes 18440 | tf_op jit(solution)/shard_map/ppermute | solution.py:23
  205.3 6.6 %collective-permute-start.16 = (f32[24,24,8]{1,2,0:T(8,128)S(1)}, f32[24,24,8]{1,2,0:T(8,128)S(1)}, u32[]{:S(2)}, u32[]{:S(2)}) collective-permute-start(f32[24,24,8]{1,2,0:T(8,128)S(1)} %pad_maximum_fusion.12), channel_id=1, source_target_pairs={{0,1},{1,2},{2,3},{4,5},{5,6},{6,7},{8,9},{9,10},{10,11},{12,13},{... | collective-permute-start | bytes 55304 | tf_op jit(solution)/shard_map/ppermute | solution.py:20
  208.7 7.3 %collective-permute-start.17 = (f32[24,24,8]{1,2,0:T(8,128)S(1)}, f32[24,24,8]{1,2,0:T(8,128)S(1)}, u32[]{:S(2)}, u32[]{:S(2)}) collective-permute-start(f32[24,24,8]{1,2,0:T(8,128)S(1)} %pad_maximum_fusion.12), channel_id=1, source_target_pairs={{1,0},{2,1},{3,2},{5,4},{6,5},{7,6},{9,8},{10,9},{11,10},{13,12},{... | collective-permute-start | bytes 55304 | tf_op jit(solution)/shard_map/ppermute | solution.py:23
  241.2 4.2 %collective-permute-start.18 = (f32[2,4,4]{2,0,1:T(2,128)S(1)}, f32[2,4,4]{2,0,1:T(2,128)S(1)}, u32[]{:S(2)}, u32[]{:S(2)}) collective-permute-start(f32[2,4,4]{2,0,1:T(2,128)S(1)} %get-tuple-element.186), channel_id=1, source_target_pairs={{0,8},{8,16},{16,24},{1,9},{9,17},{17,25},{2,10},{10,18},{18,26},{... | collective-permute-start | bytes 392 | tf_op jit(solution)/shard_map/ppermute | solution.py:20
  243.7 3.6 %collective-permute-start.19 = (f32[2,4,4]{2,0,1:T(2,128)S(1)}, f32[2,4,4]{2,0,1:T(2,128)S(1)}, u32[]{:S(2)}, u32[]{:S(2)}) collective-permute-start(f32[2,4,4]{2,0,1:T(2,128)S(1)} %get-tuple-element.187), channel_id=1, source_target_pairs={{8,0},{16,8},{24,16},{9,1},{17,9},{25,17},{10,2},{18,10},{26,18},{... | collective-permute-start | bytes 392 | tf_op jit(solution)/shard_map/ppermute | solution.py:23
  247.4 3.4 collective-permute-start.20
  249.3 5.5 %collective-permute-start.21 = (f32[8,2,4]{2,0,1:T(8,128)S(1)}, f32[8,2,4]{2,0,1:T(8,128)S(1)}, u32[]{:S(2)}, u32[]{:S(2)}) collective-permute-start(f32[8,2,4]{2,0,1:T(8,128)S(1)} %get-tuple-element.185), channel_id=1, source_target_pairs={{4,0},{5,1},{6,2},{7,3},{12,8},{13,9},{14,10},{15,11},{20,16},{21,... | collective-permute-start | bytes 776 | tf_op jit(solution)/shard_map/ppermute | solution.py:23
  256.2 6.1 %collective-permute-start.23 = (f32[8,8,2]{2,0,1:T(8,128)S(1)}, f32[8,8,2]{2,0,1:T(8,128)S(1)}, u32[]{:S(2)}, u32[]{:S(2)}) collective-permute-start(f32[8,8,2]{2,0,1:T(8,128)S(1)} %get-tuple-element.183), channel_id=1, source_target_pairs={{1,0},{2,1},{3,2},{5,4},{6,5},{7,6},{9,8},{10,9},{11,10},{13,12},{... | collective-permute-start | bytes 1544 | tf_op jit(solution)/shard_map/ppermute | solution.py:23
  263.0 3.6 %collective-permute-start.24 = (f32[2,8,8]{2,1,0:T(8,128)S(1)}, f32[2,8,8]{2,1,0:T(8,128)S(1)}, u32[]{:S(2)}, u32[]{:S(2)}) collective-permute-start(f32[2,8,8]{2,1,0:T(8,128)S(1)} %get-tuple-element.180), channel_id=1, source_target_pairs={{0,8},{8,16},{16,24},{1,9},{9,17},{17,25},{2,10},{10,18},{18,26},{... | collective-permute-start | bytes 1544 | tf_op jit(solution)/shard_map/ppermute | solution.py:20
  265.0 4.6 %collective-permute-start.25 = (f32[2,8,8]{2,1,0:T(8,128)S(1)}, f32[2,8,8]{2,1,0:T(8,128)S(1)}, u32[]{:S(2)}, u32[]{:S(2)}) collective-permute-start(f32[2,8,8]{2,1,0:T(8,128)S(1)} %get-tuple-element.181), channel_id=1, source_target_pairs={{8,0},{16,8},{24,16},{9,1},{17,9},{25,17},{10,2},{18,10},{26,18},{... | collective-permute-start | bytes 1544 | tf_op jit(solution)/shard_map/ppermute | solution.py:23
  269.6 3.2 collective-permute-start.26
  271.3 5.6 %collective-permute-start.27 = (f32[12,2,8]{2,1,0:T(2,128)S(1)}, f32[12,2,8]{2,1,0:T(2,128)S(1)}, u32[]{:S(2)}, u32[]{:S(2)}) collective-permute-start(f32[12,2,8]{2,1,0:T(2,128)S(1)} %get-tuple-element.179), channel_id=1, source_target_pairs={{4,0},{5,1},{6,2},{7,3},{12,8},{13,9},{14,10},{15,11},{20,16},{21,... | collective-permute-start | bytes 2312 | tf_op jit(solution)/shard_map/ppermute | solution.py:23
  277.0 6.8 %collective-permute-start.28 = (f32[12,12,2]{2,1,0:T(8,128)S(1)}, f32[12,12,2]{2,1,0:T(8,128)S(1)}, u32[]{:S(2)}, u32[]{:S(2)}) collective-permute-start(f32[12,12,2]{2,1,0:T(8,128)S(1)} %get-tuple-element.176), channel_id=1, source_target_pairs={{0,1},{1,2},{2,3},{4,5},{5,6},{6,7},{8,9},{9,10},{10,11},{12,13},{... | collective-permute-start | bytes 3464 | tf_op jit(solution)/shard_map/ppermute | solution.py:20
  280.7 7.3 %collective-permute-start.29 = (f32[12,12,2]{2,1,0:T(8,128)S(1)}, f32[12,12,2]{2,1,0:T(8,128)S(1)}, u32[]{:S(2)}, u32[]{:S(2)}) collective-permute-start(f32[12,12,2]{2,1,0:T(8,128)S(1)} %get-tuple-element.177), channel_id=1, source_target_pairs={{1,0},{2,1},{3,2},{5,4},{6,5},{7,6},{9,8},{10,9},{11,10},{13,12},{... | collective-permute-start | bytes 3464 | tf_op jit(solution)/shard_map/ppermute | solution.py:23
  290.9 4.4 %collective-permute-start.31 = (f32[2,16,16]{2,1,0:T(8,128)S(1)}, f32[2,16,16]{2,1,0:T(8,128)S(1)}, u32[]{:S(2)}, u32[]{:S(2)}) collective-permute-start(f32[2,16,16]{2,1,0:T(8,128)S(1)} %get-tuple-element.171), channel_id=1, source_target_pairs={{8,0},{16,8},{24,16},{9,1},{17,9},{25,17},{10,2},{18,10},{26,18},{... | collective-permute-start | bytes 6152 | tf_op jit(solution)/shard_map/ppermute | solution.py:23
  297.0 5.7 %collective-permute-start.33 = (f32[20,2,16]{2,1,0:T(2,128)S(1)}, f32[20,2,16]{2,1,0:T(2,128)S(1)}, u32[]{:S(2)}, u32[]{:S(2)}) collective-permute-start(f32[20,2,16]{2,1,0:T(2,128)S(1)} %get-tuple-element.169), channel_id=1, source_target_pairs={{4,0},{5,1},{6,2},{7,3},{12,8},{13,9},{14,10},{15,11},{20,16},{21,... | collective-permute-start | bytes 7688 | tf_op jit(solution)/shard_map/ppermute | solution.py:23
  302.9 8.2 %collective-permute-start.34 = (f32[20,20,2]{2,1,0:T(8,128)S(1)}, f32[20,20,2]{2,1,0:T(8,128)S(1)}, u32[]{:S(2)}, u32[]{:S(2)}) collective-permute-start(f32[20,20,2]{2,1,0:T(8,128)S(1)} %get-tuple-element.164), channel_id=1, source_target_pairs={{0,1},{1,2},{2,3},{4,5},{5,6},{6,7},{8,9},{9,10},{10,11},{12,13},{... | collective-permute-start | bytes 9608 | tf_op jit(solution)/shard_map/ppermute | solution.py:20
  304.8 10.5 %collective-permute-start.35 = (f32[20,20,2]{2,1,0:T(8,128)S(1)}, f32[20,20,2]{2,1,0:T(8,128)S(1)}, u32[]{:S(2)}, u32[]{:S(2)}) collective-permute-start(f32[20,20,2]{2,1,0:T(8,128)S(1)} %get-tuple-element.165), channel_id=1, source_target_pairs={{1,0},{2,1},{3,2},{5,4},{6,5},{7,6},{9,8},{10,9},{11,10},{13,12},{... | collective-permute-start | bytes 9608 | tf_op jit(solution)/shard_map/ppermute | solution.py:23
  (13 other events, 112.6 us)
where the time goes:
time: 353 us; the launch traced here: 346 us
  local copies, waits for them, and re-layouts  116 us (33%)
  waiting for transfers between devices  97.2 us (28%)
  starting transfers between devices  64.4 us (18%)
  other arithmetic  23.3 us (7%)
  blocking collectives  22.7 us (6%)
  matrix products  20.3 us (6%)
    transpose x13, local copies, waits for them, and re-layouts, place_patches(): jnp.transpose(portion, (0, 3, 1, 4, 2, 5))  71.1 us
    ppermute x18, waiting for transfers between devices, with_halo(): lax.ppermute(lax.slice_in_dim(block, 0, width, axis=dim), axis, backward)  66.8 us
    ppermute x18, starting transfers between devices, with_halo(): lax.ppermute(lax.slice_in_dim(block, block.shape[dim] - width, None, axis...  41.2 us
    ppermute x18, waiting for transfers between devices, with_halo(): lax.ppermute(lax.slice_in_dim(block, block.shape[dim] - width, None, axis...  30.4 us
    reshape x24, local copies, waits for them, and re-layouts, place_patches(): jnp.transpose(portion, (0, 3, 1, 4, 2, 5))  30.3 us
    ppermute x18, starting transfers between devices, with_halo(): lax.ppermute(lax.slice_in_dim(block, 0, width, axis=dim), axis, backward)  23.3 us
    all_gather x1, blocking collectives, body(): lax.all_gather(charge_three, 'gz', axis=2, tiled=True)  13.1 us
    dynamic_slice x8, local copies, waits for them, and re-layouts, interpolate(): lax.map(interpolate_one_slab, (patches, offset_x, offset_y, offset_z))  11 us
  transfers between devices with their start and end apart: 36, of which 28 were waited for; matrix products, arithmetic and copies ran while one was open for 1% of the time, Pallas kernels for 0%

commit v1 on v0

v1 whole, which is shorter than its diff:
```python
import functools
import math

import jax
import jax.numpy as jnp
import numpy as np
from jax import lax
from jax.experimental import pallas as pl
from jax.experimental.pallas import tpu as pltpu
from jax.sharding import PartitionSpec as P

R = 8
LANES = 128
TERMS = 5
SLOT = LANES // TERMS
RIM = 4
TAPS = (-0.0625, 0.0, 0.5625, 1.0, 0.5625, 0.0, -0.0625)
highest = lax.Precision.HIGHEST


def profile(family, offset):
    if family == 0:
        return math.exp(-((offset / (0.4 * R)) ** 2))
    if family == 1:
        return math.exp(-((offset / (0.8 * R)) ** 2))
    return 1.0 / (1.0 + (offset / R) ** 2)


def norm_factor(family):
    return sum(profile(family, float(o)) ** 2 for o in range(-R, R + 1)) ** 1.5


def stencil(points, family):
    matrix = np.zeros((points, points))
    for i in range(points):
        for k in range(max(0, i - R), min(points, i + R + 1)):
            matrix[i, k] = profile(family, float(k - i))
    return matrix


def restriction(points):
    matrix = np.zeros((points // 2, points))
    for i in range(points // 2):
        for k, tap in enumerate(TAPS):
            if 0 <= 2 * i + k - 3 < points:
                matrix[i, 2 * i + k - 3] += tap
    return matrix


def term_matrices(points):
    q_one = restriction(points)
    q_two = restriction(points // 2)
    coarse = points // 4
    far = np.array([[profile(2, float(k - i)) for k in range(coarse)] for i in range(coarse)])
    down = q_two @ q_one
    return [
        stencil(points, 0),
        stencil(points, 1),
        q_one.T @ stencil(points // 2, 0) @ q_one,
        q_one.T @ stencil(points // 2, 1) @ q_one,
        down.T @ far @ down,
    ]


def term_scales():
    n = [norm_factor(f) for f in range(3)]
    return [1.0 / n[0], 1.0 / n[1], 0.5 / n[0], 0.5 / n[1], 0.5 / n[2]]


def windowed(points, count):
    local = points // count
    width = local + RIM
    index = np.arange(count)[:, None] * local + np.arange(width)[None, :] - RIM // 2
    inside = (index >= 0) & (index < points)
    clipped = np.clip(index, 0, points - 1)
    both = inside[:, :, None, None] & inside[None, None]
    return np.stack(
        [np.where(both, m[clipped[:, :, None, None], clipped[None, None]], 0.0) for m in term_matrices(points)]
    )


def round_up(value, step):
    return -(-value // step) * step


class Plan:
    def __init__(self, nbins, counts):
        self.nbins = nbins
        self.counts = counts
        self.local = (4 * nbins[0], 4 * nbins[1], 2 * nbins[2])
        self.width = tuple(v + RIM for v in self.local)
        self.points = tuple(v * c for v, c in zip(self.local, counts))
        self.xp = round_up(self.width[0], 8)
        self.zp = round_up(self.width[2], 16)
        if self.zp - self.width[2] >= 8 and self.width[2] % 2 == 0:
            self.zp = round_up(self.width[2], 8)
        self.chunks = -(-self.width[1] // TERMS)
        self.lanes_in = round_up(self.width[1] * self.xp, LANES)
        self.lanes_out = self.chunks * LANES
        self.columns = nbins[0] * nbins[1]
        assert self.columns * nbins[2] == LANES and nbins[2] == 8
        assert self.width[2] <= SLOT and self.columns % 2 == 0

    def place_matrix(self):
        nbx, nby, _ = self.nbins
        m = np.zeros((self.columns * 64, self.lanes_in), np.float32)
        for a in range(nbx):
            for b in range(nby):
                for i in range(8):
                    for j in range(8):
                        m[(a * nby + b) * 64 + i * 8 + j, (4 * b + j) * self.xp + 4 * a + i] = 1.0
        return jnp.asarray(m, jnp.bfloat16)

    def z_table(self):
        nz, width = self.counts[2], self.width[2]
        m = windowed(self.points[2], nz)
        table = np.zeros((nz, nz * self.zp, LANES), np.float32)
        for d in range(nz):
            for o in range(nz):
                for w in range(width):
                    row = o * self.zp + (w % 2) * (self.zp // 2) + w // 2
                    for t in range(TERMS):
                        table[d, row, t * SLOT : t * SLOT + width] = m[t, d, :, (d - o) % nz, w]
        return jnp.asarray(table)

    def y_table(self):
        ny, width = self.counts[1], self.width[1]
        m = windowed(self.points[1], ny)
        table = np.zeros((ny, ny * width, self.chunks * TERMS, LANES), np.float32)
        for d in range(ny):
            for o in range(ny):
                for t in range(TERMS):
                    block = m[t, d, :, (d - o) % ny, :]
                    table[d, o * width : (o + 1) * width, :width, t * SLOT : (t + 1) * SLOT] = block.T[:, :, None]
        return jnp.asarray(table.reshape(ny, ny * width * self.chunks * TERMS, LANES))

    def x_table(self):
        nx, width = self.counts[0], self.width[0]
        m = windowed(self.points[0], nx)
        scales = term_scales()
        table = np.zeros((nx, nx * self.xp, TERMS * self.xp), np.float32)
        for d in range(nx):
            for o in range(nx):
                for t in range(TERMS):
                    table[d, o * self.xp : o * self.xp + width, t * self.xp : t * self.xp + width] = (
                        scales[t] * m[t, (d + o) % nx, :, d, :]
                    )
        return jnp.asarray(table)


def bspline(spacing):
    a = jnp.abs(spacing)
    u = jnp.maximum(2.0 - a, 0.0)
    v = jnp.maximum(1.0 - a, 0.0)
    return u * u * u * (1.0 / 6.0) - v * v * v * (2.0 / 3.0)


def counts_row(counts, nbins):
    nbx, nby, nbz = nbins
    rows = jnp.concatenate([counts[a].astype(jnp.float32) for a in range(nbx)], axis=0)
    spread = lax.broadcasted_iota(jnp.int32, (nbz, LANES), 1) % nbz == lax.broadcasted_iota(
        jnp.int32, (nbz, LANES), 0
    )
    tiled = jnp.dot(rows, spread.astype(jnp.float32), precision=highest)
    own = lax.broadcasted_iota(jnp.int32, tiled.shape, 1) // nbz == lax.broadcasted_iota(
        jnp.int32, tiled.shape, 0
    )
    return jnp.sum(jnp.where(own, tiled, 0.0), axis=0, keepdims=True)


def split_two(value):
    high = value.astype(jnp.bfloat16)
    low = (value - high.astype(jnp.float32)).astype(jnp.bfloat16)
    return high, low


def spread_kernel(plan, counts_ref, charge_ref, x_ref, y_ref, z_ref, place_ref, out_ref,
                  bx_s, by_s, bz_s, patch_s, turned_s, column_s):
    slots = charge_ref.shape[1]
    row = counts_row(counts_ref, plan.nbins)
    slot = lax.broadcasted_iota(jnp.int32, (slots, LANES), 0).astype(jnp.float32)
    weighted = jnp.where(slot < row, charge_ref[...].T, 0.0)
    along = x_ref[...].T
    for i in range(8):
        bx_s[i] = weighted * bspline(along + (2.0 - i))
    along = y_ref[...].T
    for i in range(8):
        by_s[i] = bspline(along + (2.0 - i))
    along = z_ref[...].T
    for i in range(6):
        bz_s[i] = bspline(along + (2.0 - i))

    def one_x(i, carry):
        weight_x = bx_s[i]
        rows = [[] for _ in range(6)]
        for j in range(8):
            product = weight_x * by_s[j]
            for k in range(6):
                rows[k].append(jnp.sum(product * bz_s[k], axis=0, keepdims=True))
        for k in range(6):
            patch_s[pl.ds(pl.multiple_of(k * 64 + i * 8, 8), 8), :] = jnp.concatenate(rows[k], axis=0)
        return carry

    lax.fori_loop(0, 8, one_x, 0)
    for h in range(3):
        turned_s[:, h * LANES : (h + 1) * LANES] = patch_s[h * LANES : (h + 1) * LANES, :].T
    column_s[...] = jnp.zeros_like(column_s)
    nbz = plan.nbins[2]
    half = plan.zp // 2
    lane = lax.broadcasted_iota(jnp.int32, (nbz, LANES), 1)
    for pair in range(plan.columns // 2):
        for s in range(3):
            left = turned_s[2 * pair * nbz : (2 * pair + 1) * nbz, s * LANES : (s + 1) * LANES]
            right = turned_s[(2 * pair + 1) * nbz : (2 * pair + 2) * nbz, s * LANES : (s + 1) * LANES]
            even = jnp.where(lane < 64, left, pltpu.roll(right, 64, 1))
            odd = jnp.where(lane < 64, pltpu.roll(left, 64, 1), right)
            for c, piece in enumerate((even, odd)):
                at = (pl.ds(c * half + s, nbz), pl.ds(pair * LANES, LANES))
                column_s[at] = column_s[at] + piece
    high, low = split_two(column_s[...])
    place = place_ref[...]
    out_ref[...] = jnp.dot(high, place, preferred_element_type=jnp.float32) + jnp.dot(
        low, place, preferred_element_type=jnp.float32
    )


def solve_kernel(plan, *refs):
    ny, nz = plan.counts[1:]
    nx = plan.counts[0]
    blocks = refs[: ny * nz]
    ztab_ref, ytab_ref, xtab_ref = refs[ny * nz : ny * nz + 3]
    outs = refs[ny * nz + 3 : ny * nz + 3 + nx]
    mid_s, term_s = refs[ny * nz + 3 + nx :]
    wy = plan.width[1]
    xp = plan.xp
    span = plan.chunks * TERMS
    for oy in range(ny):
        gathered = jnp.concatenate([blocks[oy * nz + oz][...] for oz in range(nz)], axis=0)
        done = lax.dot_general(
            gathered, ztab_ref[0], (((0,), (0,)), ((), ())), precision=highest,
            preferred_element_type=jnp.float32,
        )
        mid_s[oy * wy * xp : (oy + 1) * wy * xp, :] = done[: wy * xp, :]
    slot = lax.broadcasted_iota(jnp.int32, (xp, LANES), 1) // SLOT

    for chunk in range(plan.chunks):
        def one_y(y, sums):
            value = mid_s[pl.ds(pl.multiple_of(y * xp, 8), xp), :]
            return tuple(
                acc + value * ytab_ref[0, pl.ds(y * span + chunk * TERMS + b, 1), :]
                for b, acc in enumerate(sums)
            )

        sums = lax.fori_loop(
            0, ny * wy, one_y, tuple(jnp.zeros((xp, LANES), jnp.float32) for _ in range(TERMS)), unroll=8
        )
        for t in range(TERMS):
            merged = jnp.zeros((xp, LANES), jnp.float32)
            for b in range(TERMS):
                shift = (SLOT * (b - t)) % LANES
                moved = pltpu.roll(sums[b], shift, 1) if shift else sums[b]
                merged = jnp.where(slot == b, moved, merged)
            term_s[t * xp : (t + 1) * xp, chunk * LANES : (chunk + 1) * LANES] = merged
    result = jnp.dot(xtab_ref[0], term_s[...], precision=highest, preferred_element_type=jnp.float32)
    for o in range(nx):
        outs[o][...] = result[o * xp : (o + 1) * xp, :]


def gather_kernel(plan, *refs):
    nx = plan.counts[0]
    parts = refs[:nx]
    counts_ref, x_ref, y_ref, z_ref, place_ref, fine_ref, atom_ref = refs[nx : nx + 7]
    bx_s, by_s, bz_s, field_s, column_s, turned_s, patch_s = refs[nx + 7 :]
    xp = plan.xp
    wx, wy, wz = plan.width
    lx, ly, lz = plan.local
    total = parts[0][...]
    for part in parts[1:]:
        total = total + part[...]
    field_s[...] = jnp.zeros_like(field_s)
    for y in range(wy):
        chunk, b = divmod(y, TERMS)
        piece = total[:, chunk * LANES : (chunk + 1) * LANES]
        field_s[y * xp : (y + 1) * xp, :] = pltpu.roll(piece, LANES - SLOT * b, 1) if b else piece
    for x in range(lx):
        fine_ref[x] = field_s[pl.ds(2 * xp + x + 2, ly, stride=xp), :][:, 2 : 2 + lz]
    high, low = split_two(field_s[...].T[: plan.zp, :])
    place = place_ref[...]
    columns = lax.dot_general(
        high, place, (((1,), (1,)), ((), ())), preferred_element_type=jnp.float32
    ) + lax.dot_general(low, place, (((1,), (1,)), ((), ())), preferred_element_type=jnp.float32)
    for pair in range(plan.columns // 2):
        column_s[pair * plan.zp : (pair + 1) * plan.zp, :] = columns[:, pair * LANES : (pair + 1) * LANES]
    nbz = plan.nbins[2]
    lane = lax.broadcasted_iota(jnp.int32, (nbz, LANES), 1)
    for pair in range(plan.columns // 2):
        for s in range(3):
            even = column_s[pl.ds(pair * plan.zp + 2 * s, nbz, stride=2), :]
            odd = column_s[pl.ds(pair * plan.zp + 2 * s + 1, nbz, stride=2), :]
            turned_s[2 * pair * nbz : (2 * pair + 1) * nbz, s * LANES : (s + 1) * LANES] = jnp.where(
                lane < 64, even, pltpu.roll(odd, 64, 1)
            )
            turned_s[(2 * pair + 1) * nbz : (2 * pair + 2) * nbz, s * LANES : (s + 1) * LANES] = jnp.where(
                lane < 64, pltpu.roll(even, 64, 1), odd
            )
    for h in range(3):
        patch_s[h * LANES : (h + 1) * LANES, :] = turned_s[:, h * LANES : (h + 1) * LANES].T
    slots = x_ref.shape[1]
    along = x_ref[...].T
    for i in range(8):
        bx_s[i] = bspline(along + (2.0 - i))
    along = y_ref[...].T
    for i in range(8):
        by_s[i] = bspline(along + (2.0 - i))
    along = z_ref[...].T
    for i in range(6):
        bz_s[i] = bspline(along + (2.0 - i))

    def one_x(i, result):
        inner = jnp.zeros((slots, LANES), jnp.float32)
        rows = [patch_s[pl.ds(pl.multiple_of(k * 64 + i * 8, 8), 8), :] for k in range(6)]
        for j in range(8):
            along_z = rows[0][j : j + 1, :] * bz_s[0]
            for k in range(1, 6):
                along_z = along_z + rows[k][j : j + 1, :] * bz_s[k]
            inner = inner + along_z * by_s[j]
        return result + inner * bx_s[i]

    result = lax.fori_loop(0, 8, one_x, jnp.zeros((slots, LANES), jnp.float32))
    row = counts_row(counts_ref, plan.nbins)
    slot = lax.broadcasted_iota(jnp.int32, (slots, LANES), 0).astype(jnp.float32)
    atom_ref[...] = jnp.where(slot < row, result, 0.0).T


def body(charges, offset_x, offset_y, offset_z, counts):
    nbins = charges.shape[:3]
    slots = charges.shape[3]
    sizes = tuple(lax.axis_size(a) for a in ("gx", "gy", "gz"))
    nx, ny, nz = sizes
    plan = Plan(nbins, sizes)
    flat = [v.reshape(LANES, slots) for v in (charges, offset_x, offset_y, offset_z)]
    place = plan.place_matrix()
    vmem = pl.BlockSpec(memory_space=pltpu.VMEM)
    f32 = jnp.float32
    params = pltpu.CompilerParams(vmem_limit_bytes=56 << 20)

    weights = [
        pltpu.VMEM((8, slots, LANES), f32),
        pltpu.VMEM((8, slots, LANES), f32),
        pltpu.VMEM((6, slots, LANES), f32),
    ]
    spread = pl.pallas_call(
        functools.partial(spread_kernel, plan),
        out_shape=jax.ShapeDtypeStruct((plan.zp, plan.lanes_in), f32),
        in_specs=[vmem] * 6,
        out_specs=vmem,
        scratch_shapes=weights
        + [
            pltpu.VMEM((384, LANES), f32),
            pltpu.VMEM((LANES, 384), f32),
            pltpu.VMEM((plan.zp, plan.columns * 64), f32),
        ],
        compiler_params=params,
        name="spread",
    )(counts, *flat, place)

    def shifted(value, oy, oz):
        pairs = [
            (sy * nz + sz, ((sy + oy) % ny) * nz + (sz + oz) % nz) for sy in range(ny) for sz in range(nz)
        ]
        return lax.ppermute(value, ("gy", "gz"), pairs)

    blocks = [
        spread if oy == 0 and oz == 0 else shifted(spread, oy, oz) for oy in range(ny) for oz in range(nz)
    ]
    tables = (plan.z_table(), plan.y_table(), plan.x_table())
    axes = ("gz", "gy", "gx")

    def picked(table, axis):
        return pl.BlockSpec((1,) + table.shape[1:], lambda _, axis=axis: (lax.axis_index(axis), 0, 0))

    outs = pl.pallas_call(
        functools.partial(solve_kernel, plan),
        out_shape=[jax.ShapeDtypeStruct((plan.xp, plan.lanes_out), f32)] * nx,
        grid=(1,),
        in_specs=[vmem] * (ny * nz) + [picked(t, a) for t, a in zip(tables, axes)],
        out_specs=[vmem] * nx,
        scratch_shapes=[
            pltpu.VMEM((ny * plan.width[1] * plan.xp, LANES), f32),
            pltpu.VMEM((TERMS * plan.xp, plan.lanes_out), f32),
        ],
        compiler_params=params,
        name="solve",
    )(*blocks, *tables)
    parts = [
        outs[o] if o == 0 else lax.ppermute(outs[o], "gx", [(s, (s + o) % nx) for s in range(nx)])
        for o in range(nx)
    ]
    fine, atom = pl.pallas_call(
        functools.partial(gather_kernel, plan),
        out_shape=[
            jax.ShapeDtypeStruct(plan.local, f32),
            jax.ShapeDtypeStruct((LANES, slots), f32),
        ],
        in_specs=[vmem] * (nx + 5),
        out_specs=[vmem, vmem],
        scratch_shapes=weights
        + [
            pltpu.VMEM((plan.lanes_in, LANES), f32),
            pltpu.VMEM((plan.columns // 2 * plan.zp, LANES), f32),
            pltpu.VMEM((LANES, 384), f32),
            pltpu.VMEM((384, LANES), f32),
        ],
        compiler_params=params,
        name="gather",
    )(*parts, counts, *flat[1:], place)
    return fine, atom.reshape(charges.shape)


def solution(mesh):
    in_specs = (
        P("gx", "gy", "gz", None),
        P("gx", "gy", "gz", None),
        P("gx", "gy", "gz", None),
        P("gx", "gy", "gz", None),
        P("gx", "gy", "gz"),
    )
    out_specs = (P("gx", "gy", "gz"), P("gx", "gy", "gz", None))
    return jax.shard_map(body, mesh=mesh, in_specs=in_specs, out_specs=out_specs, check_vma=False)
```

time: 353 us -> 41.1 us (0.12); the launches traced: 346 us -> 40.8 us
  local copies, waits for them, and re-layouts: 116 us -> 1.26 us
  waiting for transfers between devices: 97.2 us -> 7.48 us
  starting transfers between devices: 64.4 us -> 16.1 us
  other arithmetic: 23.3 us -> 0 us
  blocking collectives: 22.7 us -> 0 us
  matrix products: 20.3 us -> 0 us
  Pallas kernels: 0 us -> 15.4 us
    ppermute x36 -> x10, waiting for transfers between devices: 97.2 us -> 7.48 us  [the longest x7 5.41 us: shifted(): return lax.ppermute(value, ('gy', 'gz'), pairs)]
    transpose x15 -> x0, local copies, waits for them, and re-layouts: 72.8 us -> none  [the longest x13 71.1 us: place_patches(): jnp.transpose(portion, (0, 3, 1, 4, 2, 5))]
    ppermute x36 -> x10, starting transfers between devices: 64.4 us -> 16.1 us  [the longest x7 13.1 us: shifted(): return lax.ppermute(value, ('gy', 'gz'), pairs)]
    reshape x25 -> x0, local copies, waits for them, and re-layouts: 30.6 us -> none  [the longest x24 30.3 us: place_patches(): jnp.transpose(portion, (0, 3, 1, 4, 2, 5))]
    all_gather x3 -> x0, blocking collectives: 22.7 us -> none  [the longest x1 13.1 us: body(): lax.all_gather(charge_three, 'gz', axis=2, tiled=True)]
    dot_general x35 -> x0, matrix products: 20.3 us -> none  [the longest x4 8.46 us: spread_one_slab(): return jnp.einsum('bcsxy,bcsz->bcxyz', outer, weight_z, precision=highest)]
    pallas_call x0 -> x3, Pallas kernels: none -> 15.4 us  [the longest x1 5.65 us: body(): pl.pallas_call(functools.partial(spread_kernel, plan), out_shape=jax.Shap...]
    add x21 -> x0, other arithmetic: 12.8 us -> none  [the longest x8 5.87 us: spline_weights(): along_x[..., None] + 2.0 - jnp.arange(8).astype(jnp.float32)]
  transfers between devices with their start and end apart: 36 -> 10, of which waited for: 28 -> 7; matrix products, arithmetic and copies ran while one was open for 1% -> 0% of each run, Pallas kernels for 0% -> 0%
where the time goes in v1:
time: 41.1 us; the launch traced here: 40.8 us
  starting transfers between devices  16.1 us (39%)
  Pallas kernels  15.4 us (37%)
  waiting for transfers between devices  7.48 us (18%)
  local copies, waits for them, and re-layouts  1.26 us (3%)
  between operations  0.68 us (2%)
    ppermute x7, starting transfers between devices, shifted(): return lax.ppermute(value, ('gy', 'gz'), pairs)  13.1 us
    pallas_call x1, Pallas kernels, body(): pl.pallas_call(functools.partial(spread_kernel, plan), out_shape=jax.Shap...  5.65 us
    pallas_call x1, Pallas kernels, body(): pl.pallas_call(functools.partial(gather_kernel, plan), out_shape=[jax.Sha...  5.65 us
    ppermute x7, waiting for transfers between devices, shifted(): return lax.ppermute(value, ('gy', 'gz'), pairs)  5.41 us
    pallas_call x1, Pallas kernels, body(): pl.pallas_call(functools.partial(solve_kernel, plan), out_shape=[jax.Shap...  4.07 us
    ppermute x3, starting transfers between devices, body(): lax.ppermute(outs[o], 'gx', [(s, (s + o) % nx) for s in range(nx)])  2.99 us
    ppermute x3, waiting for transfers between devices, body(): lax.ppermute(outs[o], 'gx', [(s, (s + o) % nx) for s in range(nx)])  2.06 us
    unnamed x20, local copies, waits for them, and re-layouts  1.26 us
  transfers between devices with their start and end apart: 10, of which 7 were waited for; matrix products, arithmetic and copies ran while one was open for 0% of the time, Pallas kernels for 0%

profile of v1, /device:TPU:0, one launch (start us, length us, event | category | flops | bytes accessed | tf_op | source)
XLA Modules:
  0.0 40.8 jit_solution(1219740923075328632)
XLA Ops:
  0.6 5.7 %spread.1.refs_0_ = f32[24,512]{1,0:T(8,128)} custom-call(s32[4,4,8]{2,1,0:T(4,128)} %refs_4_.1, f32[128,128]{1,0:T(8,128)} %bitcast.11, f32[128,128]{1,0:T(8,128)} %bitcast.5, f32[128,128]{1,0:T(8,128)} %bitcast.7, f32[128,128]{1,0:T(8,128)} %bitcast.9, bf16[1024,512]{1,0:T(8,128)(2,1)} %constant.8.clone.place_ref.refs_8_), custom_call_target="tpu_custom_call" | custom-call | tf_op jit(solution)/shard_map/spread/pallas_call | solution.py:352
  6.3 6.0 %collective-permute-start.6 = (f32[24,512]{1,0:T(8,128)}, f32[24,512]{1,0:T(8,128)S(1)}, u32[]{:S(2)}, u32[]{:S(2)}) collective-permute-start(f32[24,512]{1,0:T(8,128)} %spread.1.refs_0_), channel_id=1, source_target_pairs={{0,7},{1,4},{2,5},{3,6},{4,3},{5,0},{6,1},{7,2},{8,15},{9,12},{10,... | collective-permute-start | bytes 147464 | tf_op jit(solution)/shard_map/ppermute | solution.py:371
  12.3 0.0 collective-permute-start.5
  12.3 1.9 %collective-permute-start.4 = (f32[24,512]{1,0:T(8,128)}, f32[24,512]{1,0:T(8,128)S(1)}, u32[]{:S(2)}, u32[]{:S(2)}) collective-permute-start(f32[24,512]{1,0:T(8,128)} %spread.1.refs_0_), channel_id=1, source_target_pairs={{0,5},{1,6},{2,7},{3,4},{4,1},{5,2},{6,3},{7,0},{8,13},{9,14},{10,... | collective-permute-start | bytes 147464 | tf_op jit(solution)/shard_map/ppermute | solution.py:371
  14.2 0.5 %collective-permute-start.3 = (f32[24,512]{1,0:T(8,128)}, f32[24,512]{1,0:T(8,128)S(1)}, u32[]{:S(2)}, u32[]{:S(2)}) collective-permute-start(f32[24,512]{1,0:T(8,128)} %spread.1.refs_0_), channel_id=1, source_target_pairs={{0,4},{1,5},{2,6},{3,7},{4,0},{5,1},{6,2},{7,3},{8,12},{9,13},{10,... | collective-permute-start | bytes 147464 | tf_op jit(solution)/shard_map/ppermute | solution.py:371
  14.7 2.8 %collective-permute-start.2 = (f32[24,512]{1,0:T(8,128)}, f32[24,512]{1,0:T(8,128)S(1)}, u32[]{:S(2)}, u32[]{:S(2)}) collective-permute-start(f32[24,512]{1,0:T(8,128)} %spread.1.refs_0_), channel_id=1, source_target_pairs={{0,3},{1,0},{2,1},{3,2},{4,7},{5,4},{6,5},{7,6},{8,11},{9,8},{10,9... | collective-permute-start | bytes 147464 | tf_op jit(solution)/shard_map/ppermute | solution.py:371
  17.6 0.0 collective-permute-done.6.refs_7_
  17.6 1.1 %collective-permute-start.1 = (f32[24,512]{1,0:T(8,128)}, f32[24,512]{1,0:T(8,128)S(1)}, u32[]{:S(2)}, u32[]{:S(2)}) collective-permute-start(f32[24,512]{1,0:T(8,128)} %spread.1.refs_0_), channel_id=1, source_target_pairs={{0,2},{1,3},{2,0},{3,1},{4,6},{5,7},{6,4},{7,5},{8,10},{9,11},{10,... | collective-permute-start | bytes 147464 | tf_op jit(solution)/shard_map/ppermute | solution.py:371
  18.7 0.0 collective-permute-done.5.refs_6_
  18.7 0.7 %collective-permute-start = (f32[24,512]{1,0:T(8,128)}, f32[24,512]{1,0:T(8,128)S(1)}, u32[]{:S(2)}, u32[]{:S(2)}) collective-permute-start(f32[24,512]{1,0:T(8,128)} %spread.1.refs_0_), channel_id=1, source_target_pairs={{0,1},{1,2},{2,3},{3,0},{4,5},{5,6},{6,7},{7,4},{8,9},{9,10},{10,1... | collective-permute-start | bytes 147464 | tf_op jit(solution)/shard_map/ppermute | solution.py:371
  19.4 0.0 collective-permute-done.4.refs_5_
  19.4 0.1 collective-permute-done.3.refs_4_
  19.5 0.2 collective-permute-done.2.refs_3_
  19.6 3.3 %collective-permute-done.1.refs_2_ = f32[24,512]{1,0:T(8,128)S(1)} collective-permute-done((f32[24,512]{1,0:T(8,128)}, f32[24,512]{1,0:T(8,128)S(1)}, u32[]{:S(2)}, u32[]{:S(2)}) %collective-permute-start.1) | collective-permute-done | bytes 49184 | tf_op jit(solution)/shard_map/ppermute | solution.py:371
  23.0 1.8 %collective-permute-done.refs_1_ = f32[24,512]{1,0:T(8,128)S(1)} collective-permute-done((f32[24,512]{1,0:T(8,128)}, f32[24,512]{1,0:T(8,128)S(1)}, u32[]{:S(2)}, u32[]{:S(2)}) %collective-permute-start) | collective-permute-done | bytes 49184 | tf_op jit(solution)/shard_map/ppermute | solution.py:371
  24.8 0.0 copy-done
  24.8 0.0 copy-done.1
  24.8 0.0 copy-done.3
  24.8 0.0 copy-done.4
  24.8 0.0 copy-done.5
  24.8 0.0 copy-start.6
  24.8 0.6 %copy-done.6 = f32[24,512]{1,0:T(8,128)} copy-done((f32[24,512]{1,0:T(8,128)}, f32[24,512]{1,0:T(8,128)S(1)}, u32[]{:S(2)}) %copy-start.6) | copy-done | bytes 49176
  25.4 4.1 %solve.1 = (f32[24,512]{1,0:T(8,128)}, f32[24,512]{1,0:T(8,128)}, f32[24,512]{1,0:T(8,128)}, f32[24,512]{1,0:T(8,128)}) custom-call(f32[24,512]{1,0:T(8,128)} %spread.1.refs_0_, f32[24,512]{1,0:T(8,128)} %copy-done.6, f32[24,512]{1,0:T(8,128)} %copy-done.5, f32[24,512]{1,0:T(8,128)} %copy-done.4, f32[24,512]{1,0:T(8,128)} %copy-done.3, f32[24,512]{1,0:T(8,128)} %copy-done.2, ...), custom_call_target="tpu_custom_call" | custom-call | tf_op jit(solution)/shard_map/solve/pallas_call | solution.py:382
  29.5 0.0 collective-permute-start.7
  29.5 1.6 %collective-permute-start.8 = (f32[24,512]{1,0:T(8,128)}, f32[24,512]{1,0:T(8,128)S(1)}, u32[]{:S(2)}, u32[]{:S(2)}) collective-permute-start(f32[24,512]{1,0:T(8,128)} %get-tuple-element.10), channel_id=1, source_target_pairs={{0,16},{8,24},{16,0},{24,8},{1,17},{9,25},{17,1},{25,9},{2,18},{10... | collective-permute-start | bytes 147464 | tf_op jit(solution)/shard_map/ppermute | solution.py:396
  31.1 1.4 %collective-permute-start.9 = (f32[24,512]{1,0:T(8,128)}, f32[24,512]{1,0:T(8,128)S(1)}, u32[]{:S(2)}, u32[]{:S(2)}) collective-permute-start(f32[24,512]{1,0:T(8,128)} %get-tuple-element.11), channel_id=1, source_target_pairs={{0,24},{8,0},{16,8},{24,16},{1,25},{9,1},{17,9},{25,17},{2,26},{10... | collective-permute-start | bytes 147464 | tf_op jit(solution)/shard_map/ppermute | solution.py:396
  32.5 0.7 %collective-permute-done.7.refs_1_ = f32[24,512]{1,0:T(8,128)S(1)} collective-permute-done((f32[24,512]{1,0:T(8,128)}, f32[24,512]{1,0:T(8,128)S(1)}, u32[]{:S(2)}, u32[]{:S(2)}) %collective-permute-start.7) | collective-permute-done | bytes 49184 | tf_op jit(solution)/shard_map/ppermute | solution.py:396
  33.2 0.6 %collective-permute-done.8.refs_2_ = f32[24,512]{1,0:T(8,128)S(1)} collective-permute-done((f32[24,512]{1,0:T(8,128)}, f32[24,512]{1,0:T(8,128)S(1)}, u32[]{:S(2)}, u32[]{:S(2)}) %collective-permute-start.8) | collective-permute-done | bytes 49184 | tf_op jit(solution)/shard_map/ppermute | solution.py:396
  33.9 0.7 %collective-permute-done.9.refs_3_ = f32[24,512]{1,0:T(8,128)S(1)} collective-permute-done((f32[24,512]{1,0:T(8,128)}, f32[24,512]{1,0:T(8,128)S(1)}, u32[]{:S(2)}, u32[]{:S(2)}) %collective-permute-start.9) | collective-permute-done | bytes 49184 | tf_op jit(solution)/shard_map/ppermute | solution.py:396
  34.6 0.0 copy-done.7
  34.6 0.6 %copy-done.9 = f32[24,512]{1,0:T(8,128)} copy-done((f32[24,512]{1,0:T(8,128)}, f32[24,512]{1,0:T(8,128)S(1)}, u32[]{:S(2)}) %copy-start.9) | copy-done | bytes 49176
  35.2 5.6 %gather.1 = (f32[16,16,16]{2,1,0:T(8,128)}, f32[128,128]{1,0:T(8,128)}) custom-call(f32[24,512]{1,0:T(8,128)} %get-tuple-element.8.refs_0_, f32[24,512]{1,0:T(8,128)} %copy-done.7, f32[24,512]{1,0:T(8,128)} %copy-done.8, f32[24,512]{1,0:T(8,128)} %copy-done.9, s32[4,4,8]{2,1,0:T(4,128)} %refs_4_.1, f32[128,128]{1,0:T(8,128)} %bitcast.6, f32[128,128]{1,0:T(8,128)} %bitcast.8, ...), custom_call_target="tpu_custom_call" | custom-call | tf_op jit(solution)/shard_map/gather/pallas_call | solution.py:399
  (11 shorter events, 0.0 us)
Async XLA Ops:
  6.3 11.3 %collective-permute-start.6 = (f32[24,512]{1,0:T(8,128)}, f32[24,512]{1,0:T(8,128)S(1)}, u32[]{:S(2)}, u32[]{:S(2)}) collective-permute-start(f32[24,512]{1,0:T(8,128)} %spread.1.refs_0_), channel_id=1, source_target_pairs={{0,7},{1,4},{2,5},{3,6},{4,3},{5,0},{6,1},{7,2},{8,15},{9,12},{10,... | collective-permute-start | bytes 147464 | tf_op jit(solution)/shard_map/ppermute | solution.py:371
  12.3 6.4 %collective-permute-start.5 = (f32[24,512]{1,0:T(8,128)}, f32[24,512]{1,0:T(8,128)S(1)}, u32[]{:S(2)}, u32[]{:S(2)}) collective-permute-start(f32[24,512]{1,0:T(8,128)} %spread.1.refs_0_), channel_id=1, source_target_pairs={{0,6},{1,7},{2,4},{3,5},{4,2},{5,3},{6,0},{7,1},{8,14},{9,15},{10,... | collective-permute-start | bytes 147464 | tf_op jit(solution)/shard_map/ppermute | solution.py:371
  12.3 7.1 %collective-permute-start.4 = (f32[24,512]{1,0:T(8,128)}, f32[24,512]{1,0:T(8,128)S(1)}, u32[]{:S(2)}, u32[]{:S(2)}) collective-permute-start(f32[24,512]{1,0:T(8,128)} %spread.1.refs_0_), channel_id=1, source_target_pairs={{0,5},{1,6},{2,7},{3,4},{4,1},{5,2},{6,3},{7,0},{8,13},{9,14},{10,... | collective-permute-start | bytes 147464 | tf_op jit(solution)/shard_map/ppermute | solution.py:371
  14.2 5.3 %collective-permute-start.3 = (f32[24,512]{1,0:T(8,128)}, f32[24,512]{1,0:T(8,128)S(1)}, u32[]{:S(2)}, u32[]{:S(2)}) collective-permute-start(f32[24,512]{1,0:T(8,128)} %spread.1.refs_0_), channel_id=1, source_target_pairs={{0,4},{1,5},{2,6},{3,7},{4,0},{5,1},{6,2},{7,3},{8,12},{9,13},{10,... | collective-permute-start | bytes 147464 | tf_op jit(solution)/shard_map/ppermute | solution.py:371
  14.7 4.9 %collective-permute-start.2 = (f32[24,512]{1,0:T(8,128)}, f32[24,512]{1,0:T(8,128)S(1)}, u32[]{:S(2)}, u32[]{:S(2)}) collective-permute-start(f32[24,512]{1,0:T(8,128)} %spread.1.refs_0_), channel_id=1, source_target_pairs={{0,3},{1,0},{2,1},{3,2},{4,7},{5,4},{6,5},{7,6},{8,11},{9,8},{10,9... | collective-permute-start | bytes 147464 | tf_op jit(solution)/shard_map/ppermute | solution.py:371
  17.6 7.2 %copy-start = (f32[24,512]{1,0:T(8,128)}, f32[24,512]{1,0:T(8,128)S(1)}, u32[]{:S(2)}) copy-start(f32[24,512]{1,0:T(8,128)S(1)} %collective-permute-done.6.refs_7_) | copy-start | bytes 147460
  17.6 5.4 %collective-permute-start.1 = (f32[24,512]{1,0:T(8,128)}, f32[24,512]{1,0:T(8,128)S(1)}, u32[]{:S(2)}, u32[]{:S(2)}) collective-permute-start(f32[24,512]{1,0:T(8,128)} %spread.1.refs_0_), channel_id=1, source_target_pairs={{0,2},{1,3},{2,0},{3,1},{4,6},{5,7},{6,4},{7,5},{8,10},{9,11},{10,... | collective-permute-start | bytes 147464 | tf_op jit(solution)/shard_map/ppermute | solution.py:371
  18.7 6.1 %copy-start.1 = (f32[24,512]{1,0:T(8,128)}, f32[24,512]{1,0:T(8,128)S(1)}, u32[]{:S(2)}) copy-start(f32[24,512]{1,0:T(8,128)S(1)} %collective-permute-done.5.refs_6_) | copy-start | bytes 147460
  18.7 6.1 %collective-permute-start = (f32[24,512]{1,0:T(8,128)}, f32[24,512]{1,0:T(8,128)S(1)}, u32[]{:S(2)}, u32[]{:S(2)}) collective-permute-start(f32[24,512]{1,0:T(8,128)} %spread.1.refs_0_), channel_id=1, source_target_pairs={{0,1},{1,2},{2,3},{3,0},{4,5},{5,6},{6,7},{7,4},{8,9},{9,10},{10,1... | collective-permute-start | bytes 147464 | tf_op jit(solution)/shard_map/ppermute | solution.py:371
  19.4 5.4 %copy-start.2 = (f32[24,512]{1,0:T(8,128)}, f32[24,512]{1,0:T(8,128)S(1)}, u32[]{:S(2)}) copy-start(f32[24,512]{1,0:T(8,128)S(1)} %collective-permute-done.4.refs_5_) | copy-start | bytes 147460
  19.5 5.3 %copy-start.3 = (f32[24,512]{1,0:T(8,128)}, f32[24,512]{1,0:T(8,128)S(1)}, u32[]{:S(2)}) copy-start(f32[24,512]{1,0:T(8,128)S(1)} %collective-permute-done.3.refs_4_) | copy-start | bytes 147460
  19.6 5.2 %copy-start.4 = (f32[24,512]{1,0:T(8,128)}, f32[24,512]{1,0:T(8,128)S(1)}, u32[]{:S(2)}) copy-start(f32[24,512]{1,0:T(8,128)S(1)} %collective-permute-done.2.refs_3_) | copy-start | bytes 147460
  23.0 1.8 %copy-start.5 = (f32[24,512]{1,0:T(8,128)}, f32[24,512]{1,0:T(8,128)S(1)}, u32[]{:S(2)}) copy-start(f32[24,512]{1,0:T(8,128)S(1)} %collective-permute-done.1.refs_2_) | copy-start | bytes 147460
  24.8 0.6 %copy-start.6 = (f32[24,512]{1,0:T(8,128)}, f32[24,512]{1,0:T(8,128)S(1)}, u32[]{:S(2)}) copy-start(f32[24,512]{1,0:T(8,128)S(1)} %collective-permute-done.refs_1_) | copy-start | bytes 147460
  29.5 3.7 %collective-permute-start.7 = (f32[24,512]{1,0:T(8,128)}, f32[24,512]{1,0:T(8,128)S(1)}, u32[]{:S(2)}, u32[]{:S(2)}) collective-permute-start(f32[24,512]{1,0:T(8,128)} %get-tuple-element.9), channel_id=1, source_target_pairs={{0,8},{8,16},{16,24},{24,0},{1,9},{9,17},{17,25},{25,1},{2,10},{10... | collective-permute-start | bytes 147464 | tf_op jit(solution)/shard_map/ppermute | solution.py:396
  29.5 4.4 %collective-permute-start.8 = (f32[24,512]{1,0:T(8,128)}, f32[24,512]{1,0:T(8,128)S(1)}, u32[]{:S(2)}, u32[]{:S(2)}) collective-permute-start(f32[24,512]{1,0:T(8,128)} %get-tuple-element.10), channel_id=1, source_target_pairs={{0,16},{8,24},{16,0},{24,8},{1,17},{9,25},{17,1},{25,9},{2,18},{10... | collective-permute-start | bytes 147464 | tf_op jit(solution)/shard_map/ppermute | solution.py:396
  31.1 3.5 %collective-permute-start.9 = (f32[24,512]{1,0:T(8,128)}, f32[24,512]{1,0:T(8,128)S(1)}, u32[]{:S(2)}, u32[]{:S(2)}) collective-permute-start(f32[24,512]{1,0:T(8,128)} %get-tuple-element.11), channel_id=1, source_target_pairs={{0,24},{8,0},{16,8},{24,16},{1,25},{9,1},{17,9},{25,17},{2,26},{10... | collective-permute-start | bytes 147464 | tf_op jit(solution)/shard_map/ppermute | solution.py:396
  33.2 1.3 %copy-start.7 = (f32[24,512]{1,0:T(8,128)}, f32[24,512]{1,0:T(8,128)S(1)}, u32[]{:S(2)}) copy-start(f32[24,512]{1,0:T(8,128)S(1)} %collective-permute-done.7.refs_1_) | copy-start | bytes 147460
  33.9 0.7 %copy-start.8 = (f32[24,512]{1,0:T(8,128)}, f32[24,512]{1,0:T(8,128)S(1)}, u32[]{:S(2)}) copy-start(f32[24,512]{1,0:T(8,128)S(1)} %collective-permute-done.8.refs_2_) | copy-start | bytes 147460
  34.6 0.6 %copy-start.9 = (f32[24,512]{1,0:T(8,128)}, f32[24,512]{1,0:T(8,128)S(1)}, u32[]{:S(2)}) copy-start(f32[24,512]{1,0:T(8,128)S(1)} %collective-permute-done.9.refs_3_) | copy-start | bytes 147460

commit v2 on v1

v2 whole, which is shorter than its diff:
```python
import functools
import math

import jax
import jax.numpy as jnp
import numpy as np
from jax import lax
from jax.experimental import pallas as pl
from jax.experimental.pallas import tpu as pltpu
from jax.sharding import PartitionSpec as P

R = 8
LANES = 128
TERMS = 5
SLOT = LANES // TERMS
RIM = 4
TAPS = (-0.0625, 0.0, 0.5625, 1.0, 0.5625, 0.0, -0.0625)
highest = lax.Precision.HIGHEST


def profile(family, offset):
    if family == 0:
        return math.exp(-((offset / (0.4 * R)) ** 2))
    if family == 1:
        return math.exp(-((offset / (0.8 * R)) ** 2))
    return 1.0 / (1.0 + (offset / R) ** 2)


def norm_factor(family):
    return sum(profile(family, float(o)) ** 2 for o in range(-R, R + 1)) ** 1.5


def stencil(points, family):
    matrix = np.zeros((points, points))
    for i in range(points):
        for k in range(max(0, i - R), min(points, i + R + 1)):
            matrix[i, k] = profile(family, float(k - i))
    return matrix


def restriction(points):
    matrix = np.zeros((points // 2, points))
    for i in range(points // 2):
        for k, tap in enumerate(TAPS):
            if 0 <= 2 * i + k - 3 < points:
                matrix[i, 2 * i + k - 3] += tap
    return matrix


def term_matrices(points):
    q_one = restriction(points)
    q_two = restriction(points // 2)
    coarse = points // 4
    far = np.array([[profile(2, float(k - i)) for k in range(coarse)] for i in range(coarse)])
    down = q_two @ q_one
    return [
        stencil(points, 0),
        stencil(points, 1),
        q_one.T @ stencil(points // 2, 0) @ q_one,
        q_one.T @ stencil(points // 2, 1) @ q_one,
        down.T @ far @ down,
    ]


def term_scales():
    n = [norm_factor(f) for f in range(3)]
    return [1.0 / n[0], 1.0 / n[1], 0.5 / n[0], 0.5 / n[1], 0.5 / n[2]]


def windowed(points, count):
    local = points // count
    width = local + RIM
    index = np.arange(count)[:, None] * local + np.arange(width)[None, :] - RIM // 2
    inside = (index >= 0) & (index < points)
    clipped = np.clip(index, 0, points - 1)
    both = inside[:, :, None, None] & inside[None, None]
    return np.stack(
        [np.where(both, m[clipped[:, :, None, None], clipped[None, None]], 0.0) for m in term_matrices(points)]
    )


def round_up(value, step):
    return -(-value // step) * step


class Plan:
    def __init__(self, nbins, counts):
        self.nbins = nbins
        self.counts = counts
        self.local = (4 * nbins[0], 4 * nbins[1], 2 * nbins[2])
        self.width = tuple(v + RIM for v in self.local)
        self.points = tuple(v * c for v, c in zip(self.local, counts))
        self.xp = round_up(self.width[0], 8)
        self.zp = round_up(self.width[2], 8)
        self.chunks = -(-self.width[1] // TERMS)
        self.lanes = self.chunks * LANES
        self.columns = nbins[0] * nbins[1]
        self.mid = self.counts[1] * self.lanes
        self.pair = 2 if counts[0] % 2 == 0 else 1
        assert self.columns * nbins[2] == LANES and nbins[2] == 8 and self.columns % 2 == 0
        assert TERMS * self.zp <= LANES and self.width[0] <= SLOT

    def place_matrix(self):
        nbx, nby, _ = self.nbins
        m = np.zeros((self.width[1] * self.xp, self.columns * 64), np.float32)
        for a in range(nbx):
            for b in range(nby):
                for i in range(8):
                    for j in range(8):
                        m[(4 * b + j) * self.xp + 4 * a + i, (a * nby + b) * 64 + i * 8 + j] = 1.0
        return jnp.asarray(m, jnp.bfloat16)

    def pick_matrix(self):
        nbx, nby, _ = self.nbins
        m = np.zeros((self.columns * 64, self.lanes), np.float32)
        for a in range(nbx):
            for b in range(nby):
                for i in range(8):
                    for j in range(8):
                        chunk, part = divmod(4 * b + j, TERMS)
                        m[(a * nby + b) * 64 + i * 8 + j, chunk * LANES + part * SLOT + 4 * a + i] = 1.0
        return jnp.asarray(m, jnp.bfloat16)

    def x_table(self):
        nx, width = self.counts[0], self.width[0]
        m = windowed(self.points[0], nx)
        table = np.zeros((nx, nx * self.xp, LANES), np.float32)
        for d in range(nx):
            for o in range(nx):
                source = self.x_source(d, o)
                for t in range(TERMS):
                    table[d, o * self.xp : o * self.xp + width, t * SLOT : t * SLOT + width] = (
                        m[t, d, :, source, :].T
                    )
        return jnp.asarray(table)

    def x_source(self, device, order):
        pair = self.pair
        shift, other = divmod(order, pair)
        return (device // pair - shift) % (self.counts[0] // pair) * pair + (device % pair ^ other)

    def y_table(self):
        ny, width = self.counts[1], self.width[1]
        m = windowed(self.points[1], ny)
        table = np.zeros((ny, ny * width, self.chunks * TERMS, LANES), np.float32)
        for d in range(ny):
            for o in range(ny):
                for t in range(TERMS):
                    block = m[t, d, :, (d - o) % ny, :]
                    table[d, o * width : (o + 1) * width, :width, t * SLOT : (t + 1) * SLOT] = block.T[:, :, None]
        return jnp.asarray(table.reshape(ny, ny * width * self.chunks * TERMS, LANES))

    def z_table(self):
        nz, width = self.counts[2], self.width[2]
        m = windowed(self.points[2], nz)
        scales = term_scales()
        table = np.zeros((nz, nz * self.zp, TERMS * self.zp), np.float32)
        for d in range(nz):
            for o in range(nz):
                for t in range(TERMS):
                    table[d, o * self.zp : o * self.zp + width, t * self.zp : t * self.zp + width] = (
                        scales[t] * m[t, (d + o) % nz, :, d, :]
                    )
        return jnp.asarray(table)


def bspline(spacing):
    a = jnp.abs(spacing)
    u = jnp.maximum(2.0 - a, 0.0)
    v = jnp.maximum(1.0 - a, 0.0)
    return u * u * u * (1.0 / 6.0) - v * v * v * (2.0 / 3.0)


def counts_row(counts, nbins):
    nbx, nby, nbz = nbins
    rows = jnp.concatenate([counts[a].astype(jnp.float32) for a in range(nbx)], axis=0)
    spread = lax.broadcasted_iota(jnp.int32, (nbz, LANES), 1) % nbz == lax.broadcasted_iota(
        jnp.int32, (nbz, LANES), 0
    )
    tiled = jnp.dot(rows, spread.astype(jnp.float32), precision=highest)
    own = lax.broadcasted_iota(jnp.int32, tiled.shape, 1) // nbz == lax.broadcasted_iota(
        jnp.int32, tiled.shape, 0
    )
    return jnp.sum(jnp.where(own, tiled, 0.0), axis=0, keepdims=True)


def split_two(value):
    high = value.astype(jnp.bfloat16)
    low = (value - high.astype(jnp.float32)).astype(jnp.bfloat16)
    return high, low


def spread_kernel(plan, *refs):
    hbm, (out_ref, bx_s, by_s, bz_s, row_ref) = refs[:6], refs[6:11]
    local, (patch_s, turned_s, column_s, sems) = refs[11:17], refs[17:]
    copies = [pltpu.make_async_copy(a, b, sems.at[n]) for n, (a, b) in enumerate(zip(hbm, local))]
    for copy in copies:
        copy.start()
    x_ref, y_ref, z_ref, counts_ref, charge_ref, place_s = local
    slots = charge_ref.shape[1]
    for n, (ref, weight, points) in enumerate(((x_ref, bx_s, 8), (y_ref, by_s, 8), (z_ref, bz_s, 6))):
        copies[n].wait()
        along = ref[...].T
        for i in range(points):
            weight[i] = bspline(along + (2.0 - i))
    copies[3].wait()
    row = counts_row(counts_ref, plan.nbins)
    row_ref[...] = jnp.broadcast_to(row, row_ref.shape)
    slot = lax.broadcasted_iota(jnp.int32, (slots, LANES), 0).astype(jnp.float32)
    copies[4].wait()
    weighted = jnp.where(slot < row, charge_ref[...].T, 0.0)

    def one_x(i, carry):
        weight_x = bx_s[i] * weighted
        rows = [[] for _ in range(6)]
        for j in range(8):
            product = weight_x * by_s[j]
            for k in range(6):
                rows[k].append(jnp.sum(product * bz_s[k], axis=0, keepdims=True))
        for k in range(6):
            patch_s[pl.ds(pl.multiple_of(k * 64 + i * 8, 8), 8), :] = jnp.concatenate(rows[k], axis=0)
        return carry

    lax.fori_loop(0, 8, one_x, 0)
    for h in range(3):
        turned_s[:, h * LANES : (h + 1) * LANES] = patch_s[h * LANES : (h + 1) * LANES, :].T
    column_s[...] = jnp.zeros_like(column_s)
    nbz = plan.nbins[2]
    half = plan.zp // 2
    lane = lax.broadcasted_iota(jnp.int32, (nbz, LANES), 1)
    for pair in range(plan.columns // 2):
        for s in range(3):
            left = turned_s[2 * pair * nbz : (2 * pair + 1) * nbz, s * LANES : (s + 1) * LANES]
            right = turned_s[(2 * pair + 1) * nbz : (2 * pair + 2) * nbz, s * LANES : (s + 1) * LANES]
            even = jnp.where(lane < 64, left, pltpu.roll(right, 64, 1))
            odd = jnp.where(lane < 64, pltpu.roll(left, 64, 1), right)
            for c, piece in enumerate((even, odd)):
                at = (pl.ds(pair * plan.zp + 2 * s + c, nbz, stride=2), slice(None))
                column_s[at] = column_s[at] + piece
    columns = jnp.concatenate(
        [column_s[p * plan.zp : (p + 1) * plan.zp, :] for p in range(plan.columns // 2)], axis=1
    )
    high, low = split_two(columns)
    copies[5].wait()
    place = place_s[...]
    contract = (((1,), (1,)), ((), ()))
    grid = lax.dot_general(place, high, contract, preferred_element_type=jnp.float32) + lax.dot_general(
        place, low, contract, preferred_element_type=jnp.float32
    )
    grid = jnp.concatenate([grid, jnp.zeros((grid.shape[0], LANES - plan.zp), jnp.float32)], axis=1)
    xp = plan.xp
    group = lax.broadcasted_iota(jnp.int32, (xp, LANES), 1) // plan.zp
    for chunk in range(plan.chunks):
        merged = jnp.zeros((xp, LANES), jnp.float32)
        for b in range(TERMS):
            y = chunk * TERMS + b
            if y < plan.width[1]:
                piece = grid[y * xp : (y + 1) * xp, :]
                moved = pltpu.roll(piece, b * plan.zp, 1) if b else piece
                merged = jnp.where(group == b, moved, merged)
        out_ref[:, chunk * LANES : (chunk + 1) * LANES] = merged


def solve_kernel(plan, *refs):
    nx, ny, nz = plan.counts
    blocks = refs[: nx * ny]
    tables = refs[nx * ny : nx * ny + 3]
    outs = refs[nx * ny + 3 : nx * ny + 3 + nz]
    mid_s, term_s, ytab_s, sem = refs[nx * ny + 3 + nz :]
    copy = pltpu.make_async_copy(tables[1].at[lax.axis_index("gy")], ytab_s, sem)
    copy.start()
    x_matrix = tables[0][lax.axis_index("gx")]
    wy = plan.width[1]
    zp = plan.zp
    span = plan.chunks * TERMS
    for oy in range(ny):
        gathered = jnp.concatenate([blocks[ox * ny + oy][...] for ox in range(nx)], axis=0)
        mid_s[oy * plan.lanes : (oy + 1) * plan.lanes, :] = lax.dot_general(
            gathered, x_matrix, (((0,), (0,)), ((), ())), precision=highest,
            preferred_element_type=jnp.float32,
        )
    slot = lax.broadcasted_iota(jnp.int32, (zp, LANES), 1) // SLOT
    copy.wait()
    for chunk in range(plan.chunks):
        sums = [jnp.zeros((zp, LANES), jnp.float32) for _ in range(TERMS)]
        for oy in range(ny):
            for y in range(wy):
                at = oy * plan.lanes + (y // TERMS) * LANES + (y % TERMS) * zp
                value = mid_s[at : at + zp, :]
                for b in range(TERMS):
                    row = (oy * wy + y) * span + chunk * TERMS + b
                    sums[b] = sums[b] + value * ytab_s[row : row + 1, :]
        for t in range(TERMS):
            merged = jnp.zeros((zp, LANES), jnp.float32)
            for b in range(TERMS):
                shift = (SLOT * (b - t)) % LANES
                moved = pltpu.roll(sums[b], shift, 1) if shift else sums[b]
                merged = jnp.where(slot == b, moved, merged)
            term_s[t * zp : (t + 1) * zp, chunk * LANES : (chunk + 1) * LANES] = merged
    z_matrix = tables[2][lax.axis_index("gz")]
    result = jnp.dot(z_matrix, term_s[...], precision=highest, preferred_element_type=jnp.float32)
    for o in range(nz):
        outs[o][...] = result[o * zp : (o + 1) * zp, :]


def gather_kernel(plan, *refs):
    nz = plan.counts[2]
    parts = refs[:nz]
    bx_s, by_s, bz_s, row_ref, pick_ref, fine_ref, atom_ref = refs[nz : nz + 7]
    field_s, column_s, turned_s, patch_s = refs[nz + 7 :]
    zp = plan.zp
    lx, ly, lz = plan.local
    total = parts[0][...]
    for part in parts[1:]:
        total = total + part[...]
    high, low = split_two(total)
    pick = pick_ref[...]
    contract = (((1,), (1,)), ((), ()))
    columns = lax.dot_general(high, pick, contract, preferred_element_type=jnp.float32) + lax.dot_general(
        low, pick, contract, preferred_element_type=jnp.float32
    )
    for pair in range(plan.columns // 2):
        column_s[pair * zp : (pair + 1) * zp, :] = columns[:, pair * LANES : (pair + 1) * LANES]
    for chunk in range(plan.chunks):
        turned = total[:, chunk * LANES : (chunk + 1) * LANES].T
        field_s[chunk * LANES : (chunk + 1) * LANES, :zp] = turned
    for y in range(ly):
        chunk, b = divmod(y + 2, TERMS)
        at = chunk * LANES + b * SLOT + 2
        fine_ref[:, y, :] = field_s[at : at + lx, 2 : 2 + lz]
    nbz = plan.nbins[2]
    lane = lax.broadcasted_iota(jnp.int32, (nbz, LANES), 1)
    for pair in range(plan.columns // 2):
        for s in range(3):
            even = column_s[pl.ds(pair * zp + 2 * s, nbz, stride=2), :]
            odd = column_s[pl.ds(pair * zp + 2 * s + 1, nbz, stride=2), :]
            turned_s[2 * pair * nbz : (2 * pair + 1) * nbz, s * LANES : (s + 1) * LANES] = jnp.where(
                lane < 64, even, pltpu.roll(odd, 64, 1)
            )
            turned_s[(2 * pair + 1) * nbz : (2 * pair + 2) * nbz, s * LANES : (s + 1) * LANES] = jnp.where(
                lane < 64, pltpu.roll(even, 64, 1), odd
            )
    for h in range(3):
        patch_s[h * LANES : (h + 1) * LANES, :] = turned_s[:, h * LANES : (h + 1) * LANES].T
    slots = atom_ref.shape[1]

    def one_x(i, result):
        inner = jnp.zeros((slots, LANES), jnp.float32)
        rows = [patch_s[pl.ds(pl.multiple_of(k * 64 + i * 8, 8), 8), :] for k in range(6)]
        for j in range(8):
            along_z = rows[0][j : j + 1, :] * bz_s[0]
            for k in range(1, 6):
                along_z = along_z + rows[k][j : j + 1, :] * bz_s[k]
            inner = inner + along_z * by_s[j]
        return result + inner * bx_s[i]

    result = lax.fori_loop(0, 8, one_x, jnp.zeros((slots, LANES), jnp.float32))
    row = row_ref[0:1, :]
    slot = lax.broadcasted_iota(jnp.int32, (slots, LANES), 0).astype(jnp.float32)
    atom_ref[...] = jnp.where(slot < row, result, 0.0).T


def body(charges, offset_x, offset_y, offset_z, counts):
    nbins = charges.shape[:3]
    slots = charges.shape[3]
    sizes = tuple(lax.axis_size(a) for a in ("gx", "gy", "gz"))
    nx, ny, nz = sizes
    plan = Plan(nbins, sizes)
    flat = [v.reshape(LANES, slots) for v in (charges, offset_x, offset_y, offset_z)]
    vmem = pl.BlockSpec(memory_space=pltpu.VMEM)
    hbm = pl.BlockSpec(memory_space=pl.ANY)
    f32 = jnp.float32
    params = pltpu.CompilerParams(vmem_limit_bytes=40 << 20)
    place, pick = plan.place_matrix(), plan.pick_matrix()

    spread, *weights = pl.pallas_call(
        functools.partial(spread_kernel, plan),
        out_shape=[
            pltpu.VMEM((plan.xp, plan.lanes), f32),
            pltpu.VMEM((8, slots, LANES), f32),
            pltpu.VMEM((8, slots, LANES), f32),
            pltpu.VMEM((6, slots, LANES), f32),
            pltpu.VMEM((8, LANES), f32),
        ],
        in_specs=[pl.BlockSpec(memory_space=pltpu.HBM)] * 6,
        out_specs=[vmem] * 5,
        scratch_shapes=[
            pltpu.VMEM((LANES, slots), f32),
            pltpu.VMEM((LANES, slots), f32),
            pltpu.VMEM((LANES, slots), f32),
            pltpu.VMEM(nbins, jnp.int32),
            pltpu.VMEM((LANES, slots), f32),
            pltpu.VMEM(place.shape, place.dtype),
            pltpu.VMEM((384, LANES), f32),
            pltpu.VMEM((LANES, 384), f32),
            pltpu.VMEM((plan.columns // 2 * plan.zp, LANES), f32),
            pltpu.SemaphoreType.DMA((6,)),
        ],
        compiler_params=params,
        name="spread",
    )(*(pltpu.with_memory_space_constraint(v, pltpu.HBM) for v in (*flat[1:], counts, flat[0], place)))

    def near(value):
        return pltpu.with_memory_space_constraint(value, pltpu.VMEM)

    def moved(value, axis, pairs):
        return near(lax.ppermute(value, axis, pairs))

    def from_chip(shift, oy):
        if shift == 0 and oy == 0:
            return spread
        pairs = [
            (sx * ny + sy, (sx // pair + shift) % (nx // pair) * pair * ny + sx % pair * ny + (sy + oy) % ny)
            for sx in range(nx)
            for sy in range(ny)
        ]
        return moved(spread, ("gx", "gy"), pairs)

    pair = plan.pair
    blocks = []
    for shift in range(nx // pair):
        own = [from_chip(shift, oy) for oy in range(ny)]
        blocks += own
        if pair == 2:
            blocks += [moved(v, "gx", [(s, s ^ 1) for s in range(nx)]) for v in own]
    tables = (plan.x_table(), plan.y_table(), plan.z_table())
    outs = pl.pallas_call(
        functools.partial(solve_kernel, plan),
        out_shape=[pltpu.VMEM((plan.zp, plan.lanes), f32)] * nz,
        in_specs=[vmem] * (nx * ny) + [vmem, hbm, vmem],
        out_specs=[vmem] * nz,
        scratch_shapes=[
            pltpu.VMEM((plan.mid, LANES), f32),
            pltpu.VMEM((TERMS * plan.zp, plan.lanes), f32),
            pltpu.VMEM(tables[1].shape[1:], f32),
            pltpu.SemaphoreType.DMA(()),
        ],
        compiler_params=params,
        name="solve",
    )(*blocks, *tables)
    parts = [outs[0]] + [
        moved(outs[o], "gz", [(s, (s + o) % nz) for s in range(nz)]) for o in range(1, nz)
    ]
    fine, atom = pl.pallas_call(
        functools.partial(gather_kernel, plan),
        out_shape=[
            jax.ShapeDtypeStruct(plan.local, f32),
            jax.ShapeDtypeStruct((LANES, slots), f32),
        ],
        in_specs=[vmem] * (nz + 5),
        out_specs=[vmem, vmem],
        scratch_shapes=[
            pltpu.VMEM((plan.lanes, LANES), f32),
            pltpu.VMEM((plan.columns // 2 * plan.zp, LANES), f32),
            pltpu.VMEM((LANES, 384), f32),
            pltpu.VMEM((384, LANES), f32),
        ],
        compiler_params=params,
        name="gather",
    )(*parts, *weights, pick)
    return fine, atom.reshape(charges.shape)


def solution(mesh):
    in_specs = (
        P("gx", "gy", "gz", None),
        P("gx", "gy", "gz", None),
        P("gx", "gy", "gz", None),
        P("gx", "gy", "gz", None),
        P("gx", "gy", "gz"),
    )
    out_specs = (P("gx", "gy", "gz"), P("gx", "gy", "gz", None))
    return jax.shard_map(body, mesh=mesh, in_specs=in_specs, out_specs=out_specs, check_vma=False)
```

time: 41.1 us -> 30.4 us (0.74)
  starting transfers between devices: 16.1 us -> 10.2 us
  Pallas kernels: 15.4 us -> 11.2 us
  local copies, waits for them, and re-layouts: 1.26 us -> 0.03 us
  waiting for transfers between devices: 7.48 us -> 8.03 us
    ppermute x10, starting transfers between devices: 16.1 us -> 10.2 us  [moved(): return near(lax.ppermute(value, axis, pairs))]
    pallas_call x2, Pallas kernels: 9.72 us -> 7.54 us  [the longest x1 5.23 us: body(): pl.pallas_call(functools.partial(spread_kernel, plan), out_shape=[pltpu.V...]
    pallas_call x1, Pallas kernels: 5.65 us -> 3.7 us  [body(): pl.pallas_call(functools.partial(gather_kernel, plan), out_shape=[jax.Sha...]
    unnamed x20 -> x8, local copies, waits for them, and re-layouts: 1.26 us -> 0.03 us
    ppermute x10, waiting for transfers between devices: 7.48 us -> 8.03 us  [moved(): return near(lax.ppermute(value, axis, pairs))]
  transfers between devices with their start and end apart: 10 -> 10, of which waited for: 7 -> 8; matrix products, arithmetic and copies ran while one was open for 0% -> 0% of each run, Pallas kernels for 0% -> 0%
where the time goes in v2:
time: 30.4 us; the launch traced here: 30.2 us
  Pallas kernels  11.2 us (37%)
  starting transfers between devices  10.2 us (34%)
  waiting for transfers between devices  8.03 us (26%)
  between operations  0.69 us (2%)
    ppermute x10, starting transfers between devices, moved(): return near(lax.ppermute(value, axis, pairs))  10.2 us
    ppermute x10, waiting for transfers between devices, moved(): return near(lax.ppermute(value, axis, pairs))  8.03 us
    pallas_call x1, Pallas kernels, body(): pl.pallas_call(functools.partial(spread_kernel, plan), out_shape=[pltpu.V...  5.23 us
    pallas_call x1, Pallas kernels, body(): pl.pallas_call(functools.partial(gather_kernel, plan), out_shape=[jax.Sha...  3.7 us
    pallas_call x1, Pallas kernels, body(): pl.pallas_call(functools.partial(solve_kernel, plan), out_shape=[pltpu.VM...  2.31 us
  transfers between devices with their start and end apart: 10, of which 8 were waited for; matrix products, arithmetic and copies ran while one was open for 0% of the time, Pallas kernels for 0%

profile of v2, /device:TPU:0, one launch (start us, length us, event | category | flops | bytes accessed | tf_op | source)
XLA Modules:
  0.0 30.2 jit_solution(4234915777002251596)
XLA Ops:
  0.6 0.0 copy-start.1
  0.6 0.0 copy-start.2
  0.7 0.0 copy-start.3
  0.7 5.2 %spread.1 = (f32[24,512]{1,0:T(8,128)S(1)}, f32[8,128,128]{2,1,0:T(8,128)S(1)}, f32[8,128,128]{2,1,0:T(8,128)S(1)}, f32[6,128,128]{2,1,0:T(8,128)S(1)}, f32[8,128]{1,0:T(8,128)S(1)}) custom-call(f32[128,128]{1,0:T(8,128)} %bitcast.5, f32[128,128]{1,0:T(8,128)} %bitcast.6, f32[128,128]{1,0:T(8,128)} %bitcast.7, s32[4,4,8]{2,1,0:T(4,128)} %refs_3_.1, ...), custom_call_target="tpu_custom_call" | custom-call | tf_op jit(solution)/shard_map/spread/pallas_call | solution.py:376
  5.9 0.0 copy-start
  5.9 4.0 %collective-permute-start.4 = (f32[24,512]{1,0:T(8,128)S(1)}, f32[24,512]{1,0:T(8,128)S(1)}, u32[]{:S(2)}, u32[]{:S(2)}) collective-permute-start(f32[24,512]{1,0:T(8,128)S(1)} %get-tuple-element.13.refs_0_), channel_id=1, source_target_pairs={{0,20},{4,16},{8,28},{12,24},{16,4},{20,0},{24,12},{28,8},{1,21},{... | collective-permute-start | bytes 147464 | tf_op jit(solution)/shard_map/ppermute | solution.py:407
  9.9 0.5 %collective-permute-start.3 = (f32[24,512]{1,0:T(8,128)S(1)}, f32[24,512]{1,0:T(8,128)S(1)}, u32[]{:S(2)}, u32[]{:S(2)}) collective-permute-start(f32[24,512]{1,0:T(8,128)S(1)} %get-tuple-element.13.refs_0_), channel_id=1, source_target_pairs={{0,16},{4,20},{8,24},{12,28},{16,0},{20,4},{24,8},{28,12},{1,17},{... | collective-permute-start | bytes 147464 | tf_op jit(solution)/shard_map/ppermute | solution.py:407
  10.4 0.2 collective-permute-start
  10.6 0.0 collective-permute-start.1
  10.6 1.4 %collective-permute-done.4.refs_5_ = f32[24,512]{1,0:T(8,128)S(1)} collective-permute-done((f32[24,512]{1,0:T(8,128)S(1)}, f32[24,512]{1,0:T(8,128)S(1)}, u32[]{:S(2)}, u32[]{:S(2)}) %collective-permute-start.4) | collective-permute-done | bytes 49184 | tf_op jit(solution)/shard_map/ppermute | solution.py:407
  12.0 0.0 collective-permute-start.6
  12.0 2.0 %collective-permute-done.3.refs_4_ = f32[24,512]{1,0:T(8,128)S(1)} collective-permute-done((f32[24,512]{1,0:T(8,128)S(1)}, f32[24,512]{1,0:T(8,128)S(1)}, u32[]{:S(2)}, u32[]{:S(2)}) %collective-permute-start.3) | collective-permute-done | bytes 49184 | tf_op jit(solution)/shard_map/ppermute | solution.py:407
  14.0 0.0 collective-permute-start.5
  14.0 0.5 %collective-permute-done.refs_1_ = f32[24,512]{1,0:T(8,128)S(1)} collective-permute-done((f32[24,512]{1,0:T(8,128)S(1)}, f32[24,512]{1,0:T(8,128)S(1)}, u32[]{:S(2)}, u32[]{:S(2)}) %collective-permute-start) | collective-permute-done | bytes 49184 | tf_op jit(solution)/shard_map/ppermute | solution.py:407
  14.5 0.0 collective-permute-start.2
  14.5 0.0 collective-permute-done.1.refs_2_
  14.5 0.0 collective-permute-done.6.refs_7_
  14.5 0.7 %collective-permute-done.5.refs_6_ = f32[24,512]{1,0:T(8,128)S(1)} collective-permute-done((f32[24,512]{1,0:T(8,128)S(1)}, f32[24,512]{1,0:T(8,128)S(1)}, u32[]{:S(2)}, u32[]{:S(2)}) %collective-permute-start.5) | collective-permute-done | bytes 49184 | tf_op jit(solution)/shard_map/ppermute | solution.py:407
  15.2 0.5 %collective-permute-done.2.refs_3_ = f32[24,512]{1,0:T(8,128)S(1)} collective-permute-done((f32[24,512]{1,0:T(8,128)S(1)}, f32[24,512]{1,0:T(8,128)S(1)}, u32[]{:S(2)}, u32[]{:S(2)}) %collective-permute-start.2) | collective-permute-done | bytes 49184 | tf_op jit(solution)/shard_map/ppermute | solution.py:407
  15.7 0.0 copy-done.1
  15.7 0.0 copy-done.2
  15.7 0.0 copy-done.3
  15.8 2.3 %solve.1 = (f32[24,512]{1,0:T(8,128)S(1)}, f32[24,512]{1,0:T(8,128)S(1)}, f32[24,512]{1,0:T(8,128)S(1)}, f32[24,512]{1,0:T(8,128)S(1)}) custom-call(f32[24,512]{1,0:T(8,128)S(1)} %get-tuple-element.13.refs_0_, f32[24,512]{1,0:T(8,128)S(1)} %collective-permute-done.refs_1_, f32[24,512]{1,0:T(8,128)S(1)} %collective-permute-done.1.refs_2_, ...), custom_call_target="tpu_custom_call" | custom-call | tf_op jit(solution)/shard_map/solve/pallas_call | solution.py:427
  18.1 1.6 %collective-permute-start.7 = (f32[24,512]{1,0:T(8,128)S(1)}, f32[24,512]{1,0:T(8,128)S(1)}, u32[]{:S(2)}, u32[]{:S(2)}) collective-permute-start(f32[24,512]{1,0:T(8,128)S(1)} %get-tuple-element.15), channel_id=1, source_target_pairs={{0,1},{1,2},{2,3},{3,0},{4,5},{5,6},{6,7},{7,4},{8,9},{9,10},{10,1... | collective-permute-start | bytes 147464 | tf_op jit(solution)/shard_map/ppermute | solution.py:407
  19.7 2.6 %collective-permute-start.8 = (f32[24,512]{1,0:T(8,128)S(1)}, f32[24,512]{1,0:T(8,128)S(1)}, u32[]{:S(2)}, u32[]{:S(2)}) collective-permute-start(f32[24,512]{1,0:T(8,128)S(1)} %get-tuple-element.16), channel_id=1, source_target_pairs={{0,2},{1,3},{2,0},{3,1},{4,6},{5,7},{6,4},{7,5},{8,10},{9,11},{10,... | collective-permute-start | bytes 147464 | tf_op jit(solution)/shard_map/ppermute | solution.py:407
  22.3 1.3 %collective-permute-start.9 = (f32[24,512]{1,0:T(8,128)S(1)}, f32[24,512]{1,0:T(8,128)S(1)}, u32[]{:S(2)}, u32[]{:S(2)}) collective-permute-start(f32[24,512]{1,0:T(8,128)S(1)} %get-tuple-element.17), channel_id=1, source_target_pairs={{0,3},{1,0},{2,1},{3,2},{4,7},{5,4},{6,5},{7,6},{8,11},{9,8},{10,9... | collective-permute-start | bytes 147464 | tf_op jit(solution)/shard_map/ppermute | solution.py:407
  23.6 0.4 %collective-permute-done.7.refs_1_ = f32[24,512]{1,0:T(8,128)S(1)} collective-permute-done((f32[24,512]{1,0:T(8,128)S(1)}, f32[24,512]{1,0:T(8,128)S(1)}, u32[]{:S(2)}, u32[]{:S(2)}) %collective-permute-start.7) | collective-permute-done | bytes 49184 | tf_op jit(solution)/shard_map/ppermute | solution.py:407
  24.0 2.1 %collective-permute-done.8.refs_2_ = f32[24,512]{1,0:T(8,128)S(1)} collective-permute-done((f32[24,512]{1,0:T(8,128)S(1)}, f32[24,512]{1,0:T(8,128)S(1)}, u32[]{:S(2)}, u32[]{:S(2)}) %collective-permute-start.8) | collective-permute-done | bytes 49184 | tf_op jit(solution)/shard_map/ppermute | solution.py:407
  26.2 0.4 %collective-permute-done.9.refs_3_ = f32[24,512]{1,0:T(8,128)S(1)} collective-permute-done((f32[24,512]{1,0:T(8,128)S(1)}, f32[24,512]{1,0:T(8,128)S(1)}, u32[]{:S(2)}, u32[]{:S(2)}) %collective-permute-start.9) | collective-permute-done | bytes 49184 | tf_op jit(solution)/shard_map/ppermute | solution.py:407
  26.5 0.0 copy-done
  26.5 3.7 %gather.1 = (f32[16,16,16]{2,1,0:T(8,128)}, f32[128,128]{1,0:T(8,128)}) custom-call(f32[24,512]{1,0:T(8,128)S(1)} %get-tuple-element.14.refs_0_, f32[24,512]{1,0:T(8,128)S(1)} %collective-permute-done.7.refs_1_, f32[24,512]{1,0:T(8,128)S(1)} %collective-permute-done.8.refs_2_, f32[24,512]{1,0:T(8,128)S(1)} %collective-permute-done.9.refs_3_, ...), custom_call_target="tpu_custom_call" | custom-call | tf_op jit(solution)/shard_map/gather/pallas_call | solution.py:444
Async XLA Ops:
  0.6 15.1 %copy-start.1 = (f32[2,800,128]{2,1,0:T(8,128)S(1)}, f32[2,800,128]{2,1,0:T(8,128)}, u32[]{:S(2)}) copy-start(f32[2,800,128]{2,1,0:T(8,128)} %constant.13.clone.refs_9_) | copy-start | bytes 2457604
  0.6 15.1 %copy-start.2 = (f32[4,96,120]{2,1,0:T(8,128)S(1)}, f32[4,96,120]{2,1,0:T(8,128)}, u32[]{:S(2)}) copy-start(f32[4,96,120]{2,1,0:T(8,128)} %constant.14.clone.refs_10_) | copy-start | bytes 552964
  0.7 15.1 %copy-start.3 = (f32[4,96,128]{2,1,0:T(8,128)S(1)}, f32[4,96,128]{2,1,0:T(8,128)}, u32[]{:S(2)}) copy-start(f32[4,96,128]{2,1,0:T(8,128)} %constant.12.clone.refs_8_) | copy-start | bytes 589828
  5.9 20.6 %copy-start = (bf16[1024,512]{1,0:T(8,128)(2,1)S(1)}, bf16[1024,512]{1,0:T(8,128)(2,1)}, u32[]{:S(2)}) copy-start(bf16[1024,512]{1,0:T(8,128)(2,1)} %constant.11.clone.refs_8_) | copy-start | bytes 3145732
  5.9 6.1 %collective-permute-start.4 = (f32[24,512]{1,0:T(8,128)S(1)}, f32[24,512]{1,0:T(8,128)S(1)}, u32[]{:S(2)}, u32[]{:S(2)}) collective-permute-start(f32[24,512]{1,0:T(8,128)S(1)} %get-tuple-element.13.refs_0_), channel_id=1, source_target_pairs={{0,20},{4,16},{8,28},{12,24},{16,4},{20,0},{24,12},{28,8},{1,21},{... | collective-permute-start | bytes 147464 | tf_op jit(solution)/shard_map/ppermute | solution.py:407
  9.9 4.1 %collective-permute-start.3 = (f32[24,512]{1,0:T(8,128)S(1)}, f32[24,512]{1,0:T(8,128)S(1)}, u32[]{:S(2)}, u32[]{:S(2)}) collective-permute-start(f32[24,512]{1,0:T(8,128)S(1)} %get-tuple-element.13.refs_0_), channel_id=1, source_target_pairs={{0,16},{4,20},{8,24},{12,28},{16,0},{20,4},{24,8},{28,12},{1,17},{... | collective-permute-start | bytes 147464 | tf_op jit(solution)/shard_map/ppermute | solution.py:407
  10.4 4.1 %collective-permute-start = (f32[24,512]{1,0:T(8,128)S(1)}, f32[24,512]{1,0:T(8,128)S(1)}, u32[]{:S(2)}, u32[]{:S(2)}) collective-permute-start(f32[24,512]{1,0:T(8,128)S(1)} %get-tuple-element.13.refs_0_), channel_id=1, source_target_pairs={{0,4},{4,0},{8,12},{12,8},{16,20},{20,16},{24,28},{28,24},{1,5},{5... | collective-permute-start | bytes 147464 | tf_op jit(solution)/shard_map/ppermute | solution.py:407
  10.6 4.0 %collective-permute-start.1 = (f32[24,512]{1,0:T(8,128)S(1)}, f32[24,512]{1,0:T(8,128)S(1)}, u32[]{:S(2)}, u32[]{:S(2)}) collective-permute-start(f32[24,512]{1,0:T(8,128)S(1)} %get-tuple-element.13.refs_0_), channel_id=1, source_target_pairs={{0,8},{8,0},{16,24},{24,16},{1,9},{9,1},{17,25},{25,17},{2,10},{10... | collective-permute-start | bytes 147464 | tf_op jit(solution)/shard_map/ppermute | solution.py:407
  12.0 2.5 %collective-permute-start.6 = (f32[24,512]{1,0:T(8,128)S(1)}, f32[24,512]{1,0:T(8,128)S(1)}, u32[]{:S(2)}, u32[]{:S(2)}) collective-permute-start(f32[24,512]{1,0:T(8,128)S(1)} %collective-permute-done.4.refs_5_), channel_id=1, source_target_pairs={{0,8},{8,0},{16,24},{24,16},{1,9},{9,1},{17,25},{25,17},{2,10},{10... | collective-permute-start | bytes 147464 | tf_op jit(solution)/shard_map/ppermute | solution.py:407
  14.0 1.2 %collective-permute-start.5 = (f32[24,512]{1,0:T(8,128)S(1)}, f32[24,512]{1,0:T(8,128)S(1)}, u32[]{:S(2)}, u32[]{:S(2)}) collective-permute-start(f32[24,512]{1,0:T(8,128)S(1)} %collective-permute-done.3.refs_4_), channel_id=1, source_target_pairs={{0,8},{8,0},{16,24},{24,16},{1,9},{9,1},{17,25},{25,17},{2,10},{10... | collective-permute-start | bytes 147464 | tf_op jit(solution)/shard_map/ppermute | solution.py:407
  14.5 1.2 %collective-permute-start.2 = (f32[24,512]{1,0:T(8,128)S(1)}, f32[24,512]{1,0:T(8,128)S(1)}, u32[]{:S(2)}, u32[]{:S(2)}) collective-permute-start(f32[24,512]{1,0:T(8,128)S(1)} %collective-permute-done.refs_1_), channel_id=1, source_target_pairs={{0,8},{8,0},{16,24},{24,16},{1,9},{9,1},{17,25},{25,17},{2,10},{10... | collective-permute-start | bytes 147464 | tf_op jit(solution)/shard_map/ppermute | solution.py:407
  18.1 5.9 %collective-permute-start.7 = (f32[24,512]{1,0:T(8,128)S(1)}, f32[24,512]{1,0:T(8,128)S(1)}, u32[]{:S(2)}, u32[]{:S(2)}) collective-permute-start(f32[24,512]{1,0:T(8,128)S(1)} %get-tuple-element.15), channel_id=1, source_target_pairs={{0,1},{1,2},{2,3},{3,0},{4,5},{5,6},{6,7},{7,4},{8,9},{9,10},{10,1... | collective-permute-start | bytes 147464 | tf_op jit(solution)/shard_map/ppermute | solution.py:407
  19.7 6.5 %collective-permute-start.8 = (f32[24,512]{1,0:T(8,128)S(1)}, f32[24,512]{1,0:T(8,128)S(1)}, u32[]{:S(2)}, u32[]{:S(2)}) collective-permute-start(f32[24,512]{1,0:T(8,128)S(1)} %get-tuple-element.16), channel_id=1, source_target_pairs={{0,2},{1,3},{2,0},{3,1},{4,6},{5,7},{6,4},{7,5},{8,10},{9,11},{10,... | collective-permute-start | bytes 147464 | tf_op jit(solution)/shard_map/ppermute | solution.py:407
  22.3 4.2 %collective-permute-start.9 = (f32[24,512]{1,0:T(8,128)S(1)}, f32[24,512]{1,0:T(8,128)S(1)}, u32[]{:S(2)}, u32[]{:S(2)}) collective-permute-start(f32[24,512]{1,0:T(8,128)S(1)} %get-tuple-element.17), channel_id=1, source_target_pairs={{0,3},{1,0},{2,1},{3,2},{4,7},{5,4},{6,5},{7,6},{8,11},{9,8},{10,9... | collective-permute-start | bytes 147464 | tf_op jit(solution)/shard_map/ppermute | solution.py:407

commit v3 on v2

--- a/solution.py
+++ b/solution.py
@@ -13,6 +13,7 @@
 LANES = 128
 TERMS = 5
 SLOT = LANES // TERMS
+GROUP = 2
 RIM = 4
 TAPS = (-0.0625, 0.0, 0.5625, 1.0, 0.5625, 0.0, -0.0625)
 highest = lax.Precision.HIGHEST
@@ -171,83 +172,85 @@
     return u * u * u * (1.0 / 6.0) - v * v * v * (2.0 / 3.0)
 
 
-def counts_row(counts, nbins):
-    nbx, nby, nbz = nbins
-    rows = jnp.concatenate([counts[a].astype(jnp.float32) for a in range(nbx)], axis=0)
-    spread = lax.broadcasted_iota(jnp.int32, (nbz, LANES), 1) % nbz == lax.broadcasted_iota(
-        jnp.int32, (nbz, LANES), 0
-    )
-    tiled = jnp.dot(rows, spread.astype(jnp.float32), precision=highest)
-    own = lax.broadcasted_iota(jnp.int32, tiled.shape, 1) // nbz == lax.broadcasted_iota(
-        jnp.int32, tiled.shape, 0
-    )
-    return jnp.sum(jnp.where(own, tiled, 0.0), axis=0, keepdims=True)
-
-
 def split_two(value):
     high = value.astype(jnp.bfloat16)
     low = (value - high.astype(jnp.float32)).astype(jnp.bfloat16)
     return high, low
 
 
+def split_rows(value):
+    high = value.astype(jnp.bfloat16).astype(jnp.float32)
+    return jnp.concatenate([high, value - high], axis=0).astype(jnp.bfloat16)
+
+
 def spread_kernel(plan, *refs):
-    hbm, (out_ref, bx_s, by_s, bz_s, row_ref) = refs[:6], refs[6:11]
-    local, (patch_s, turned_s, column_s, sems) = refs[11:17], refs[17:]
+    hbm, tables, (out_ref, outer_s, along_z_s) = refs[:6], refs[6:10], refs[10:13]
+    tables_out, local, (column_s, sems) = refs[13:17], refs[17:23], refs[23:]
     copies = [pltpu.make_async_copy(a, b, sems.at[n]) for n, (a, b) in enumerate(zip(hbm, local))]
+    for n, (table, target, axis) in enumerate(zip(tables, tables_out, ("gx", "gy", "gz", None))):
+        source = table if axis is None else table.at[lax.axis_index(axis)]
+        copies.append(pltpu.make_async_copy(source, target, sems.at[6 + n]))
     for copy in copies:
         copy.start()
-    x_ref, y_ref, z_ref, counts_ref, charge_ref, place_s = local
+    x_ref, y_ref, z_ref, charge_ref, counts_ref, place_s = local
     slots = charge_ref.shape[1]
-    for n, (ref, weight, points) in enumerate(((x_ref, bx_s, 8), (y_ref, by_s, 8), (z_ref, bz_s, 6))):
-        copies[n].wait()
-        along = ref[...].T
-        for i in range(points):
-            weight[i] = bspline(along + (2.0 - i))
-    copies[3].wait()
-    row = counts_row(counts_ref, plan.nbins)
-    row_ref[...] = jnp.broadcast_to(row, row_ref.shape)
-    slot = lax.broadcasted_iota(jnp.int32, (slots, LANES), 0).astype(jnp.float32)
-    copies[4].wait()
-    weighted = jnp.where(slot < row, charge_ref[...].T, 0.0)
-
-    def one_x(i, carry):
-        weight_x = bx_s[i] * weighted
-        rows = [[] for _ in range(6)]
-        for j in range(8):
-            product = weight_x * by_s[j]
-            for k in range(6):
-                rows[k].append(jnp.sum(product * bz_s[k], axis=0, keepdims=True))
-        for k in range(6):
-            patch_s[pl.ds(pl.multiple_of(k * 64 + i * 8, 8), 8), :] = jnp.concatenate(rows[k], axis=0)
+    nbx, nby, nbz = plan.nbins
+    zp = plan.zp
+    node = 2.0 - lax.broadcasted_iota(jnp.int32, (8, slots), 0).astype(jnp.float32)
+    slot = lax.broadcasted_iota(jnp.int32, (1, slots), 1)
+    rank = lax.broadcasted_iota(jnp.int32, (8, LANES), 0)
+    for copy in copies[:5]:
+        copy.wait()
+
+    def one_column(p):
+        sums = [jnp.zeros((8, LANES), jnp.float32) for _ in range(zp // 8)]
+        for c in range(nbz):
+            r = p * nbz + c
+            weight_x = bspline(x_ref[pl.ds(r, 1), :] + node)
+            weight_y = bspline(y_ref[pl.ds(r, 1), :] + node)
+            weight_z = bspline(z_ref[pl.ds(r, 1), :] + node)
+            outer = split_rows(
+                jnp.concatenate([weight_x[i : i + 1, :] * weight_y for i in range(8)], axis=0)
+            )
+            outer_s[r] = outer
+            along_z_s[r] = weight_z
+            weighted = jnp.where(slot < counts_ref[p // nby, p % nby, c], charge_ref[pl.ds(r, 1), :], 0.0)
+            both = lax.dot_general(
+                split_rows(weight_z * weighted), outer, (((1,), (1,)), ((), ())),
+                preferred_element_type=jnp.float32,
+            )
+            part = both[:8, :] + both[8:, :]
+            at, shift = divmod(2 * c, 8)
+            if shift:
+                part = pltpu.roll(part, shift, 0)
+                sums[at] = sums[at] + jnp.where(rank >= shift, part, 0.0)
+                sums[at + 1] = sums[at + 1] + jnp.where(rank < shift, part, 0.0)
+            else:
+                sums[at] = sums[at] + part
+        return [v + pltpu.roll(v, 64, 1) for v in sums]
+
+    left = lax.broadcasted_iota(jnp.int32, (8, LANES), 1) < 64
+
+    def one_group(g, carry):
+        for q in range(GROUP):
+            pair = g * GROUP + q
+            even = one_column(2 * pair)
+            odd = one_column(2 * pair + 1)
+            for n, (a, b) in enumerate(zip(even, odd)):
+                column_s[pl.ds(pl.multiple_of(pair * zp, 8) + 8 * n, 8), :] = jnp.where(left, a, b)
         return carry
 
-    lax.fori_loop(0, 8, one_x, 0)
-    for h in range(3):
-        turned_s[:, h * LANES : (h + 1) * LANES] = patch_s[h * LANES : (h + 1) * LANES, :].T
-    column_s[...] = jnp.zeros_like(column_s)
-    nbz = plan.nbins[2]
-    half = plan.zp // 2
-    lane = lax.broadcasted_iota(jnp.int32, (nbz, LANES), 1)
-    for pair in range(plan.columns // 2):
-        for s in range(3):
-            left = turned_s[2 * pair * nbz : (2 * pair + 1) * nbz, s * LANES : (s + 1) * LANES]
-            right = turned_s[(2 * pair + 1) * nbz : (2 * pair + 2) * nbz, s * LANES : (s + 1) * LANES]
-            even = jnp.where(lane < 64, left, pltpu.roll(right, 64, 1))
-            odd = jnp.where(lane < 64, pltpu.roll(left, 64, 1), right)
-            for c, piece in enumerate((even, odd)):
-                at = (pl.ds(pair * plan.zp + 2 * s + c, nbz, stride=2), slice(None))
-                column_s[at] = column_s[at] + piece
+    lax.fori_loop(0, plan.columns // 2 // GROUP, one_group, 0)
     columns = jnp.concatenate(
         [column_s[p * plan.zp : (p + 1) * plan.zp, :] for p in range(plan.columns // 2)], axis=1
     )
-    high, low = split_two(columns)
+    pad = jnp.zeros((LANES - 2 * zp, columns.shape[1]), jnp.bfloat16)
     copies[5].wait()
-    place = place_s[...]
-    contract = (((1,), (1,)), ((), ()))
-    grid = lax.dot_general(place, high, contract, preferred_element_type=jnp.float32) + lax.dot_general(
-        place, low, contract, preferred_element_type=jnp.float32
+    grid = lax.dot_general(
+        place_s[...], jnp.concatenate([split_rows(columns), pad], axis=0), (((1,), (1,)), ((), ())),
+        preferred_element_type=jnp.float32,
     )
-    grid = jnp.concatenate([grid, jnp.zeros((grid.shape[0], LANES - plan.zp), jnp.float32)], axis=1)
+    grid = grid + pltpu.roll(grid, LANES - zp, 1)
     xp = plan.xp
     group = lax.broadcasted_iota(jnp.int32, (xp, LANES), 1) // plan.zp
     for chunk in range(plan.chunks):
@@ -259,6 +262,8 @@
                 moved = pltpu.roll(piece, b * plan.zp, 1) if b else piece
                 merged = jnp.where(group == b, moved, merged)
         out_ref[:, chunk * LANES : (chunk + 1) * LANES] = merged
+    for copy in copies[6:]:
+        copy.wait()
 
 
 def solve_kernel(plan, *refs):
@@ -266,10 +271,9 @@
     blocks = refs[: nx * ny]
     tables = refs[nx * ny : nx * ny + 3]
     outs = refs[nx * ny + 3 : nx * ny + 3 + nz]
-    mid_s, term_s, ytab_s, sem = refs[nx * ny + 3 + nz :]
-    copy = pltpu.make_async_copy(tables[1].at[lax.axis_index("gy")], ytab_s, sem)
-    copy.start()
-    x_matrix = tables[0][lax.axis_index("gx")]
+    mid_s, term_s = refs[nx * ny + 3 + nz :]
+    ytab_s = tables[1]
+    x_matrix = tables[0][...]
     wy = plan.width[1]
     zp = plan.zp
     span = plan.chunks * TERMS
@@ -280,7 +284,6 @@
             preferred_element_type=jnp.float32,
         )
     slot = lax.broadcasted_iota(jnp.int32, (zp, LANES), 1) // SLOT
-    copy.wait()
     for chunk in range(plan.chunks):
         sums = [jnp.zeros((zp, LANES), jnp.float32) for _ in range(TERMS)]
         for oy in range(ny):
@@ -297,8 +300,7 @@
                 moved = pltpu.roll(sums[b], shift, 1) if shift else sums[b]
                 merged = jnp.where(slot == b, moved, merged)
             term_s[t * zp : (t + 1) * zp, chunk * LANES : (chunk + 1) * LANES] = merged
-    z_matrix = tables[2][lax.axis_index("gz")]
-    result = jnp.dot(z_matrix, term_s[...], precision=highest, preferred_element_type=jnp.float32)
+    result = jnp.dot(tables[2][...], term_s[...], precision=highest, preferred_element_type=jnp.float32)
     for o in range(nz):
         outs[o][...] = result[o * zp : (o + 1) * zp, :]
 
@@ -306,21 +308,26 @@
 def gather_kernel(plan, *refs):
     nz = plan.counts[2]
     parts = refs[:nz]
-    bx_s, by_s, bz_s, row_ref, pick_ref, fine_ref, atom_ref = refs[nz : nz + 7]
-    field_s, column_s, turned_s, patch_s = refs[nz + 7 :]
+    outer_s, along_z_s, counts_hbm, pick_ref, fine_ref, atom_ref = refs[nz : nz + 6]
+    field_s, column_s, counts_ref, sem = refs[nz + 6 :]
+    copy = pltpu.make_async_copy(counts_hbm, counts_ref, sem)
+    copy.start()
+    nbx, nby, nbz = plan.nbins
     zp = plan.zp
     lx, ly, lz = plan.local
     total = parts[0][...]
     for part in parts[1:]:
         total = total + part[...]
-    high, low = split_two(total)
-    pick = pick_ref[...]
-    contract = (((1,), (1,)), ((), ()))
-    columns = lax.dot_general(high, pick, contract, preferred_element_type=jnp.float32) + lax.dot_general(
-        low, pick, contract, preferred_element_type=jnp.float32
+    columns = lax.dot_general(
+        split_rows(total), pick_ref[...], (((1,), (1,)), ((), ())), preferred_element_type=jnp.float32
     )
+    columns = columns[:zp, :] + columns[zp:, :]
+    left = lax.broadcasted_iota(jnp.int32, (zp, LANES), 1) < 64
     for pair in range(plan.columns // 2):
-        column_s[pair * zp : (pair + 1) * zp, :] = columns[:, pair * LANES : (pair + 1) * LANES]
+        both = columns[:, pair * LANES : (pair + 1) * LANES]
+        turned = pltpu.roll(both, 64, 1)
+        column_s[2 * pair * zp : (2 * pair + 1) * zp, :] = jnp.where(left, both, turned)
+        column_s[(2 * pair + 1) * zp : (2 * pair + 2) * zp, :] = jnp.where(left, turned, both)
     for chunk in range(plan.chunks):
         turned = total[:, chunk * LANES : (chunk + 1) * LANES].T
         field_s[chunk * LANES : (chunk + 1) * LANES, :zp] = turned
@@ -328,36 +335,26 @@
         chunk, b = divmod(y + 2, TERMS)
         at = chunk * LANES + b * SLOT + 2
         fine_ref[:, y, :] = field_s[at : at + lx, 2 : 2 + lz]
-    nbz = plan.nbins[2]
-    lane = lax.broadcasted_iota(jnp.int32, (nbz, LANES), 1)
-    for pair in range(plan.columns // 2):
-        for s in range(3):
-            even = column_s[pl.ds(pair * zp + 2 * s, nbz, stride=2), :]
-            odd = column_s[pl.ds(pair * zp + 2 * s + 1, nbz, stride=2), :]
-            turned_s[2 * pair * nbz : (2 * pair + 1) * nbz, s * LANES : (s + 1) * LANES] = jnp.where(
-                lane < 64, even, pltpu.roll(odd, 64, 1)
-            )
-            turned_s[(2 * pair + 1) * nbz : (2 * pair + 2) * nbz, s * LANES : (s + 1) * LANES] = jnp.where(
-                lane < 64, pltpu.roll(even, 64, 1), odd
-            )
-    for h in range(3):
-        patch_s[h * LANES : (h + 1) * LANES, :] = turned_s[:, h * LANES : (h + 1) * LANES].T
     slots = atom_ref.shape[1]
-
-    def one_x(i, result):
-        inner = jnp.zeros((slots, LANES), jnp.float32)
-        rows = [patch_s[pl.ds(pl.multiple_of(k * 64 + i * 8, 8), 8), :] for k in range(6)]
-        for j in range(8):
-            along_z = rows[0][j : j + 1, :] * bz_s[0]
-            for k in range(1, 6):
-                along_z = along_z + rows[k][j : j + 1, :] * bz_s[k]
-            inner = inner + along_z * by_s[j]
-        return result + inner * bx_s[i]
-
-    result = lax.fori_loop(0, 8, one_x, jnp.zeros((slots, LANES), jnp.float32))
-    row = row_ref[0:1, :]
-    slot = lax.broadcasted_iota(jnp.int32, (slots, LANES), 0).astype(jnp.float32)
-    atom_ref[...] = jnp.where(slot < row, result, 0.0).T
+    slot = lax.broadcasted_iota(jnp.int32, (1, slots), 1)
+    copy.wait()
+
+    def one_column(p):
+        rows = []
+        for c in range(nbz):
+            r = p * nbz + c
+            patch = column_s[pl.ds(p * zp + 2 * c, 8), :]
+            both = jnp.dot(split_rows(patch), outer_s[r], preferred_element_type=jnp.float32)
+            value = jnp.sum((both[:8, :] + both[8:, :]) * along_z_s[r], axis=0, keepdims=True)
+            rows.append(jnp.where(slot < counts_ref[p // nby, p % nby, c], value, 0.0))
+        atom_ref[pl.ds(pl.multiple_of(p * nbz, 8), nbz), :] = jnp.concatenate(rows, axis=0)
+
+    def one_group(g, carry):
+        for q in range(2 * GROUP):
+            one_column(g * 2 * GROUP + q)
+        return carry
+
+    lax.fori_loop(0, plan.columns // 2 // GROUP, one_group, 0)
 
 
 def body(charges, offset_x, offset_y, offset_z, counts):
@@ -368,37 +365,37 @@
     plan = Plan(nbins, sizes)
     flat = [v.reshape(LANES, slots) for v in (charges, offset_x, offset_y, offset_z)]
     vmem = pl.BlockSpec(memory_space=pltpu.VMEM)
-    hbm = pl.BlockSpec(memory_space=pl.ANY)
+    hbm = pl.BlockSpec(memory_space=pltpu.HBM)
     f32 = jnp.float32
-    params = pltpu.CompilerParams(vmem_limit_bytes=40 << 20)
+    params = pltpu.CompilerParams(vmem_limit_bytes=12 << 20)
     place, pick = plan.place_matrix(), plan.pick_matrix()
 
+    def far(value):
+        return pltpu.with_memory_space_constraint(value, pltpu.HBM)
+
+    tables = (plan.x_table(), plan.y_table(), plan.z_table(), pick)
     spread, *weights = pl.pallas_call(
         functools.partial(spread_kernel, plan),
         out_shape=[
             pltpu.VMEM((plan.xp, plan.lanes), f32),
-            pltpu.VMEM((8, slots, LANES), f32),
-            pltpu.VMEM((8, slots, LANES), f32),
-            pltpu.VMEM((6, slots, LANES), f32),
-            pltpu.VMEM((8, LANES), f32),
-        ],
-        in_specs=[pl.BlockSpec(memory_space=pltpu.HBM)] * 6,
-        out_specs=[vmem] * 5,
-        scratch_shapes=[
-            pltpu.VMEM((LANES, slots), f32),
-            pltpu.VMEM((LANES, slots), f32),
-            pltpu.VMEM((LANES, slots), f32),
-            pltpu.VMEM(nbins, jnp.int32),
-            pltpu.VMEM((LANES, slots), f32),
+            pltpu.VMEM((LANES, LANES, slots), jnp.bfloat16),
+            pltpu.VMEM((LANES, 8, slots), f32),
+        ]
+        + [pltpu.VMEM(t.shape[1:], t.dtype) for t in tables[:3]]
+        + [pltpu.VMEM(pick.shape, pick.dtype)],
+        in_specs=[hbm] * 10,
+        out_specs=[vmem] * 7,
+        scratch_shapes=[pltpu.VMEM((LANES, slots), f32)] * 4
+        + [
+            pltpu.SMEM(nbins, jnp.int32),
             pltpu.VMEM(place.shape, place.dtype),
-            pltpu.VMEM((384, LANES), f32),
-            pltpu.VMEM((LANES, 384), f32),
             pltpu.VMEM((plan.columns // 2 * plan.zp, LANES), f32),
-            pltpu.SemaphoreType.DMA((6,)),
+            pltpu.SemaphoreType.DMA((10,)),
         ],
         compiler_params=params,
         name="spread",
-    )(*(pltpu.with_memory_space_constraint(v, pltpu.HBM) for v in (*flat[1:], counts, flat[0], place)))
+    )(*(far(v) for v in (*flat[1:], flat[0], counts, place, *tables)))
+    weights, tables, pick = weights[:2], weights[2:5], weights[5]
 
     def near(value):
         return pltpu.with_memory_space_constraint(value, pltpu.VMEM)
@@ -423,17 +420,14 @@
         blocks += own
         if pair == 2:
             blocks += [moved(v, "gx", [(s, s ^ 1) for s in range(nx)]) for v in own]
-    tables = (plan.x_table(), plan.y_table(), plan.z_table())
     outs = pl.pallas_call(
         functools.partial(solve_kernel, plan),
         out_shape=[pltpu.VMEM((plan.zp, plan.lanes), f32)] * nz,
-        in_specs=[vmem] * (nx * ny) + [vmem, hbm, vmem],
+        in_specs=[vmem] * (nx * ny + 3),
         out_specs=[vmem] * nz,
         scratch_shapes=[
             pltpu.VMEM((plan.mid, LANES), f32),
             pltpu.VMEM((TERMS * plan.zp, plan.lanes), f32),
-            pltpu.VMEM(tables[1].shape[1:], f32),
-            pltpu.SemaphoreType.DMA(()),
         ],
         compiler_params=params,
         name="solve",
@@ -447,17 +441,17 @@
             jax.ShapeDtypeStruct(plan.local, f32),
             jax.ShapeDtypeStruct((LANES, slots), f32),
         ],
-        in_specs=[vmem] * (nz + 5),
+        in_specs=[vmem] * (nz + 2) + [hbm, vmem],
         out_specs=[vmem, vmem],
         scratch_shapes=[
             pltpu.VMEM((plan.lanes, LANES), f32),
-            pltpu.VMEM((plan.columns // 2 * plan.zp, LANES), f32),
-            pltpu.VMEM((LANES, 384), f32),
-            pltpu.VMEM((384, LANES), f32),
+            pltpu.VMEM((plan.columns * plan.zp, LANES), f32),
+            pltpu.SMEM(nbins, jnp.int32),
+            pltpu.SemaphoreType.DMA(()),
         ],
         compiler_params=params,
         name="gather",
-    )(*parts, *weights, pick)
+    )(*parts, *weights, far(counts), pick)
     return fine, atom.reshape(charges.shape)
 
 

time: 30.4 us -> 28.7 us (0.944)
  Pallas kernels: 11.2 us -> 9.57 us
    pallas_call x1, Pallas kernels: 5.23 us -> 4.56 us  [body(): pl.pallas_call(functools.partial(spread_kernel, plan), out_shape=[pltpu.V...]
    pallas_call x1, Pallas kernels: 2.31 us -> 1.69 us  [body(): pl.pallas_call(functools.partial(solve_kernel, plan), out_shape=[pltpu.VM...]
    pallas_call x1, Pallas kernels: 3.7 us -> 3.32 us  [body(): pl.pallas_call(functools.partial(gather_kernel, plan), out_shape=[jax.Sha...]
where the time goes in v3:
time: 28.7 us; the launch traced here: 28.5 us
  starting transfers between devices  10.2 us (36%)
  Pallas kernels  9.57 us (33%)
  waiting for transfers between devices  8.08 us (28%)
  between operations  0.66 us (2%)
    ppermute x10, starting transfers between devices, moved(): return near(lax.ppermute(value, axis, pairs))  10.2 us
    ppermute x10, waiting for transfers between devices, moved(): return near(lax.ppermute(value, axis, pairs))  8.08 us
    pallas_call x1, Pallas kernels, body(): pl.pallas_call(functools.partial(spread_kernel, plan), out_shape=[pltpu.V...  4.56 us
    pallas_call x1, Pallas kernels, body(): pl.pallas_call(functools.partial(gather_kernel, plan), out_shape=[jax.Sha...  3.32 us
    pallas_call x1, Pallas kernels, body(): pl.pallas_call(functools.partial(solve_kernel, plan), out_shape=[pltpu.VM...  1.69 us
  transfers between devices with their start and end apart: 10, of which 8 were waited for; matrix products, arithmetic and copies ran while one was open for 0% of the time, Pallas kernels for 0%

profile of v3, /device:TPU:0, one launch (start us, length us, event | category | flops | bytes accessed | tf_op | source)
XLA Modules:
  0.0 28.5 jit_solution(17514602432982719676)
XLA Ops:
  0.6 4.6 %spread.1 = (f32[24,512]{1,0:T(8,128)S(1)}, bf16[128,128,128]{2,1,0:T(8,128)(2,1)S(1)}, f32[128,8,128]{2,1,0:T(8,128)S(1)}, f32[96,128]{1,0:T(8,128)S(1)}, f32[8...) custom-call(f32[128,128]{1,0:T(8,128)} %bitcast.5, f32[128,128]{1,0:T(8,128)} %bitcast.6, ...), custom_call_target="tpu_custom_call" | custom-call | tf_op jit(solution)/shard_map/spread/pallas_call | solution.py:377
  5.2 4.0 %collective-permute-start.4 = (f32[24,512]{1,0:T(8,128)S(1)}, f32[24,512]{1,0:T(8,128)S(1)}, u32[]{:S(2)}, u32[]{:S(2)}) collective-permute-start(f32[24,512]{1,0:T(8,128)S(1)} %get-tuple-element.15.refs_0_), channel_id=1, source_target_pairs={{0,20},{4,16},{8,28},{12,24},{16,4},{20,0},{24,12},{28,8},{1,21},{... | collective-permute-start | bytes 147464 | tf_op jit(solution)/shard_map/ppermute | solution.py:404
  9.2 0.5 %collective-permute-start.3 = (f32[24,512]{1,0:T(8,128)S(1)}, f32[24,512]{1,0:T(8,128)S(1)}, u32[]{:S(2)}, u32[]{:S(2)}) collective-permute-start(f32[24,512]{1,0:T(8,128)S(1)} %get-tuple-element.15.refs_0_), channel_id=1, source_target_pairs={{0,16},{4,20},{8,24},{12,28},{16,0},{20,4},{24,8},{28,12},{1,17},{... | collective-permute-start | bytes 147464 | tf_op jit(solution)/shard_map/ppermute | solution.py:404
  9.7 0.1 collective-permute-start
  9.8 0.0 collective-permute-start.1
  9.8 1.4 %collective-permute-done.4.refs_5_ = f32[24,512]{1,0:T(8,128)S(1)} collective-permute-done((f32[24,512]{1,0:T(8,128)S(1)}, f32[24,512]{1,0:T(8,128)S(1)}, u32[]{:S(2)}, u32[]{:S(2)}) %collective-permute-start.4) | collective-permute-done | bytes 49184 | tf_op jit(solution)/shard_map/ppermute | solution.py:404
  11.3 0.0 collective-permute-start.6
  11.3 2.0 %collective-permute-done.3.refs_4_ = f32[24,512]{1,0:T(8,128)S(1)} collective-permute-done((f32[24,512]{1,0:T(8,128)S(1)}, f32[24,512]{1,0:T(8,128)S(1)}, u32[]{:S(2)}, u32[]{:S(2)}) %collective-permute-start.3) | collective-permute-done | bytes 49184 | tf_op jit(solution)/shard_map/ppermute | solution.py:404
  13.3 0.0 collective-permute-start.5
  13.3 0.5 %collective-permute-done.refs_1_ = f32[24,512]{1,0:T(8,128)S(1)} collective-permute-done((f32[24,512]{1,0:T(8,128)S(1)}, f32[24,512]{1,0:T(8,128)S(1)}, u32[]{:S(2)}, u32[]{:S(2)}) %collective-permute-start) | collective-permute-done | bytes 49184 | tf_op jit(solution)/shard_map/ppermute | solution.py:404
  13.8 0.0 collective-permute-start.2
  13.8 0.0 collective-permute-done.1.refs_2_
  13.8 0.0 collective-permute-done.6.refs_7_
  13.8 0.7 %collective-permute-done.5.refs_6_ = f32[24,512]{1,0:T(8,128)S(1)} collective-permute-done((f32[24,512]{1,0:T(8,128)S(1)}, f32[24,512]{1,0:T(8,128)S(1)}, u32[]{:S(2)}, u32[]{:S(2)}) %collective-permute-start.5) | collective-permute-done | bytes 49184 | tf_op jit(solution)/shard_map/ppermute | solution.py:404
  14.5 0.5 %collective-permute-done.2.refs_3_ = f32[24,512]{1,0:T(8,128)S(1)} collective-permute-done((f32[24,512]{1,0:T(8,128)S(1)}, f32[24,512]{1,0:T(8,128)S(1)}, u32[]{:S(2)}, u32[]{:S(2)}) %collective-permute-start.2) | collective-permute-done | bytes 49184 | tf_op jit(solution)/shard_map/ppermute | solution.py:404
  15.0 1.7 %solve.1 = (f32[24,512]{1,0:T(8,128)S(1)}, f32[24,512]{1,0:T(8,128)S(1)}, f32[24,512]{1,0:T(8,128)S(1)}, f32[24,512]{1,0:T(8,128)S(1)}) custom-call(f32[24,512]{1,0:T(8,128)S(1)} %get-tuple-element.15.refs_0_, f32[24,512]{1,0:T(8,128)S(1)} %collective-permute-done.refs_1_, f32[24,512]{1,0:T(8,128)S(1)} %collective-permute-done.1.refs_2_, ...), custom_call_target="tpu_custom_call" | custom-call | tf_op jit(solution)/shard_map/solve/pallas_call | solution.py:423
  16.7 1.6 %collective-permute-start.7 = (f32[24,512]{1,0:T(8,128)S(1)}, f32[24,512]{1,0:T(8,128)S(1)}, u32[]{:S(2)}, u32[]{:S(2)}) collective-permute-start(f32[24,512]{1,0:T(8,128)S(1)} %get-tuple-element.20), channel_id=1, source_target_pairs={{0,1},{1,2},{2,3},{3,0},{4,5},{5,6},{6,7},{7,4},{8,9},{9,10},{10,1... | collective-permute-start | bytes 147464 | tf_op jit(solution)/shard_map/ppermute | solution.py:404
  18.3 2.6 %collective-permute-start.8 = (f32[24,512]{1,0:T(8,128)S(1)}, f32[24,512]{1,0:T(8,128)S(1)}, u32[]{:S(2)}, u32[]{:S(2)}) collective-permute-start(f32[24,512]{1,0:T(8,128)S(1)} %get-tuple-element.21), channel_id=1, source_target_pairs={{0,2},{1,3},{2,0},{3,1},{4,6},{5,7},{6,4},{7,5},{8,10},{9,11},{10,... | collective-permute-start | bytes 147464 | tf_op jit(solution)/shard_map/ppermute | solution.py:404
  20.9 1.3 %collective-permute-start.9 = (f32[24,512]{1,0:T(8,128)S(1)}, f32[24,512]{1,0:T(8,128)S(1)}, u32[]{:S(2)}, u32[]{:S(2)}) collective-permute-start(f32[24,512]{1,0:T(8,128)S(1)} %get-tuple-element.22), channel_id=1, source_target_pairs={{0,3},{1,0},{2,1},{3,2},{4,7},{5,4},{6,5},{7,6},{8,11},{9,8},{10,9... | collective-permute-start | bytes 147464 | tf_op jit(solution)/shard_map/ppermute | solution.py:404
  22.3 0.4 %collective-permute-done.7.refs_1_ = f32[24,512]{1,0:T(8,128)S(1)} collective-permute-done((f32[24,512]{1,0:T(8,128)S(1)}, f32[24,512]{1,0:T(8,128)S(1)}, u32[]{:S(2)}, u32[]{:S(2)}) %collective-permute-start.7) | collective-permute-done | bytes 49184 | tf_op jit(solution)/shard_map/ppermute | solution.py:404
  22.7 2.2 %collective-permute-done.8.refs_2_ = f32[24,512]{1,0:T(8,128)S(1)} collective-permute-done((f32[24,512]{1,0:T(8,128)S(1)}, f32[24,512]{1,0:T(8,128)S(1)}, u32[]{:S(2)}, u32[]{:S(2)}) %collective-permute-start.8) | collective-permute-done | bytes 49184 | tf_op jit(solution)/shard_map/ppermute | solution.py:404
  24.8 0.4 %collective-permute-done.9.refs_3_ = f32[24,512]{1,0:T(8,128)S(1)} collective-permute-done((f32[24,512]{1,0:T(8,128)S(1)}, f32[24,512]{1,0:T(8,128)S(1)}, u32[]{:S(2)}, u32[]{:S(2)}) %collective-permute-start.9) | collective-permute-done | bytes 49184 | tf_op jit(solution)/shard_map/ppermute | solution.py:404
  25.2 3.3 %gather.1 = (f32[16,16,16]{2,1,0:T(8,128)}, f32[128,128]{1,0:T(8,128)}) custom-call(f32[24,512]{1,0:T(8,128)S(1)} %get-tuple-element.19.refs_0_, f32[24,512]{1,0:T(8,128)S(1)} %collective-permute-done.7.refs_1_, f32[24,512]{1,0:T(8,128)S(1)} %collective-permute-done.8.refs_2_, f32[24,512]{1,0:T(8,128)S(1)} %collective-permute-done.9.refs_3_, ...), custom_call_target="tpu_custom_call" | custom-call | tf_op jit(solution)/shard_map/gather/pallas_call | solution.py:438
Async XLA Ops:
  5.2 6.1 %collective-permute-start.4 = (f32[24,512]{1,0:T(8,128)S(1)}, f32[24,512]{1,0:T(8,128)S(1)}, u32[]{:S(2)}, u32[]{:S(2)}) collective-permute-start(f32[24,512]{1,0:T(8,128)S(1)} %get-tuple-element.15.refs_0_), channel_id=1, source_target_pairs={{0,20},{4,16},{8,28},{12,24},{16,4},{20,0},{24,12},{28,8},{1,21},{... | collective-permute-start | bytes 147464 | tf_op jit(solution)/shard_map/ppermute | solution.py:404
  9.2 4.1 %collective-permute-start.3 = (f32[24,512]{1,0:T(8,128)S(1)}, f32[24,512]{1,0:T(8,128)S(1)}, u32[]{:S(2)}, u32[]{:S(2)}) collective-permute-start(f32[24,512]{1,0:T(8,128)S(1)} %get-tuple-element.15.refs_0_), channel_id=1, source_target_pairs={{0,16},{4,20},{8,24},{12,28},{16,0},{20,4},{24,8},{28,12},{1,17},{... | collective-permute-start | bytes 147464 | tf_op jit(solution)/shard_map/ppermute | solution.py:404
  9.7 4.1 %collective-permute-start = (f32[24,512]{1,0:T(8,128)S(1)}, f32[24,512]{1,0:T(8,128)S(1)}, u32[]{:S(2)}, u32[]{:S(2)}) collective-permute-start(f32[24,512]{1,0:T(8,128)S(1)} %get-tuple-element.15.refs_0_), channel_id=1, source_target_pairs={{0,4},{4,0},{8,12},{12,8},{16,20},{20,16},{24,28},{28,24},{1,5},{5... | collective-permute-start | bytes 147464 | tf_op jit(solution)/shard_map/ppermute | solution.py:404
  9.8 4.0 %collective-permute-start.1 = (f32[24,512]{1,0:T(8,128)S(1)}, f32[24,512]{1,0:T(8,128)S(1)}, u32[]{:S(2)}, u32[]{:S(2)}) collective-permute-start(f32[24,512]{1,0:T(8,128)S(1)} %get-tuple-element.15.refs_0_), channel_id=1, source_target_pairs={{0,8},{8,0},{16,24},{24,16},{1,9},{9,1},{17,25},{25,17},{2,10},{10... | collective-permute-start | bytes 147464 | tf_op jit(solution)/shard_map/ppermute | solution.py:404
  11.3 2.5 %collective-permute-start.6 = (f32[24,512]{1,0:T(8,128)S(1)}, f32[24,512]{1,0:T(8,128)S(1)}, u32[]{:S(2)}, u32[]{:S(2)}) collective-permute-start(f32[24,512]{1,0:T(8,128)S(1)} %collective-permute-done.4.refs_5_), channel_id=1, source_target_pairs={{0,8},{8,0},{16,24},{24,16},{1,9},{9,1},{17,25},{25,17},{2,10},{10... | collective-permute-start | bytes 147464 | tf_op jit(solution)/shard_map/ppermute | solution.py:404
  13.3 1.2 %collective-permute-start.5 = (f32[24,512]{1,0:T(8,128)S(1)}, f32[24,512]{1,0:T(8,128)S(1)}, u32[]{:S(2)}, u32[]{:S(2)}) collective-permute-start(f32[24,512]{1,0:T(8,128)S(1)} %collective-permute-done.3.refs_4_), channel_id=1, source_target_pairs={{0,8},{8,0},{16,24},{24,16},{1,9},{9,1},{17,25},{25,17},{2,10},{10... | collective-permute-start | bytes 147464 | tf_op jit(solution)/shard_map/ppermute | solution.py:404
  13.8 1.2 %collective-permute-start.2 = (f32[24,512]{1,0:T(8,128)S(1)}, f32[24,512]{1,0:T(8,128)S(1)}, u32[]{:S(2)}, u32[]{:S(2)}) collective-permute-start(f32[24,512]{1,0:T(8,128)S(1)} %collective-permute-done.refs_1_), channel_id=1, source_target_pairs={{0,8},{8,0},{16,24},{24,16},{1,9},{9,1},{17,25},{25,17},{2,10},{10... | collective-permute-start | bytes 147464 | tf_op jit(solution)/shard_map/ppermute | solution.py:404
  16.7 5.9 %collective-permute-start.7 = (f32[24,512]{1,0:T(8,128)S(1)}, f32[24,512]{1,0:T(8,128)S(1)}, u32[]{:S(2)}, u32[]{:S(2)}) collective-permute-start(f32[24,512]{1,0:T(8,128)S(1)} %get-tuple-element.20), channel_id=1, source_target_pairs={{0,1},{1,2},{2,3},{3,0},{4,5},{5,6},{6,7},{7,4},{8,9},{9,10},{10,1... | collective-permute-start | bytes 147464 | tf_op jit(solution)/shard_map/ppermute | solution.py:404
  18.3 6.5 %collective-permute-start.8 = (f32[24,512]{1,0:T(8,128)S(1)}, f32[24,512]{1,0:T(8,128)S(1)}, u32[]{:S(2)}, u32[]{:S(2)}) collective-permute-start(f32[24,512]{1,0:T(8,128)S(1)} %get-tuple-element.21), channel_id=1, source_target_pairs={{0,2},{1,3},{2,0},{3,1},{4,6},{5,7},{6,4},{7,5},{8,10},{9,11},{10,... | collective-permute-start | bytes 147464 | tf_op jit(solution)/shard_map/ppermute | solution.py:404
  20.9 4.3 %collective-permute-start.9 = (f32[24,512]{1,0:T(8,128)S(1)}, f32[24,512]{1,0:T(8,128)S(1)}, u32[]{:S(2)}, u32[]{:S(2)}) collective-permute-start(f32[24,512]{1,0:T(8,128)S(1)} %get-tuple-element.22), channel_id=1, source_target_pairs={{0,3},{1,0},{2,1},{3,2},{4,7},{5,4},{6,5},{7,6},{8,11},{9,8},{10,9... | collective-permute-start | bytes 147464 | tf_op jit(solution)/shard_map/ppermute | solution.py:404

commit v4 on v3

--- a/solution.py
+++ b/solution.py
@@ -13,7 +13,8 @@
 LANES = 128
 TERMS = 5
 SLOT = LANES // TERMS
-GROUP = 2
+PARTS = 4
+GROUP = 8
 RIM = 4
 TAPS = (-0.0625, 0.0, 0.5625, 1.0, 0.5625, 0.0, -0.0625)
 highest = lax.Precision.HIGHEST
@@ -82,6 +83,10 @@
 
 def round_up(value, step):
     return -(-value // step) * step
+
+
+def partner(device, order, count):
+    return (device + order) % count
 
 
 class Plan:
@@ -160,22 +165,19 @@
             for o in range(nz):
                 for t in range(TERMS):
                     table[d, o * self.zp : o * self.zp + width, t * self.zp : t * self.zp + width] = (
-                        scales[t] * m[t, (d + o) % nz, :, d, :]
+                        scales[t] * m[t, partner(d, o, nz), :, d, :]
                     )
         return jnp.asarray(table)
 
 
-def bspline(spacing):
-    a = jnp.abs(spacing)
-    u = jnp.maximum(2.0 - a, 0.0)
-    v = jnp.maximum(1.0 - a, 0.0)
-    return u * u * u * (1.0 / 6.0) - v * v * v * (2.0 / 3.0)
-
-
-def split_two(value):
-    high = value.astype(jnp.bfloat16)
-    low = (value - high.astype(jnp.float32)).astype(jnp.bfloat16)
-    return high, low
+SCALE = (1.0 / 6.0) ** (1.0 / 3.0)
+
+
+def bspline(scaled):
+    a = jnp.abs(scaled)
+    u = jnp.maximum(2.0 * SCALE - a, 0.0)
+    v = jnp.maximum(SCALE - a, 0.0)
+    return u * u * u - v * v * (4.0 * v)
 
 
 def split_rows(value):
@@ -196,37 +198,47 @@
     slots = charge_ref.shape[1]
     nbx, nby, nbz = plan.nbins
     zp = plan.zp
-    node = 2.0 - lax.broadcasted_iota(jnp.int32, (8, slots), 0).astype(jnp.float32)
-    slot = lax.broadcasted_iota(jnp.int32, (1, slots), 1)
+    node = (2.0 - lax.broadcasted_iota(jnp.int32, (8, slots), 0).astype(jnp.float32)) * SCALE
+    slot = lax.broadcasted_iota(jnp.int32, (8, slots), 1)
     rank = lax.broadcasted_iota(jnp.int32, (8, LANES), 0)
     for copy in copies[:5]:
         copy.wait()
+    for ref in (x_ref, y_ref, z_ref):
+        ref[...] = ref[...] * SCALE
+
+    def one_bin(p, c):
+        r = p * nbz + c
+        weight_x = bspline(x_ref[pl.ds(r, 1), :] + node)
+        weight_y = bspline(y_ref[pl.ds(r, 1), :] + node)
+        weight_z = bspline(z_ref[pl.ds(r, 1), :] + node)
+        weight_z = jnp.where(slot < counts_ref[p // nby, p % nby, c], weight_z, 0.0)
+        outer = split_rows(jnp.concatenate([weight_x[i : i + 1, :] * weight_y for i in range(8)], axis=0))
+        outer_s[r // 2, :, (c % 2) * slots : (c % 2 + 1) * slots] = outer
+        along_z_s[r] = weight_z
+        return outer, split_rows(weight_z * charge_ref[pl.ds(r, 1), :])
 
     def one_column(p):
         sums = [jnp.zeros((8, LANES), jnp.float32) for _ in range(zp // 8)]
-        for c in range(nbz):
-            r = p * nbz + c
-            weight_x = bspline(x_ref[pl.ds(r, 1), :] + node)
-            weight_y = bspline(y_ref[pl.ds(r, 1), :] + node)
-            weight_z = bspline(z_ref[pl.ds(r, 1), :] + node)
-            outer = split_rows(
-                jnp.concatenate([weight_x[i : i + 1, :] * weight_y for i in range(8)], axis=0)
-            )
-            outer_s[r] = outer
-            along_z_s[r] = weight_z
-            weighted = jnp.where(slot < counts_ref[p // nby, p % nby, c], charge_ref[pl.ds(r, 1), :], 0.0)
+        for c in range(0, nbz, 2):
+            (outer_a, z_a), (outer_b, z_b) = one_bin(p, c), one_bin(p, c + 1)
+            none = jnp.zeros_like(z_a)
             both = lax.dot_general(
-                split_rows(weight_z * weighted), outer, (((1,), (1,)), ((), ())),
+                jnp.concatenate(
+                    [jnp.concatenate([z_a, none], axis=1), jnp.concatenate([none, z_b], axis=1)], axis=0
+                ),
+                jnp.concatenate([outer_a, outer_b], axis=1),
+                (((1,), (1,)), ((), ())),
                 preferred_element_type=jnp.float32,
             )
-            part = both[:8, :] + both[8:, :]
-            at, shift = divmod(2 * c, 8)
-            if shift:
-                part = pltpu.roll(part, shift, 0)
-                sums[at] = sums[at] + jnp.where(rank >= shift, part, 0.0)
-                sums[at + 1] = sums[at + 1] + jnp.where(rank < shift, part, 0.0)
-            else:
-                sums[at] = sums[at] + part
+            for n in range(2):
+                part = both[16 * n : 16 * n + 8, :] + both[16 * n + 8 : 16 * n + 16, :]
+                at, shift = divmod(2 * (c + n), 8)
+                if shift:
+                    part = pltpu.roll(part, shift, 0)
+                    sums[at] = sums[at] + jnp.where(rank >= shift, part, 0.0)
+                    sums[at + 1] = sums[at + 1] + jnp.where(rank < shift, part, 0.0)
+                else:
+                    sums[at] = sums[at] + part
         return [v + pltpu.roll(v, 64, 1) for v in sums]
 
     left = lax.broadcasted_iota(jnp.int32, (8, LANES), 1) < 64
@@ -308,10 +320,8 @@
 def gather_kernel(plan, *refs):
     nz = plan.counts[2]
     parts = refs[:nz]
-    outer_s, along_z_s, counts_hbm, pick_ref, fine_ref, atom_ref = refs[nz : nz + 6]
-    field_s, column_s, counts_ref, sem = refs[nz + 6 :]
-    copy = pltpu.make_async_copy(counts_hbm, counts_ref, sem)
-    copy.start()
+    outer_s, along_z_s, pick_ref, fine_hbm, atom_hbm = refs[nz : nz + 5]
+    field_s, column_s, fine_ref, atom_ref, sems = refs[nz + 5 :]
     nbx, nby, nbz = plan.nbins
     zp = plan.zp
     lx, ly, lz = plan.local
@@ -335,26 +345,35 @@
         chunk, b = divmod(y + 2, TERMS)
         at = chunk * LANES + b * SLOT + 2
         fine_ref[:, y, :] = field_s[at : at + lx, 2 : 2 + lz]
+    copies = [pltpu.make_async_copy(fine_ref, fine_hbm, sems.at[0])]
+    copies[0].start()
     slots = atom_ref.shape[1]
-    slot = lax.broadcasted_iota(jnp.int32, (1, slots), 1)
-    copy.wait()
 
     def one_column(p):
         rows = []
-        for c in range(nbz):
-            r = p * nbz + c
-            patch = column_s[pl.ds(p * zp + 2 * c, 8), :]
-            both = jnp.dot(split_rows(patch), outer_s[r], preferred_element_type=jnp.float32)
-            value = jnp.sum((both[:8, :] + both[8:, :]) * along_z_s[r], axis=0, keepdims=True)
-            rows.append(jnp.where(slot < counts_ref[p // nby, p % nby, c], value, 0.0))
-        atom_ref[pl.ds(pl.multiple_of(p * nbz, 8), nbz), :] = jnp.concatenate(rows, axis=0)
-
-    def one_group(g, carry):
-        for q in range(2 * GROUP):
-            one_column(g * 2 * GROUP + q)
-        return carry
-
-    lax.fori_loop(0, plan.columns // 2 // GROUP, one_group, 0)
+        for c in range(0, nbz, 2):
+            patches = [
+                split_rows(column_s[p * zp + 2 * n : p * zp + 2 * n + 8, :]) for n in (c, c + 1)
+            ]
+            both = jnp.dot(
+                jnp.concatenate(patches, axis=0), outer_s[(p * nbz + c) // 2],
+                preferred_element_type=jnp.float32,
+            )
+            for n in range(2):
+                field = both[16 * n : 16 * n + 8, n * slots : (n + 1) * slots]
+                field = field + both[16 * n + 8 : 16 * n + 16, n * slots : (n + 1) * slots]
+                rows.append(jnp.sum(field * along_z_s[p * nbz + c + n], axis=0, keepdims=True))
+        atom_ref[p * nbz : (p + 1) * nbz, :] = jnp.concatenate(rows, axis=0)
+
+    for part in range(PARTS):
+        span = LANES // PARTS
+        for p in range(part * span // nbz, (part + 1) * span // nbz):
+            one_column(p)
+        rows = pl.ds(part * span, span)
+        copies.append(pltpu.make_async_copy(atom_ref.at[rows], atom_hbm.at[rows], sems.at[1 + part]))
+        copies[-1].start()
+    for copy in copies:
+        copy.wait()
 
 
 def body(charges, offset_x, offset_y, offset_z, counts):
@@ -378,7 +397,7 @@
         functools.partial(spread_kernel, plan),
         out_shape=[
             pltpu.VMEM((plan.xp, plan.lanes), f32),
-            pltpu.VMEM((LANES, LANES, slots), jnp.bfloat16),
+            pltpu.VMEM((LANES // 2, LANES, 2 * slots), jnp.bfloat16),
             pltpu.VMEM((LANES, 8, slots), f32),
         ]
         + [pltpu.VMEM(t.shape[1:], t.dtype) for t in tables[:3]]
@@ -433,7 +452,7 @@
         name="solve",
     )(*blocks, *tables)
     parts = [outs[0]] + [
-        moved(outs[o], "gz", [(s, (s + o) % nz) for s in range(nz)]) for o in range(1, nz)
+        moved(outs[o], "gz", [(s, partner(s, o, nz)) for s in range(nz)]) for o in range(1, nz)
     ]
     fine, atom = pl.pallas_call(
         functools.partial(gather_kernel, plan),
@@ -441,17 +460,18 @@
             jax.ShapeDtypeStruct(plan.local, f32),
             jax.ShapeDtypeStruct((LANES, slots), f32),
         ],
-        in_specs=[vmem] * (nz + 2) + [hbm, vmem],
-        out_specs=[vmem, vmem],
+        in_specs=[vmem] * (nz + 3),
+        out_specs=[hbm, hbm],
         scratch_shapes=[
             pltpu.VMEM((plan.lanes, LANES), f32),
             pltpu.VMEM((plan.columns * plan.zp, LANES), f32),
-            pltpu.SMEM(nbins, jnp.int32),
-            pltpu.SemaphoreType.DMA(()),
+            pltpu.VMEM(plan.local, f32),
+            pltpu.VMEM((LANES, slots), f32),
+            pltpu.SemaphoreType.DMA((1 + PARTS,)),
         ],
         compiler_params=params,
         name="gather",
-    )(*parts, *weights, far(counts), pick)
+    )(*parts, *weights, pick)
     return fine, atom.reshape(charges.shape)
 
 

time: 28.7 us -> 26.1 us (0.909)
  Pallas kernels: 9.57 us -> 7.05 us
    pallas_call x1, Pallas kernels: 3.32 us -> 1.67 us  [body(): pl.pallas_call(functools.partial(gather_kernel, plan), out_shape=[jax.Sha...]
    pallas_call x1, Pallas kernels: 4.56 us -> 3.69 us  [body(): pl.pallas_call(functools.partial(spread_kernel, plan), out_shape=[pltpu.V...]
where the time goes in v4:
time: 26.1 us; the launch traced here: 26 us
  starting transfers between devices  10.2 us (39%)
  waiting for transfers between devices  8.07 us (31%)
  Pallas kernels  7.05 us (27%)
  between operations  0.66 us (3%)
    ppermute x10, starting transfers between devices, moved(): return near(lax.ppermute(value, axis, pairs))  10.2 us
    ppermute x10, waiting for transfers between devices, moved(): return near(lax.ppermute(value, axis, pairs))  8.07 us
    pallas_call x1, Pallas kernels, body(): pl.pallas_call(functools.partial(spread_kernel, plan), out_shape=[pltpu.V...  3.69 us
    pallas_call x1, Pallas kernels, body(): pl.pallas_call(functools.partial(solve_kernel, plan), out_shape=[pltpu.VM...  1.69 us
    pallas_call x1, Pallas kernels, body(): pl.pallas_call(functools.partial(gather_kernel, plan), out_shape=[jax.Sha...  1.67 us
  transfers between devices with their start and end apart: 10, of which 8 were waited for; matrix products, arithmetic and copies ran while one was open for 0% of the time, Pallas kernels for 0%

profile of v4, /device:TPU:0, one launch (start us, length us, event | category | flops | bytes accessed | tf_op | source)
XLA Modules:
  0.0 26.0 jit_solution(4716652844040762636)
XLA Ops:
  0.6 3.7 %spread.1 = (f32[24,512]{1,0:T(8,128)S(1)}, bf16[64,128,256]{2,1,0:T(8,128)(2,1)S(1)}, f32[128,8,128]{2,1,0:T(8,128)S(1)}, f32[96,128]{1,0:T(8,128)S(1)}, f32[80...) custom-call(f32[128,128]{1,0:T(8,128)} %bitcast.5, f32[128,128]{1,0:T(8,128)} %bitcast.6, ...), custom_call_target="tpu_custom_call" | custom-call | tf_op jit(solution)/shard_map/spread/pallas_call | solution.py:396
  4.3 4.0 %collective-permute-start.4 = (f32[24,512]{1,0:T(8,128)S(1)}, f32[24,512]{1,0:T(8,128)S(1)}, u32[]{:S(2)}, u32[]{:S(2)}) collective-permute-start(f32[24,512]{1,0:T(8,128)S(1)} %get-tuple-element.15.refs_0_), channel_id=1, source_target_pairs={{0,20},{4,16},{8,28},{12,24},{16,4},{20,0},{24,12},{28,8},{1,21},{... | collective-permute-start | bytes 147464 | tf_op jit(solution)/shard_map/ppermute | solution.py:423
  8.3 0.5 %collective-permute-start.3 = (f32[24,512]{1,0:T(8,128)S(1)}, f32[24,512]{1,0:T(8,128)S(1)}, u32[]{:S(2)}, u32[]{:S(2)}) collective-permute-start(f32[24,512]{1,0:T(8,128)S(1)} %get-tuple-element.15.refs_0_), channel_id=1, source_target_pairs={{0,16},{4,20},{8,24},{12,28},{16,0},{20,4},{24,8},{28,12},{1,17},{... | collective-permute-start | bytes 147464 | tf_op jit(solution)/shard_map/ppermute | solution.py:423
  8.8 0.1 collective-permute-start
  9.0 0.0 collective-permute-start.1
  9.0 1.4 %collective-permute-done.4.refs_5_ = f32[24,512]{1,0:T(8,128)S(1)} collective-permute-done((f32[24,512]{1,0:T(8,128)S(1)}, f32[24,512]{1,0:T(8,128)S(1)}, u32[]{:S(2)}, u32[]{:S(2)}) %collective-permute-start.4) | collective-permute-done | bytes 49184 | tf_op jit(solution)/shard_map/ppermute | solution.py:423
  10.4 0.0 collective-permute-start.6
  10.4 2.0 %collective-permute-done.3.refs_4_ = f32[24,512]{1,0:T(8,128)S(1)} collective-permute-done((f32[24,512]{1,0:T(8,128)S(1)}, f32[24,512]{1,0:T(8,128)S(1)}, u32[]{:S(2)}, u32[]{:S(2)}) %collective-permute-start.3) | collective-permute-done | bytes 49184 | tf_op jit(solution)/shard_map/ppermute | solution.py:423
  12.4 0.0 collective-permute-start.5
  12.4 0.5 %collective-permute-done.refs_1_ = f32[24,512]{1,0:T(8,128)S(1)} collective-permute-done((f32[24,512]{1,0:T(8,128)S(1)}, f32[24,512]{1,0:T(8,128)S(1)}, u32[]{:S(2)}, u32[]{:S(2)}) %collective-permute-start) | collective-permute-done | bytes 49184 | tf_op jit(solution)/shard_map/ppermute | solution.py:423
  12.9 0.0 collective-permute-start.2
  12.9 0.0 collective-permute-done.1.refs_2_
  12.9 0.0 collective-permute-done.6.refs_7_
  12.9 0.7 %collective-permute-done.5.refs_6_ = f32[24,512]{1,0:T(8,128)S(1)} collective-permute-done((f32[24,512]{1,0:T(8,128)S(1)}, f32[24,512]{1,0:T(8,128)S(1)}, u32[]{:S(2)}, u32[]{:S(2)}) %collective-permute-start.5) | collective-permute-done | bytes 49184 | tf_op jit(solution)/shard_map/ppermute | solution.py:423
  13.6 0.5 %collective-permute-done.2.refs_3_ = f32[24,512]{1,0:T(8,128)S(1)} collective-permute-done((f32[24,512]{1,0:T(8,128)S(1)}, f32[24,512]{1,0:T(8,128)S(1)}, u32[]{:S(2)}, u32[]{:S(2)}) %collective-permute-start.2) | collective-permute-done | bytes 49184 | tf_op jit(solution)/shard_map/ppermute | solution.py:423
  14.1 1.7 %solve.1 = (f32[24,512]{1,0:T(8,128)S(1)}, f32[24,512]{1,0:T(8,128)S(1)}, f32[24,512]{1,0:T(8,128)S(1)}, f32[24,512]{1,0:T(8,128)S(1)}) custom-call(f32[24,512]{1,0:T(8,128)S(1)} %get-tuple-element.15.refs_0_, f32[24,512]{1,0:T(8,128)S(1)} %collective-permute-done.refs_1_, f32[24,512]{1,0:T(8,128)S(1)} %collective-permute-done.1.refs_2_, ...), custom_call_target="tpu_custom_call" | custom-call | tf_op jit(solution)/shard_map/solve/pallas_call | solution.py:442
  15.8 1.6 %collective-permute-start.7 = (f32[24,512]{1,0:T(8,128)S(1)}, f32[24,512]{1,0:T(8,128)S(1)}, u32[]{:S(2)}, u32[]{:S(2)}) collective-permute-start(f32[24,512]{1,0:T(8,128)S(1)} %get-tuple-element.20), channel_id=1, source_target_pairs={{0,1},{1,2},{2,3},{3,0},{4,5},{5,6},{6,7},{7,4},{8,9},{9,10},{10,1... | collective-permute-start | bytes 147464 | tf_op jit(solution)/shard_map/ppermute | solution.py:423
  17.5 2.6 %collective-permute-start.8 = (f32[24,512]{1,0:T(8,128)S(1)}, f32[24,512]{1,0:T(8,128)S(1)}, u32[]{:S(2)}, u32[]{:S(2)}) collective-permute-start(f32[24,512]{1,0:T(8,128)S(1)} %get-tuple-element.21), channel_id=1, source_target_pairs={{0,2},{1,3},{2,0},{3,1},{4,6},{5,7},{6,4},{7,5},{8,10},{9,11},{10,... | collective-permute-start | bytes 147464 | tf_op jit(solution)/shard_map/ppermute | solution.py:423
  20.1 1.3 %collective-permute-start.9 = (f32[24,512]{1,0:T(8,128)S(1)}, f32[24,512]{1,0:T(8,128)S(1)}, u32[]{:S(2)}, u32[]{:S(2)}) collective-permute-start(f32[24,512]{1,0:T(8,128)S(1)} %get-tuple-element.22), channel_id=1, source_target_pairs={{0,3},{1,0},{2,1},{3,2},{4,7},{5,4},{6,5},{7,6},{8,11},{9,8},{10,9... | collective-permute-start | bytes 147464 | tf_op jit(solution)/shard_map/ppermute | solution.py:423
  21.4 0.4 %collective-permute-done.7.refs_1_ = f32[24,512]{1,0:T(8,128)S(1)} collective-permute-done((f32[24,512]{1,0:T(8,128)S(1)}, f32[24,512]{1,0:T(8,128)S(1)}, u32[]{:S(2)}, u32[]{:S(2)}) %collective-permute-start.7) | collective-permute-done | bytes 49184 | tf_op jit(solution)/shard_map/ppermute | solution.py:423
  21.8 2.2 %collective-permute-done.8.refs_2_ = f32[24,512]{1,0:T(8,128)S(1)} collective-permute-done((f32[24,512]{1,0:T(8,128)S(1)}, f32[24,512]{1,0:T(8,128)S(1)}, u32[]{:S(2)}, u32[]{:S(2)}) %collective-permute-start.8) | collective-permute-done | bytes 49184 | tf_op jit(solution)/shard_map/ppermute | solution.py:423
  24.0 0.4 %collective-permute-done.9.refs_3_ = f32[24,512]{1,0:T(8,128)S(1)} collective-permute-done((f32[24,512]{1,0:T(8,128)S(1)}, f32[24,512]{1,0:T(8,128)S(1)}, u32[]{:S(2)}, u32[]{:S(2)}) %collective-permute-start.9) | collective-permute-done | bytes 49184 | tf_op jit(solution)/shard_map/ppermute | solution.py:423
  24.3 1.7 %gather.1 = (f32[16,16,16]{2,1,0:T(8,128)}, f32[128,128]{1,0:T(8,128)}) custom-call(f32[24,512]{1,0:T(8,128)S(1)} %get-tuple-element.19.refs_0_, f32[24,512]{1,0:T(8,128)S(1)} %collective-permute-done.7.refs_1_, f32[24,512]{1,0:T(8,128)S(1)} %collective-permute-done.8.refs_2_, f32[24,512]{1,0:T(8,128)S(1)} %collective-permute-done.9.refs_3_, ...), custom_call_target="tpu_custom_call" | custom-call | tf_op jit(solution)/shard_map/gather/pallas_call | solution.py:457
Async XLA Ops:
  4.3 6.0 %collective-permute-start.4 = (f32[24,512]{1,0:T(8,128)S(1)}, f32[24,512]{1,0:T(8,128)S(1)}, u32[]{:S(2)}, u32[]{:S(2)}) collective-permute-start(f32[24,512]{1,0:T(8,128)S(1)} %get-tuple-element.15.refs_0_), channel_id=1, source_target_pairs={{0,20},{4,16},{8,28},{12,24},{16,4},{20,0},{24,12},{28,8},{1,21},{... | collective-permute-start | bytes 147464 | tf_op jit(solution)/shard_map/ppermute | solution.py:423
  8.3 4.1 %collective-permute-start.3 = (f32[24,512]{1,0:T(8,128)S(1)}, f32[24,512]{1,0:T(8,128)S(1)}, u32[]{:S(2)}, u32[]{:S(2)}) collective-permute-start(f32[24,512]{1,0:T(8,128)S(1)} %get-tuple-element.15.refs_0_), channel_id=1, source_target_pairs={{0,16},{4,20},{8,24},{12,28},{16,0},{20,4},{24,8},{28,12},{1,17},{... | collective-permute-start | bytes 147464 | tf_op jit(solution)/shard_map/ppermute | solution.py:423
  8.8 4.1 %collective-permute-start = (f32[24,512]{1,0:T(8,128)S(1)}, f32[24,512]{1,0:T(8,128)S(1)}, u32[]{:S(2)}, u32[]{:S(2)}) collective-permute-start(f32[24,512]{1,0:T(8,128)S(1)} %get-tuple-element.15.refs_0_), channel_id=1, source_target_pairs={{0,4},{4,0},{8,12},{12,8},{16,20},{20,16},{24,28},{28,24},{1,5},{5... | collective-permute-start | bytes 147464 | tf_op jit(solution)/shard_map/ppermute | solution.py:423
  9.0 4.0 %collective-permute-start.1 = (f32[24,512]{1,0:T(8,128)S(1)}, f32[24,512]{1,0:T(8,128)S(1)}, u32[]{:S(2)}, u32[]{:S(2)}) collective-permute-start(f32[24,512]{1,0:T(8,128)S(1)} %get-tuple-element.15.refs_0_), channel_id=1, source_target_pairs={{0,8},{8,0},{16,24},{24,16},{1,9},{9,1},{17,25},{25,17},{2,10},{10... | collective-permute-start | bytes 147464 | tf_op jit(solution)/shard_map/ppermute | solution.py:423
  10.4 2.5 %collective-permute-start.6 = (f32[24,512]{1,0:T(8,128)S(1)}, f32[24,512]{1,0:T(8,128)S(1)}, u32[]{:S(2)}, u32[]{:S(2)}) collective-permute-start(f32[24,512]{1,0:T(8,128)S(1)} %collective-permute-done.4.refs_5_), channel_id=1, source_target_pairs={{0,8},{8,0},{16,24},{24,16},{1,9},{9,1},{17,25},{25,17},{2,10},{10... | collective-permute-start | bytes 147464 | tf_op jit(solution)/shard_map/ppermute | solution.py:423
  12.4 1.2 %collective-permute-start.5 = (f32[24,512]{1,0:T(8,128)S(1)}, f32[24,512]{1,0:T(8,128)S(1)}, u32[]{:S(2)}, u32[]{:S(2)}) collective-permute-start(f32[24,512]{1,0:T(8,128)S(1)} %collective-permute-done.3.refs_4_), channel_id=1, source_target_pairs={{0,8},{8,0},{16,24},{24,16},{1,9},{9,1},{17,25},{25,17},{2,10},{10... | collective-permute-start | bytes 147464 | tf_op jit(solution)/shard_map/ppermute | solution.py:423
  12.9 1.2 %collective-permute-start.2 = (f32[24,512]{1,0:T(8,128)S(1)}, f32[24,512]{1,0:T(8,128)S(1)}, u32[]{:S(2)}, u32[]{:S(2)}) collective-permute-start(f32[24,512]{1,0:T(8,128)S(1)} %collective-permute-done.refs_1_), channel_id=1, source_target_pairs={{0,8},{8,0},{16,24},{24,16},{1,9},{9,1},{17,25},{25,17},{2,10},{10... | collective-permute-start | bytes 147464 | tf_op jit(solution)/shard_map/ppermute | solution.py:423
  15.8 5.9 %collective-permute-start.7 = (f32[24,512]{1,0:T(8,128)S(1)}, f32[24,512]{1,0:T(8,128)S(1)}, u32[]{:S(2)}, u32[]{:S(2)}) collective-permute-start(f32[24,512]{1,0:T(8,128)S(1)} %get-tuple-element.20), channel_id=1, source_target_pairs={{0,1},{1,2},{2,3},{3,0},{4,5},{5,6},{6,7},{7,4},{8,9},{9,10},{10,1... | collective-permute-start | bytes 147464 | tf_op jit(solution)/shard_map/ppermute | solution.py:423
  17.5 6.5 %collective-permute-start.8 = (f32[24,512]{1,0:T(8,128)S(1)}, f32[24,512]{1,0:T(8,128)S(1)}, u32[]{:S(2)}, u32[]{:S(2)}) collective-permute-start(f32[24,512]{1,0:T(8,128)S(1)} %get-tuple-element.21), channel_id=1, source_target_pairs={{0,2},{1,3},{2,0},{3,1},{4,6},{5,7},{6,4},{7,5},{8,10},{9,11},{10,... | collective-permute-start | bytes 147464 | tf_op jit(solution)/shard_map/ppermute | solution.py:423
  20.1 4.3 %collective-permute-start.9 = (f32[24,512]{1,0:T(8,128)S(1)}, f32[24,512]{1,0:T(8,128)S(1)}, u32[]{:S(2)}, u32[]{:S(2)}) collective-permute-start(f32[24,512]{1,0:T(8,128)S(1)} %get-tuple-element.22), channel_id=1, source_target_pairs={{0,3},{1,0},{2,1},{3,2},{4,7},{5,4},{6,5},{7,6},{8,11},{9,8},{10,9... | collective-permute-start | bytes 147464 | tf_op jit(solution)/shard_map/ppermute | solution.py:423

commit v5 on v4

--- a/solution.py
+++ b/solution.py
@@ -14,7 +14,6 @@
 TERMS = 5
 SLOT = LANES // TERMS
 PARTS = 4
-GROUP = 8
 RIM = 4
 TAPS = (-0.0625, 0.0, 0.5625, 1.0, 0.5625, 0.0, -0.0625)
 highest = lax.Precision.HIGHEST
@@ -83,6 +82,11 @@
 
 def round_up(value, step):
     return -(-value // step) * step
+
+
+def halves(table):
+    high = table.astype(jnp.bfloat16)
+    return high, (table - high.astype(np.float32)).astype(jnp.bfloat16)
 
 
 def partner(device, order, count):
@@ -106,27 +110,6 @@
         assert self.columns * nbins[2] == LANES and nbins[2] == 8 and self.columns % 2 == 0
         assert TERMS * self.zp <= LANES and self.width[0] <= SLOT
 
-    def place_matrix(self):
-        nbx, nby, _ = self.nbins
-        m = np.zeros((self.width[1] * self.xp, self.columns * 64), np.float32)
-        for a in range(nbx):
-            for b in range(nby):
-                for i in range(8):
-                    for j in range(8):
-                        m[(4 * b + j) * self.xp + 4 * a + i, (a * nby + b) * 64 + i * 8 + j] = 1.0
-        return jnp.asarray(m, jnp.bfloat16)
-
-    def pick_matrix(self):
-        nbx, nby, _ = self.nbins
-        m = np.zeros((self.columns * 64, self.lanes), np.float32)
-        for a in range(nbx):
-            for b in range(nby):
-                for i in range(8):
-                    for j in range(8):
-                        chunk, part = divmod(4 * b + j, TERMS)
-                        m[(a * nby + b) * 64 + i * 8 + j, chunk * LANES + part * SLOT + 4 * a + i] = 1.0
-        return jnp.asarray(m, jnp.bfloat16)
-
     def x_table(self):
         nx, width = self.counts[0], self.width[0]
         m = windowed(self.points[0], nx)
@@ -138,7 +121,10 @@
                     table[d, o * self.xp : o * self.xp + width, t * SLOT : t * SLOT + width] = (
                         m[t, d, :, source, :].T
                     )
-        return jnp.asarray(table)
+        high, low = halves(table)
+        upper = np.concatenate([high, low], axis=2)
+        lower = np.concatenate([high, np.zeros_like(low)], axis=2)
+        return jnp.asarray(np.concatenate([upper, lower], axis=1))
 
     def x_source(self, device, order):
         pair = self.pair
@@ -167,7 +153,10 @@
                     table[d, o * self.zp : o * self.zp + width, t * self.zp : t * self.zp + width] = (
                         scales[t] * m[t, partner(d, o, nz), :, d, :]
                     )
-        return jnp.asarray(table)
+        high, low = halves(table)
+        upper = np.concatenate([high, high], axis=2)
+        lower = np.concatenate([low, np.zeros_like(low)], axis=2)
+        return jnp.asarray(np.concatenate([upper, lower], axis=1))
 
 
 SCALE = (1.0 / 6.0) ** (1.0 / 3.0)
@@ -186,15 +175,14 @@
 
 
 def spread_kernel(plan, *refs):
-    hbm, tables, (out_ref, outer_s, along_z_s) = refs[:6], refs[6:10], refs[10:13]
-    tables_out, local, (column_s, sems) = refs[13:17], refs[17:23], refs[23:]
+    hbm, tables, (out_ref, outer_s, along_z_s) = refs[:5], refs[5:8], refs[8:11]
+    tables_out, local, (column_s, turned_s, grid_s, sems) = refs[11:14], refs[14:19], refs[19:]
     copies = [pltpu.make_async_copy(a, b, sems.at[n]) for n, (a, b) in enumerate(zip(hbm, local))]
-    for n, (table, target, axis) in enumerate(zip(tables, tables_out, ("gx", "gy", "gz", None))):
-        source = table if axis is None else table.at[lax.axis_index(axis)]
-        copies.append(pltpu.make_async_copy(source, target, sems.at[6 + n]))
+    for n, (table, target, axis) in enumerate(zip(tables, tables_out, ("gx", "gy", "gz"))):
+        copies.append(pltpu.make_async_copy(table.at[lax.axis_index(axis)], target, sems.at[5 + n]))
     for copy in copies:
         copy.start()
-    x_ref, y_ref, z_ref, charge_ref, counts_ref, place_s = local
+    x_ref, y_ref, z_ref, charge_ref, counts_ref = local
     slots = charge_ref.shape[1]
     nbx, nby, nbz = plan.nbins
     zp = plan.zp
@@ -212,7 +200,9 @@
         weight_y = bspline(y_ref[pl.ds(r, 1), :] + node)
         weight_z = bspline(z_ref[pl.ds(r, 1), :] + node)
         weight_z = jnp.where(slot < counts_ref[p // nby, p % nby, c], weight_z, 0.0)
-        outer = split_rows(jnp.concatenate([weight_x[i : i + 1, :] * weight_y for i in range(8)], axis=0))
+        outer = split_rows(
+            jnp.concatenate([weight_y[j : j + 1, :] * weight_x for j in range(8)], axis=0)
+        )
         outer_s[r // 2, :, (c % 2) * slots : (c % 2 + 1) * slots] = outer
         along_z_s[r] = weight_z
         return outer, split_rows(weight_z * charge_ref[pl.ds(r, 1), :])
@@ -243,38 +233,45 @@
 
     left = lax.broadcasted_iota(jnp.int32, (8, LANES), 1) < 64
 
-    def one_group(g, carry):
-        for q in range(GROUP):
-            pair = g * GROUP + q
-            even = one_column(2 * pair)
-            odd = one_column(2 * pair + 1)
-            for n, (a, b) in enumerate(zip(even, odd)):
-                column_s[pl.ds(pl.multiple_of(pair * zp, 8) + 8 * n, 8), :] = jnp.where(left, a, b)
-        return carry
-
-    lax.fori_loop(0, plan.columns // 2 // GROUP, one_group, 0)
-    columns = jnp.concatenate(
-        [column_s[p * plan.zp : (p + 1) * plan.zp, :] for p in range(plan.columns // 2)], axis=1
-    )
-    pad = jnp.zeros((LANES - 2 * zp, columns.shape[1]), jnp.bfloat16)
-    copies[5].wait()
-    grid = lax.dot_general(
-        place_s[...], jnp.concatenate([split_rows(columns), pad], axis=0), (((1,), (1,)), ((), ())),
-        preferred_element_type=jnp.float32,
-    )
-    grid = grid + pltpu.roll(grid, LANES - zp, 1)
+    for pair in range(plan.columns // 2):
+        even = one_column(2 * pair)
+        odd = one_column(2 * pair + 1)
+        for n, (a, b) in enumerate(zip(even, odd)):
+            at = pair * zp + 8 * n
+            column_s[at : at + 8, :] = jnp.where(left, a, b)
     xp = plan.xp
+    for pair in range(plan.columns // 2):
+        turned_s[pair * LANES : (pair + 1) * LANES, :zp] = column_s[pair * zp : (pair + 1) * zp, :].T
+
+    def folded(a, y):
+        total = None
+        for b in range(nby):
+            j = y - 4 * b
+            if 0 <= j < 8:
+                at = (a * nby + b) * 64 + j * 8
+                piece = turned_s[at : at + 8, :]
+                total = piece if total is None else total + piece
+        return total
+
+    for y in range(plan.width[1]):
+        for a in range(0, nbx, 2):
+            grid_s[y * xp + 4 * a : y * xp + 4 * a + 8, :] = folded(a, y)
+        rest = xp - 4 * nbx
+        grid_s[(y + 1) * xp - rest : (y + 1) * xp, :] = jnp.zeros((rest, LANES), jnp.float32)
+        for a in range(1, nbx, 2):
+            at = slice(y * xp + 4 * a, y * xp + 4 * a + 8)
+            grid_s[at, :] = grid_s[at, :] + folded(a, y)
     group = lax.broadcasted_iota(jnp.int32, (xp, LANES), 1) // plan.zp
     for chunk in range(plan.chunks):
         merged = jnp.zeros((xp, LANES), jnp.float32)
         for b in range(TERMS):
             y = chunk * TERMS + b
             if y < plan.width[1]:
-                piece = grid[y * xp : (y + 1) * xp, :]
+                piece = grid_s[y * xp : (y + 1) * xp, :]
                 moved = pltpu.roll(piece, b * plan.zp, 1) if b else piece
                 merged = jnp.where(group == b, moved, merged)
         out_ref[:, chunk * LANES : (chunk + 1) * LANES] = merged
-    for copy in copies[6:]:
+    for copy in copies[5:]:
         copy.wait()
 
 
@@ -291,10 +288,10 @@
     span = plan.chunks * TERMS
     for oy in range(ny):
         gathered = jnp.concatenate([blocks[ox * ny + oy][...] for ox in range(nx)], axis=0)
-        mid_s[oy * plan.lanes : (oy + 1) * plan.lanes, :] = lax.dot_general(
-            gathered, x_matrix, (((0,), (0,)), ((), ())), precision=highest,
-            preferred_element_type=jnp.float32,
+        both = lax.dot_general(
+            split_rows(gathered), x_matrix, (((0,), (0,)), ((), ())), preferred_element_type=jnp.float32
         )
+        mid_s[oy * plan.lanes : (oy + 1) * plan.lanes, :] = both[:, :LANES] + both[:, LANES:]
     slot = lax.broadcasted_iota(jnp.int32, (zp, LANES), 1) // SLOT
     for chunk in range(plan.chunks):
         sums = [jnp.zeros((zp, LANES), jnp.float32) for _ in range(TERMS)]
@@ -312,7 +309,8 @@
                 moved = pltpu.roll(sums[b], shift, 1) if shift else sums[b]
                 merged = jnp.where(slot == b, moved, merged)
             term_s[t * zp : (t + 1) * zp, chunk * LANES : (chunk + 1) * LANES] = merged
-    result = jnp.dot(tables[2][...], term_s[...], precision=highest, preferred_element_type=jnp.float32)
+    both = jnp.dot(tables[2][...], split_rows(term_s[...]), preferred_element_type=jnp.float32)
+    result = both[: nz * zp, :] + both[nz * zp :, :]
     for o in range(nz):
         outs[o][...] = result[o * zp : (o + 1) * zp, :]
 
@@ -320,31 +318,39 @@
 def gather_kernel(plan, *refs):
     nz = plan.counts[2]
     parts = refs[:nz]
-    outer_s, along_z_s, pick_ref, fine_hbm, atom_hbm = refs[nz : nz + 5]
-    field_s, column_s, fine_ref, atom_ref, sems = refs[nz + 5 :]
+    outer_s, along_z_s, fine_hbm, atom_hbm = refs[nz : nz + 4]
+    field_s, column_s, turned_s, inner_s, order_s, fine_ref, atom_ref, sems = refs[nz + 4 :]
     nbx, nby, nbz = plan.nbins
     zp = plan.zp
     lx, ly, lz = plan.local
     total = parts[0][...]
     for part in parts[1:]:
         total = total + part[...]
-    columns = lax.dot_general(
-        split_rows(total), pick_ref[...], (((1,), (1,)), ((), ())), preferred_element_type=jnp.float32
-    )
-    columns = columns[:zp, :] + columns[zp:, :]
+    for chunk in range(plan.chunks):
+        field_s[chunk * LANES : (chunk + 1) * LANES, :zp] = total[:, chunk * LANES : (chunk + 1) * LANES].T
     left = lax.broadcasted_iota(jnp.int32, (zp, LANES), 1) < 64
     for pair in range(plan.columns // 2):
-        both = columns[:, pair * LANES : (pair + 1) * LANES]
+        for half in range(2):
+            a, b = divmod(2 * pair + half, nby)
+            for j in range(8):
+                chunk, part = divmod(4 * b + j, TERMS)
+                at = chunk * LANES + part * SLOT + 4 * a
+                to = pair * LANES + half * 64 + j * 8
+                turned_s[to : to + 8, :] = field_s[at : at + 8, :]
+        both = turned_s[pair * LANES : (pair + 1) * LANES, :zp].T
         turned = pltpu.roll(both, 64, 1)
         column_s[2 * pair * zp : (2 * pair + 1) * zp, :] = jnp.where(left, both, turned)
         column_s[(2 * pair + 1) * zp : (2 * pair + 2) * zp, :] = jnp.where(left, turned, both)
     for chunk in range(plan.chunks):
-        turned = total[:, chunk * LANES : (chunk + 1) * LANES].T
-        field_s[chunk * LANES : (chunk + 1) * LANES, :zp] = turned
+        inner_s[chunk * LANES : (chunk + 1) * LANES, :lz] = total[
+            2 : 2 + lz, chunk * LANES : (chunk + 1) * LANES
+        ].T
     for y in range(ly):
         chunk, b = divmod(y + 2, TERMS)
         at = chunk * LANES + b * SLOT + 2
-        fine_ref[:, y, :] = field_s[at : at + lx, 2 : 2 + lz]
+        order_s[pl.ds(y, lx, stride=ly), :] = inner_s[at : at + lx, :]
+    for x in range(lx):
+        fine_ref[x] = order_s[x * ly : (x + 1) * ly, :lz]
     copies = [pltpu.make_async_copy(fine_ref, fine_hbm, sems.at[0])]
     copies[0].start()
     slots = atom_ref.shape[1]
@@ -387,12 +393,11 @@
     hbm = pl.BlockSpec(memory_space=pltpu.HBM)
     f32 = jnp.float32
     params = pltpu.CompilerParams(vmem_limit_bytes=12 << 20)
-    place, pick = plan.place_matrix(), plan.pick_matrix()
 
     def far(value):
         return pltpu.with_memory_space_constraint(value, pltpu.HBM)
 
-    tables = (plan.x_table(), plan.y_table(), plan.z_table(), pick)
+    tables = (plan.x_table(), plan.y_table(), plan.z_table())
     spread, *weights = pl.pallas_call(
         functools.partial(spread_kernel, plan),
         out_shape=[
@@ -400,21 +405,21 @@
             pltpu.VMEM((LANES // 2, LANES, 2 * slots), jnp.bfloat16),
             pltpu.VMEM((LANES, 8, slots), f32),
         ]
-        + [pltpu.VMEM(t.shape[1:], t.dtype) for t in tables[:3]]
-        + [pltpu.VMEM(pick.shape, pick.dtype)],
-        in_specs=[hbm] * 10,
-        out_specs=[vmem] * 7,
+        + [pltpu.VMEM(t.shape[1:], t.dtype) for t in tables],
+        in_specs=[hbm] * 8,
+        out_specs=[vmem] * 6,
         scratch_shapes=[pltpu.VMEM((LANES, slots), f32)] * 4
         + [
             pltpu.SMEM(nbins, jnp.int32),
-            pltpu.VMEM(place.shape, place.dtype),
             pltpu.VMEM((plan.columns // 2 * plan.zp, LANES), f32),
-            pltpu.SemaphoreType.DMA((10,)),
+            pltpu.VMEM((plan.columns * 64, LANES), f32),
+            pltpu.VMEM((plan.width[1] * plan.xp, LANES), f32),
+            pltpu.SemaphoreType.DMA((8,)),
         ],
         compiler_params=params,
         name="spread",
-    )(*(far(v) for v in (*flat[1:], flat[0], counts, place, *tables)))
-    weights, tables, pick = weights[:2], weights[2:5], weights[5]
+    )(*(far(v) for v in (*flat[1:], flat[0], counts, *tables)))
+    weights, tables = weights[:2], weights[2:]
 
     def near(value):
         return pltpu.with_memory_space_constraint(value, pltpu.VMEM)
@@ -460,18 +465,21 @@
             jax.ShapeDtypeStruct(plan.local, f32),
             jax.ShapeDtypeStruct((LANES, slots), f32),
         ],
-        in_specs=[vmem] * (nz + 3),
+        in_specs=[vmem] * (nz + 2),
         out_specs=[hbm, hbm],
         scratch_shapes=[
             pltpu.VMEM((plan.lanes, LANES), f32),
             pltpu.VMEM((plan.columns * plan.zp, LANES), f32),
+            pltpu.VMEM((plan.columns * 64, LANES), f32),
+            pltpu.VMEM((plan.lanes, LANES), f32),
+            pltpu.VMEM((plan.local[0] * plan.local[1], LANES), f32),
             pltpu.VMEM(plan.local, f32),
             pltpu.VMEM((LANES, slots), f32),
             pltpu.SemaphoreType.DMA((1 + PARTS,)),
         ],
         compiler_params=params,
         name="gather",
-    )(*parts, *weights, pick)
+    )(*parts, *weights)
     return fine, atom.reshape(charges.shape)
 
 

time: 26.1 us -> 25.7 us (0.985)
  Pallas kernels: 7.05 us -> 6.59 us
    pallas_call x1, Pallas kernels: 1.69 us -> 1.3 us  [body(): pl.pallas_call(functools.partial(solve_kernel, plan), out_shape=[pltpu.VM...]
    pallas_call x1, Pallas kernels: 3.69 us -> 3.42 us  [body(): pl.pallas_call(functools.partial(spread_kernel, plan), out_shape=[pltpu.V...]
where the time goes in v5:
time: 25.7 us; the launch traced here: 25.5 us
  starting transfers between devices  10.2 us (40%)
  waiting for transfers between devices  8.08 us (31%)
  Pallas kernels  6.59 us (26%)
  between operations  0.66 us (3%)
    ppermute x10, starting transfers between devices, moved(): return near(lax.ppermute(value, axis, pairs))  10.2 us
    ppermute x10, waiting for transfers between devices, moved(): return near(lax.ppermute(value, axis, pairs))  8.08 us
    pallas_call x1, Pallas kernels, body(): pl.pallas_call(functools.partial(spread_kernel, plan), out_shape=[pltpu.V...  3.42 us
    pallas_call x1, Pallas kernels, body(): pl.pallas_call(functools.partial(gather_kernel, plan), out_shape=[jax.Sha...  1.87 us
    pallas_call x1, Pallas kernels, body(): pl.pallas_call(functools.partial(solve_kernel, plan), out_shape=[pltpu.VM...  1.3 us
  transfers between devices with their start and end apart: 10, of which 8 were waited for; matrix products, arithmetic and copies ran while one was open for 0% of the time, Pallas kernels for 0%

profile of v5, /device:TPU:0, one launch (start us, length us, event | category | flops | bytes accessed | tf_op | source)
XLA Modules:
  0.0 25.5 jit_solution(11770775909747005455)
XLA Ops:
  0.6 3.4 %spread.1 = (f32[24,512]{1,0:T(8,128)S(1)}, bf16[64,128,256]{2,1,0:T(8,128)(2,1)S(1)}, f32[128,8,128]{2,1,0:T(8,128)S(1)}, bf16[192,256]{1,0:T(8,128)(2,1)S(1)},...) custom-call(f32[128,128]{1,0:T(8,128)} %bitcast.5, f32[128,128]{1,0:T(8,128)} %bitcast.6, f32[128,128]{1,0:T(8,128)} %bitcast.7, ...), custom_call_target="tpu_custom_call" | custom-call | tf_op jit(solution)/shard_map/spread/pallas_call | solution.py:401
  4.1 4.0 %collective-permute-start.4 = (f32[24,512]{1,0:T(8,128)S(1)}, f32[24,512]{1,0:T(8,128)S(1)}, u32[]{:S(2)}, u32[]{:S(2)}) collective-permute-start(f32[24,512]{1,0:T(8,128)S(1)} %get-tuple-element.14.refs_0_), channel_id=1, source_target_pairs={{0,20},{4,16},{8,28},{12,24},{16,4},{20,0},{24,12},{28,8},{1,21},{... | collective-permute-start | bytes 147464 | tf_op jit(solution)/shard_map/ppermute | solution.py:428
  8.1 0.5 %collective-permute-start.3 = (f32[24,512]{1,0:T(8,128)S(1)}, f32[24,512]{1,0:T(8,128)S(1)}, u32[]{:S(2)}, u32[]{:S(2)}) collective-permute-start(f32[24,512]{1,0:T(8,128)S(1)} %get-tuple-element.14.refs_0_), channel_id=1, source_target_pairs={{0,16},{4,20},{8,24},{12,28},{16,0},{20,4},{24,8},{28,12},{1,17},{... | collective-permute-start | bytes 147464 | tf_op jit(solution)/shard_map/ppermute | solution.py:428
  8.6 0.1 collective-permute-start
  8.7 0.0 collective-permute-start.1
  8.7 1.4 %collective-permute-done.4.refs_5_ = f32[24,512]{1,0:T(8,128)S(1)} collective-permute-done((f32[24,512]{1,0:T(8,128)S(1)}, f32[24,512]{1,0:T(8,128)S(1)}, u32[]{:S(2)}, u32[]{:S(2)}) %collective-permute-start.4) | collective-permute-done | bytes 49184 | tf_op jit(solution)/shard_map/ppermute | solution.py:428
  10.1 0.0 collective-permute-start.6
  10.1 2.0 %collective-permute-done.3.refs_4_ = f32[24,512]{1,0:T(8,128)S(1)} collective-permute-done((f32[24,512]{1,0:T(8,128)S(1)}, f32[24,512]{1,0:T(8,128)S(1)}, u32[]{:S(2)}, u32[]{:S(2)}) %collective-permute-start.3) | collective-permute-done | bytes 49184 | tf_op jit(solution)/shard_map/ppermute | solution.py:428
  12.1 0.0 collective-permute-start.5
  12.1 0.5 %collective-permute-done.refs_1_ = f32[24,512]{1,0:T(8,128)S(1)} collective-permute-done((f32[24,512]{1,0:T(8,128)S(1)}, f32[24,512]{1,0:T(8,128)S(1)}, u32[]{:S(2)}, u32[]{:S(2)}) %collective-permute-start) | collective-permute-done | bytes 49184 | tf_op jit(solution)/shard_map/ppermute | solution.py:428
  12.6 0.0 collective-permute-start.2
  12.7 0.0 collective-permute-done.1.refs_2_
  12.7 0.0 collective-permute-done.6.refs_7_
  12.7 0.7 %collective-permute-done.5.refs_6_ = f32[24,512]{1,0:T(8,128)S(1)} collective-permute-done((f32[24,512]{1,0:T(8,128)S(1)}, f32[24,512]{1,0:T(8,128)S(1)}, u32[]{:S(2)}, u32[]{:S(2)}) %collective-permute-start.5) | collective-permute-done | bytes 49184 | tf_op jit(solution)/shard_map/ppermute | solution.py:428
  13.4 0.5 %collective-permute-done.2.refs_3_ = f32[24,512]{1,0:T(8,128)S(1)} collective-permute-done((f32[24,512]{1,0:T(8,128)S(1)}, f32[24,512]{1,0:T(8,128)S(1)}, u32[]{:S(2)}, u32[]{:S(2)}) %collective-permute-start.2) | collective-permute-done | bytes 49184 | tf_op jit(solution)/shard_map/ppermute | solution.py:428
  13.9 1.3 %solve.1 = (f32[24,512]{1,0:T(8,128)S(1)}, f32[24,512]{1,0:T(8,128)S(1)}, f32[24,512]{1,0:T(8,128)S(1)}, f32[24,512]{1,0:T(8,128)S(1)}) custom-call(f32[24,512]{1,0:T(8,128)S(1)} %get-tuple-element.14.refs_0_, f32[24,512]{1,0:T(8,128)S(1)} %collective-permute-done.refs_1_, f32[24,512]{1,0:T(8,128)S(1)} %collective-permute-done.1.refs_2_, ...), custom_call_target="tpu_custom_call" | custom-call | tf_op jit(solution)/shard_map/solve/pallas_call | solution.py:447
  15.2 1.6 %collective-permute-start.7 = (f32[24,512]{1,0:T(8,128)S(1)}, f32[24,512]{1,0:T(8,128)S(1)}, u32[]{:S(2)}, u32[]{:S(2)}) collective-permute-start(f32[24,512]{1,0:T(8,128)S(1)} %get-tuple-element.19), channel_id=1, source_target_pairs={{0,1},{1,2},{2,3},{3,0},{4,5},{5,6},{6,7},{7,4},{8,9},{9,10},{10,1... | collective-permute-start | bytes 147464 | tf_op jit(solution)/shard_map/ppermute | solution.py:428
  16.8 2.6 %collective-permute-start.8 = (f32[24,512]{1,0:T(8,128)S(1)}, f32[24,512]{1,0:T(8,128)S(1)}, u32[]{:S(2)}, u32[]{:S(2)}) collective-permute-start(f32[24,512]{1,0:T(8,128)S(1)} %get-tuple-element.20), channel_id=1, source_target_pairs={{0,2},{1,3},{2,0},{3,1},{4,6},{5,7},{6,4},{7,5},{8,10},{9,11},{10,... | collective-permute-start | bytes 147464 | tf_op jit(solution)/shard_map/ppermute | solution.py:428
  19.4 1.3 %collective-permute-start.9 = (f32[24,512]{1,0:T(8,128)S(1)}, f32[24,512]{1,0:T(8,128)S(1)}, u32[]{:S(2)}, u32[]{:S(2)}) collective-permute-start(f32[24,512]{1,0:T(8,128)S(1)} %get-tuple-element.21), channel_id=1, source_target_pairs={{0,3},{1,0},{2,1},{3,2},{4,7},{5,4},{6,5},{7,6},{8,11},{9,8},{10,9... | collective-permute-start | bytes 147464 | tf_op jit(solution)/shard_map/ppermute | solution.py:428
  20.8 0.4 %collective-permute-done.7.refs_1_ = f32[24,512]{1,0:T(8,128)S(1)} collective-permute-done((f32[24,512]{1,0:T(8,128)S(1)}, f32[24,512]{1,0:T(8,128)S(1)}, u32[]{:S(2)}, u32[]{:S(2)}) %collective-permute-start.7) | collective-permute-done | bytes 49184 | tf_op jit(solution)/shard_map/ppermute | solution.py:428
  21.1 2.2 %collective-permute-done.8.refs_2_ = f32[24,512]{1,0:T(8,128)S(1)} collective-permute-done((f32[24,512]{1,0:T(8,128)S(1)}, f32[24,512]{1,0:T(8,128)S(1)}, u32[]{:S(2)}, u32[]{:S(2)}) %collective-permute-start.8) | collective-permute-done | bytes 49184 | tf_op jit(solution)/shard_map/ppermute | solution.py:428
  23.3 0.4 %collective-permute-done.9.refs_3_ = f32[24,512]{1,0:T(8,128)S(1)} collective-permute-done((f32[24,512]{1,0:T(8,128)S(1)}, f32[24,512]{1,0:T(8,128)S(1)}, u32[]{:S(2)}, u32[]{:S(2)}) %collective-permute-start.9) | collective-permute-done | bytes 49184 | tf_op jit(solution)/shard_map/ppermute | solution.py:428
  23.7 1.9 %gather.1 = (f32[16,16,16]{2,1,0:T(8,128)}, f32[128,128]{1,0:T(8,128)}) custom-call(f32[24,512]{1,0:T(8,128)S(1)} %get-tuple-element.18.refs_0_, f32[24,512]{1,0:T(8,128)S(1)} %collective-permute-done.7.refs_1_, f32[24,512]{1,0:T(8,128)S(1)} %collective-permute-done.8.refs_2_, f32[24,512]{1,0:T(8,128)S(1)} %collective-permute-done.9.refs_3_, ...), custom_call_target="tpu_custom_call" | custom-call | tf_op jit(solution)/shard_map/gather/pallas_call | solution.py:462
Async XLA Ops:
  4.1 6.1 %collective-permute-start.4 = (f32[24,512]{1,0:T(8,128)S(1)}, f32[24,512]{1,0:T(8,128)S(1)}, u32[]{:S(2)}, u32[]{:S(2)}) collective-permute-start(f32[24,512]{1,0:T(8,128)S(1)} %get-tuple-element.14.refs_0_), channel_id=1, source_target_pairs={{0,20},{4,16},{8,28},{12,24},{16,4},{20,0},{24,12},{28,8},{1,21},{... | collective-permute-start | bytes 147464 | tf_op jit(solution)/shard_map/ppermute | solution.py:428
  8.1 4.1 %collective-permute-start.3 = (f32[24,512]{1,0:T(8,128)S(1)}, f32[24,512]{1,0:T(8,128)S(1)}, u32[]{:S(2)}, u32[]{:S(2)}) collective-permute-start(f32[24,512]{1,0:T(8,128)S(1)} %get-tuple-element.14.refs_0_), channel_id=1, source_target_pairs={{0,16},{4,20},{8,24},{12,28},{16,0},{20,4},{24,8},{28,12},{1,17},{... | collective-permute-start | bytes 147464 | tf_op jit(solution)/shard_map/ppermute | solution.py:428
  8.6 4.1 %collective-permute-start = (f32[24,512]{1,0:T(8,128)S(1)}, f32[24,512]{1,0:T(8,128)S(1)}, u32[]{:S(2)}, u32[]{:S(2)}) collective-permute-start(f32[24,512]{1,0:T(8,128)S(1)} %get-tuple-element.14.refs_0_), channel_id=1, source_target_pairs={{0,4},{4,0},{8,12},{12,8},{16,20},{20,16},{24,28},{28,24},{1,5},{5... | collective-permute-start | bytes 147464 | tf_op jit(solution)/shard_map/ppermute | solution.py:428
  8.7 4.0 %collective-permute-start.1 = (f32[24,512]{1,0:T(8,128)S(1)}, f32[24,512]{1,0:T(8,128)S(1)}, u32[]{:S(2)}, u32[]{:S(2)}) collective-permute-start(f32[24,512]{1,0:T(8,128)S(1)} %get-tuple-element.14.refs_0_), channel_id=1, source_target_pairs={{0,8},{8,0},{16,24},{24,16},{1,9},{9,1},{17,25},{25,17},{2,10},{10... | collective-permute-start | bytes 147464 | tf_op jit(solution)/shard_map/ppermute | solution.py:428
  10.1 2.5 %collective-permute-start.6 = (f32[24,512]{1,0:T(8,128)S(1)}, f32[24,512]{1,0:T(8,128)S(1)}, u32[]{:S(2)}, u32[]{:S(2)}) collective-permute-start(f32[24,512]{1,0:T(8,128)S(1)} %collective-permute-done.4.refs_5_), channel_id=1, source_target_pairs={{0,8},{8,0},{16,24},{24,16},{1,9},{9,1},{17,25},{25,17},{2,10},{10... | collective-permute-start | bytes 147464 | tf_op jit(solution)/shard_map/ppermute | solution.py:428
  12.1 1.2 %collective-permute-start.5 = (f32[24,512]{1,0:T(8,128)S(1)}, f32[24,512]{1,0:T(8,128)S(1)}, u32[]{:S(2)}, u32[]{:S(2)}) collective-permute-start(f32[24,512]{1,0:T(8,128)S(1)} %collective-permute-done.3.refs_4_), channel_id=1, source_target_pairs={{0,8},{8,0},{16,24},{24,16},{1,9},{9,1},{17,25},{25,17},{2,10},{10... | collective-permute-start | bytes 147464 | tf_op jit(solution)/shard_map/ppermute | solution.py:428
  12.6 1.2 %collective-permute-start.2 = (f32[24,512]{1,0:T(8,128)S(1)}, f32[24,512]{1,0:T(8,128)S(1)}, u32[]{:S(2)}, u32[]{:S(2)}) collective-permute-start(f32[24,512]{1,0:T(8,128)S(1)} %collective-permute-done.refs_1_), channel_id=1, source_target_pairs={{0,8},{8,0},{16,24},{24,16},{1,9},{9,1},{17,25},{25,17},{2,10},{10... | collective-permute-start | bytes 147464 | tf_op jit(solution)/shard_map/ppermute | solution.py:428
  15.2 5.9 %collective-permute-start.7 = (f32[24,512]{1,0:T(8,128)S(1)}, f32[24,512]{1,0:T(8,128)S(1)}, u32[]{:S(2)}, u32[]{:S(2)}) collective-permute-start(f32[24,512]{1,0:T(8,128)S(1)} %get-tuple-element.19), channel_id=1, source_target_pairs={{0,1},{1,2},{2,3},{3,0},{4,5},{5,6},{6,7},{7,4},{8,9},{9,10},{10,1... | collective-permute-start | bytes 147464 | tf_op jit(solution)/shard_map/ppermute | solution.py:428
  16.8 6.5 %collective-permute-start.8 = (f32[24,512]{1,0:T(8,128)S(1)}, f32[24,512]{1,0:T(8,128)S(1)}, u32[]{:S(2)}, u32[]{:S(2)}) collective-permute-start(f32[24,512]{1,0:T(8,128)S(1)} %get-tuple-element.20), channel_id=1, source_target_pairs={{0,2},{1,3},{2,0},{3,1},{4,6},{5,7},{6,4},{7,5},{8,10},{9,11},{10,... | collective-permute-start | bytes 147464 | tf_op jit(solution)/shard_map/ppermute | solution.py:428
  19.4 4.3 %collective-permute-start.9 = (f32[24,512]{1,0:T(8,128)S(1)}, f32[24,512]{1,0:T(8,128)S(1)}, u32[]{:S(2)}, u32[]{:S(2)}) collective-permute-start(f32[24,512]{1,0:T(8,128)S(1)} %get-tuple-element.21), channel_id=1, source_target_pairs={{0,3},{1,0},{2,1},{3,2},{4,7},{5,4},{6,5},{7,6},{8,11},{9,8},{10,9... | collective-permute-start | bytes 147464 | tf_op jit(solution)/shard_map/ppermute | solution.py:428

commit v6 on v5

--- a/solution.py
+++ b/solution.py
@@ -102,13 +102,27 @@
         self.points = tuple(v * c for v, c in zip(self.local, counts))
         self.xp = round_up(self.width[0], 8)
         self.zp = round_up(self.width[2], 8)
-        self.chunks = -(-self.width[1] // TERMS)
+        self.kept = self.width[1] - RIM // 2 if counts[1] <= 2 else self.width[1]
+        self.per = LANES // max(self.width[0], self.width[2])
+        self.step = LANES // self.per
+        self.chunks = -(-self.kept // self.per)
         self.lanes = self.chunks * LANES
         self.columns = nbins[0] * nbins[1]
         self.mid = self.counts[1] * self.lanes
         self.pair = 2 if counts[0] % 2 == 0 else 1
         assert self.columns * nbins[2] == LANES and nbins[2] == 8 and self.columns % 2 == 0
-        assert TERMS * self.zp <= LANES and self.width[0] <= SLOT
+        assert self.width[0] <= SLOT and max(self.width[0], self.width[2]) <= self.step
+
+    def first(self, device):
+        return RIM // 2 if self.counts[1] <= 2 and device == 0 else 0
+
+    def first_here(self):
+        if self.counts[1] > 2:
+            return 0
+        return jnp.where(lax.axis_index("gy") == 0, RIM // 2, 0)
+
+    def row(self, y):
+        return y // self.per * LANES + y % self.per * self.step
 
     def x_table(self):
         nx, width = self.counts[0], self.width[0]
@@ -132,15 +146,17 @@
         return (device // pair - shift) % (self.counts[0] // pair) * pair + (device % pair ^ other)
 
     def y_table(self):
-        ny, width = self.counts[1], self.width[1]
+        ny, kept = self.counts[1], self.kept
         m = windowed(self.points[1], ny)
-        table = np.zeros((ny, ny * width, self.chunks * TERMS, LANES), np.float32)
+        table = np.zeros((ny, ny * kept, self.chunks * self.per, LANES), np.float32)
         for d in range(ny):
             for o in range(ny):
+                source = (d - o) % ny
+                target_at, source_at = self.first(d), self.first(source)
                 for t in range(TERMS):
-                    block = m[t, d, :, (d - o) % ny, :]
-                    table[d, o * width : (o + 1) * width, :width, t * SLOT : (t + 1) * SLOT] = block.T[:, :, None]
-        return jnp.asarray(table.reshape(ny, ny * width * self.chunks * TERMS, LANES))
+                    block = m[t, d, target_at : target_at + kept, source, source_at : source_at + kept]
+                    table[d, o * kept : (o + 1) * kept, :kept, t * SLOT : (t + 1) * SLOT] = block.T[:, :, None]
+        return jnp.asarray(table.reshape(ny, ny * kept * self.chunks * self.per, LANES))
 
     def z_table(self):
         nz, width = self.counts[2], self.width[2]
@@ -261,14 +277,15 @@
         for a in range(1, nbx, 2):
             at = slice(y * xp + 4 * a, y * xp + 4 * a + 8)
             grid_s[at, :] = grid_s[at, :] + folded(a, y)
-    group = lax.broadcasted_iota(jnp.int32, (xp, LANES), 1) // plan.zp
+    group = lax.broadcasted_iota(jnp.int32, (xp, LANES), 1) // plan.step
+    first = plan.first_here()
     for chunk in range(plan.chunks):
         merged = jnp.zeros((xp, LANES), jnp.float32)
-        for b in range(TERMS):
-            y = chunk * TERMS + b
-            if y < plan.width[1]:
-                piece = grid_s[y * xp : (y + 1) * xp, :]
-                moved = pltpu.roll(piece, b * plan.zp, 1) if b else piece
+        for b in range(plan.per):
+            y = chunk * plan.per + b
+            if y < plan.kept:
+                piece = grid_s[pl.ds(pl.multiple_of((y + first) * xp, 8), xp), :]
+                moved = pltpu.roll(piece, b * plan.step, 1) if b else piece
                 merged = jnp.where(group == b, moved, merged)
         out_ref[:, chunk * LANES : (chunk + 1) * LANES] = merged
     for copy in copies[5:]:
@@ -283,31 +300,31 @@
     mid_s, term_s = refs[nx * ny + 3 + nz :]
     ytab_s = tables[1]
     x_matrix = tables[0][...]
-    wy = plan.width[1]
-    zp = plan.zp
-    span = plan.chunks * TERMS
+    kept, per, zp = plan.kept, plan.per, plan.zp
+    span = plan.chunks * per
+    mid_s[plan.mid : plan.mid + 8, :] = jnp.zeros((8, LANES), jnp.float32)
     for oy in range(ny):
         gathered = jnp.concatenate([blocks[ox * ny + oy][...] for ox in range(nx)], axis=0)
         both = lax.dot_general(
             split_rows(gathered), x_matrix, (((0,), (0,)), ((), ())), preferred_element_type=jnp.float32
         )
         mid_s[oy * plan.lanes : (oy + 1) * plan.lanes, :] = both[:, :LANES] + both[:, LANES:]
-    slot = lax.broadcasted_iota(jnp.int32, (zp, LANES), 1) // SLOT
+    group = lax.broadcasted_iota(jnp.int32, (zp, LANES), 1) // plan.step
     for chunk in range(plan.chunks):
-        sums = [jnp.zeros((zp, LANES), jnp.float32) for _ in range(TERMS)]
+        sums = [jnp.zeros((zp, LANES), jnp.float32) for _ in range(per)]
         for oy in range(ny):
-            for y in range(wy):
-                at = oy * plan.lanes + (y // TERMS) * LANES + (y % TERMS) * zp
+            for y in range(kept):
+                at = oy * plan.lanes + plan.row(y)
                 value = mid_s[at : at + zp, :]
-                for b in range(TERMS):
-                    row = (oy * wy + y) * span + chunk * TERMS + b
+                for b in range(per):
+                    row = (oy * kept + y) * span + chunk * per + b
                     sums[b] = sums[b] + value * ytab_s[row : row + 1, :]
         for t in range(TERMS):
             merged = jnp.zeros((zp, LANES), jnp.float32)
-            for b in range(TERMS):
-                shift = (SLOT * (b - t)) % LANES
+            for b in range(per):
+                shift = (plan.step * b - SLOT * t) % LANES
                 moved = pltpu.roll(sums[b], shift, 1) if shift else sums[b]
-                merged = jnp.where(slot == b, moved, merged)
+                merged = jnp.where(group == b, moved, merged)
             term_s[t * zp : (t + 1) * zp, chunk * LANES : (chunk + 1) * LANES] = merged
     both = jnp.dot(tables[2][...], split_rows(term_s[...]), preferred_element_type=jnp.float32)
     result = both[: nz * zp, :] + both[nz * zp :, :]
@@ -328,15 +345,25 @@
         total = total + part[...]
     for chunk in range(plan.chunks):
         field_s[chunk * LANES : (chunk + 1) * LANES, :zp] = total[:, chunk * LANES : (chunk + 1) * LANES].T
+    nothing = plan.lanes
+    field_s[nothing:, :] = jnp.zeros((field_s.shape[0] - nothing, LANES), jnp.float32)
+    first = plan.first_here()
+
+    def row_of(y):
+        if plan.counts[1] > 2:
+            return plan.row(y)
+        at_start = plan.row(y - RIM // 2) if y >= RIM // 2 else nothing
+        at_end = plan.row(y) if y < plan.kept else nothing
+        return jnp.where(first == 0, at_end, at_start)
+
+    rows_of = [row_of(y) for y in range(plan.width[1])]
     left = lax.broadcasted_iota(jnp.int32, (zp, LANES), 1) < 64
     for pair in range(plan.columns // 2):
         for half in range(2):
             a, b = divmod(2 * pair + half, nby)
             for j in range(8):
-                chunk, part = divmod(4 * b + j, TERMS)
-                at = chunk * LANES + part * SLOT + 4 * a
                 to = pair * LANES + half * 64 + j * 8
-                turned_s[to : to + 8, :] = field_s[at : at + 8, :]
+                turned_s[to : to + 8, :] = field_s[pl.ds(rows_of[4 * b + j] + 4 * a, 8), :]
         both = turned_s[pair * LANES : (pair + 1) * LANES, :zp].T
         turned = pltpu.roll(both, 64, 1)
         column_s[2 * pair * zp : (2 * pair + 1) * zp, :] = jnp.where(left, both, turned)
@@ -346,9 +373,7 @@
             2 : 2 + lz, chunk * LANES : (chunk + 1) * LANES
         ].T
     for y in range(ly):
-        chunk, b = divmod(y + 2, TERMS)
-        at = chunk * LANES + b * SLOT + 2
-        order_s[pl.ds(y, lx, stride=ly), :] = inner_s[at : at + lx, :]
+        order_s[pl.ds(y, lx, stride=ly), :] = inner_s[pl.ds(rows_of[y + 2] + 2, lx), :]
     for x in range(lx):
         fine_ref[x] = order_s[x * ly : (x + 1) * ly, :lz]
     copies = [pltpu.make_async_copy(fine_ref, fine_hbm, sems.at[0])]
@@ -450,7 +475,7 @@
         in_specs=[vmem] * (nx * ny + 3),
         out_specs=[vmem] * nz,
         scratch_shapes=[
-            pltpu.VMEM((plan.mid, LANES), f32),
+            pltpu.VMEM((plan.mid + 8, LANES), f32),
             pltpu.VMEM((TERMS * plan.zp, plan.lanes), f32),
         ],
         compiler_params=params,
@@ -468,7 +493,7 @@
         in_specs=[vmem] * (nz + 2),
         out_specs=[hbm, hbm],
         scratch_shapes=[
-            pltpu.VMEM((plan.lanes, LANES), f32),
+            pltpu.VMEM((plan.lanes + plan.xp, LANES), f32),
             pltpu.VMEM((plan.columns * plan.zp, LANES), f32),
             pltpu.VMEM((plan.columns * 64, LANES), f32),
             pltpu.VMEM((plan.lanes, LANES), f32),

time: 25.7 us -> 25.4 us (0.988)
  waiting for transfers between devices: 8.08 us -> 7.63 us
    ppermute x10, waiting for transfers between devices: 8.08 us -> 7.63 us  [moved(): return near(lax.ppermute(value, axis, pairs))]
where the time goes in v6:
time: 25.4 us; the launch traced here: 25.2 us
  starting transfers between devices  10.2 us (40%)
  waiting for transfers between devices  7.63 us (30%)
  Pallas kernels  6.72 us (26%)
  between operations  0.66 us (3%)
    ppermute x10, starting transfers between devices, moved(): return near(lax.ppermute(value, axis, pairs))  10.2 us
    ppermute x10, waiting for transfers between devices, moved(): return near(lax.ppermute(value, axis, pairs))  7.63 us
    pallas_call x1, Pallas kernels, body(): pl.pallas_call(functools.partial(spread_kernel, plan), out_shape=[pltpu.V...  3.44 us
    pallas_call x1, Pallas kernels, body(): pl.pallas_call(functools.partial(gather_kernel, plan), out_shape=[jax.Sha...  1.82 us
    pallas_call x1, Pallas kernels, body(): pl.pallas_call(functools.partial(solve_kernel, plan), out_shape=[pltpu.VM...  1.46 us
  transfers between devices with their start and end apart: 10, of which 8 were waited for; matrix products, arithmetic and copies ran while one was open for 0% of the time, Pallas kernels for 0%

profile of v6, /device:TPU:0, one launch (start us, length us, event | category | flops | bytes accessed | tf_op | source)
XLA Modules:
  0.0 25.2 jit_solution(3786344274559233919)
XLA Ops:
  0.6 3.4 %spread.1 = (f32[24,384]{1,0:T(8,128)S(1)}, bf16[64,128,256]{2,1,0:T(8,128)(2,1)S(1)}, f32[128,8,128]{2,1,0:T(8,128)S(1)}, bf16[192,256]{1,0:T(8,128)(2,1)S(1)},...) custom-call(f32[128,128]{1,0:T(8,128)} %bitcast.5, f32[128,128]{1,0:T(8,128)} %bitcast.6, f32[128,128]{1,0:T(8,128)} %bitcast.7, ...), custom_call_target="tpu_custom_call" | custom-call | tf_op jit(solution)/shard_map/spread/pallas_call | solution.py:426
  4.1 4.0 %collective-permute-start.4 = (f32[24,384]{1,0:T(8,128)S(1)}, f32[24,384]{1,0:T(8,128)S(1)}, u32[]{:S(2)}, u32[]{:S(2)}) collective-permute-start(f32[24,384]{1,0:T(8,128)S(1)} %get-tuple-element.14.refs_0_), channel_id=1, source_target_pairs={{0,20},{4,16},{8,28},{12,24},{16,4},{20,0},{24,12},{28,8},{1,21},{... | collective-permute-start | bytes 110600 | tf_op jit(solution)/shard_map/ppermute | solution.py:453
  8.1 0.5 %collective-permute-start.3 = (f32[24,384]{1,0:T(8,128)S(1)}, f32[24,384]{1,0:T(8,128)S(1)}, u32[]{:S(2)}, u32[]{:S(2)}) collective-permute-start(f32[24,384]{1,0:T(8,128)S(1)} %get-tuple-element.14.refs_0_), channel_id=1, source_target_pairs={{0,16},{4,20},{8,24},{12,28},{16,0},{20,4},{24,8},{28,12},{1,17},{... | collective-permute-start | bytes 110600 | tf_op jit(solution)/shard_map/ppermute | solution.py:453
  8.6 0.1 collective-permute-start
  8.7 0.0 collective-permute-start.1
  8.7 1.3 %collective-permute-done.4.refs_5_ = f32[24,384]{1,0:T(8,128)S(1)} collective-permute-done((f32[24,384]{1,0:T(8,128)S(1)}, f32[24,384]{1,0:T(8,128)S(1)}, u32[]{:S(2)}, u32[]{:S(2)}) %collective-permute-start.4) | collective-permute-done | bytes 36896 | tf_op jit(solution)/shard_map/ppermute | solution.py:453
  10.0 0.0 collective-permute-start.6
  10.0 2.0 %collective-permute-done.3.refs_4_ = f32[24,384]{1,0:T(8,128)S(1)} collective-permute-done((f32[24,384]{1,0:T(8,128)S(1)}, f32[24,384]{1,0:T(8,128)S(1)}, u32[]{:S(2)}, u32[]{:S(2)}) %collective-permute-start.3) | collective-permute-done | bytes 36896 | tf_op jit(solution)/shard_map/ppermute | solution.py:453
  12.0 0.0 collective-permute-start.5
  12.0 0.5 %collective-permute-done.refs_1_ = f32[24,384]{1,0:T(8,128)S(1)} collective-permute-done((f32[24,384]{1,0:T(8,128)S(1)}, f32[24,384]{1,0:T(8,128)S(1)}, u32[]{:S(2)}, u32[]{:S(2)}) %collective-permute-start) | collective-permute-done | bytes 36896 | tf_op jit(solution)/shard_map/ppermute | solution.py:453
  12.5 0.0 collective-permute-start.2
  12.5 0.0 collective-permute-done.1.refs_2_
  12.5 0.0 collective-permute-done.6.refs_7_
  12.5 0.7 %collective-permute-done.5.refs_6_ = f32[24,384]{1,0:T(8,128)S(1)} collective-permute-done((f32[24,384]{1,0:T(8,128)S(1)}, f32[24,384]{1,0:T(8,128)S(1)}, u32[]{:S(2)}, u32[]{:S(2)}) %collective-permute-start.5) | collective-permute-done | bytes 36896 | tf_op jit(solution)/shard_map/ppermute | solution.py:453
  13.2 0.5 %collective-permute-done.2.refs_3_ = f32[24,384]{1,0:T(8,128)S(1)} collective-permute-done((f32[24,384]{1,0:T(8,128)S(1)}, f32[24,384]{1,0:T(8,128)S(1)}, u32[]{:S(2)}, u32[]{:S(2)}) %collective-permute-start.2) | collective-permute-done | bytes 36896 | tf_op jit(solution)/shard_map/ppermute | solution.py:453
  13.7 1.5 %solve.1 = (f32[24,384]{1,0:T(8,128)S(1)}, f32[24,384]{1,0:T(8,128)S(1)}, f32[24,384]{1,0:T(8,128)S(1)}, f32[24,384]{1,0:T(8,128)S(1)}) custom-call(f32[24,384]{1,0:T(8,128)S(1)} %get-tuple-element.14.refs_0_, f32[24,384]{1,0:T(8,128)S(1)} %collective-permute-done.refs_1_, f32[24,384]{1,0:T(8,128)S(1)} %collective-permute-done.1.refs_2_, ...), custom_call_target="tpu_custom_call" | custom-call | tf_op jit(solution)/shard_map/solve/pallas_call | solution.py:472
  15.2 1.6 %collective-permute-start.7 = (f32[24,384]{1,0:T(8,128)S(1)}, f32[24,384]{1,0:T(8,128)S(1)}, u32[]{:S(2)}, u32[]{:S(2)}) collective-permute-start(f32[24,384]{1,0:T(8,128)S(1)} %get-tuple-element.19), channel_id=1, source_target_pairs={{0,1},{1,2},{2,3},{3,0},{4,5},{5,6},{6,7},{7,4},{8,9},{9,10},{10,1... | collective-permute-start | bytes 110600 | tf_op jit(solution)/shard_map/ppermute | solution.py:453
  16.8 2.6 %collective-permute-start.8 = (f32[24,384]{1,0:T(8,128)S(1)}, f32[24,384]{1,0:T(8,128)S(1)}, u32[]{:S(2)}, u32[]{:S(2)}) collective-permute-start(f32[24,384]{1,0:T(8,128)S(1)} %get-tuple-element.20), channel_id=1, source_target_pairs={{0,2},{1,3},{2,0},{3,1},{4,6},{5,7},{6,4},{7,5},{8,10},{9,11},{10,... | collective-permute-start | bytes 110600 | tf_op jit(solution)/shard_map/ppermute | solution.py:453
  19.4 1.3 %collective-permute-start.9 = (f32[24,384]{1,0:T(8,128)S(1)}, f32[24,384]{1,0:T(8,128)S(1)}, u32[]{:S(2)}, u32[]{:S(2)}) collective-permute-start(f32[24,384]{1,0:T(8,128)S(1)} %get-tuple-element.21), channel_id=1, source_target_pairs={{0,3},{1,0},{2,1},{3,2},{4,7},{5,4},{6,5},{7,6},{8,11},{9,8},{10,9... | collective-permute-start | bytes 110600 | tf_op jit(solution)/shard_map/ppermute | solution.py:453
  20.8 0.2 collective-permute-done.7.refs_1_
  21.0 1.4 %collective-permute-done.8.refs_2_ = f32[24,384]{1,0:T(8,128)S(1)} collective-permute-done((f32[24,384]{1,0:T(8,128)S(1)}, f32[24,384]{1,0:T(8,128)S(1)}, u32[]{:S(2)}, u32[]{:S(2)}) %collective-permute-start.8) | collective-permute-done | bytes 36896 | tf_op jit(solution)/shard_map/ppermute | solution.py:453
  22.4 1.0 %collective-permute-done.9.refs_3_ = f32[24,384]{1,0:T(8,128)S(1)} collective-permute-done((f32[24,384]{1,0:T(8,128)S(1)}, f32[24,384]{1,0:T(8,128)S(1)}, u32[]{:S(2)}, u32[]{:S(2)}) %collective-permute-start.9) | collective-permute-done | bytes 36896 | tf_op jit(solution)/shard_map/ppermute | solution.py:453
  23.4 1.8 %gather.1 = (f32[16,16,16]{2,1,0:T(8,128)}, f32[128,128]{1,0:T(8,128)}) custom-call(f32[24,384]{1,0:T(8,128)S(1)} %get-tuple-element.18.refs_0_, f32[24,384]{1,0:T(8,128)S(1)} %collective-permute-done.7.refs_1_, f32[24,384]{1,0:T(8,128)S(1)} %collective-permute-done.8.refs_2_, f32[24,384]{1,0:T(8,128)S(1)} %collective-permute-done.9.refs_3_, ...), custom_call_target="tpu_custom_call" | custom-call | tf_op jit(solution)/shard_map/gather/pallas_call | solution.py:487
Async XLA Ops:
  4.1 5.9 %collective-permute-start.4 = (f32[24,384]{1,0:T(8,128)S(1)}, f32[24,384]{1,0:T(8,128)S(1)}, u32[]{:S(2)}, u32[]{:S(2)}) collective-permute-start(f32[24,384]{1,0:T(8,128)S(1)} %get-tuple-element.14.refs_0_), channel_id=1, source_target_pairs={{0,20},{4,16},{8,28},{12,24},{16,4},{20,0},{24,12},{28,8},{1,21},{... | collective-permute-start | bytes 110600 | tf_op jit(solution)/shard_map/ppermute | solution.py:453
  8.1 4.0 %collective-permute-start.3 = (f32[24,384]{1,0:T(8,128)S(1)}, f32[24,384]{1,0:T(8,128)S(1)}, u32[]{:S(2)}, u32[]{:S(2)}) collective-permute-start(f32[24,384]{1,0:T(8,128)S(1)} %get-tuple-element.14.refs_0_), channel_id=1, source_target_pairs={{0,16},{4,20},{8,24},{12,28},{16,0},{20,4},{24,8},{28,12},{1,17},{... | collective-permute-start | bytes 110600 | tf_op jit(solution)/shard_map/ppermute | solution.py:453
  8.6 4.0 %collective-permute-start = (f32[24,384]{1,0:T(8,128)S(1)}, f32[24,384]{1,0:T(8,128)S(1)}, u32[]{:S(2)}, u32[]{:S(2)}) collective-permute-start(f32[24,384]{1,0:T(8,128)S(1)} %get-tuple-element.14.refs_0_), channel_id=1, source_target_pairs={{0,4},{4,0},{8,12},{12,8},{16,20},{20,16},{24,28},{28,24},{1,5},{5... | collective-permute-start | bytes 110600 | tf_op jit(solution)/shard_map/ppermute | solution.py:453
  8.7 3.8 %collective-permute-start.1 = (f32[24,384]{1,0:T(8,128)S(1)}, f32[24,384]{1,0:T(8,128)S(1)}, u32[]{:S(2)}, u32[]{:S(2)}) collective-permute-start(f32[24,384]{1,0:T(8,128)S(1)} %get-tuple-element.14.refs_0_), channel_id=1, source_target_pairs={{0,8},{8,0},{16,24},{24,16},{1,9},{9,1},{17,25},{25,17},{2,10},{10... | collective-permute-start | bytes 110600 | tf_op jit(solution)/shard_map/ppermute | solution.py:453
  10.0 2.5 %collective-permute-start.6 = (f32[24,384]{1,0:T(8,128)S(1)}, f32[24,384]{1,0:T(8,128)S(1)}, u32[]{:S(2)}, u32[]{:S(2)}) collective-permute-start(f32[24,384]{1,0:T(8,128)S(1)} %collective-permute-done.4.refs_5_), channel_id=1, source_target_pairs={{0,8},{8,0},{16,24},{24,16},{1,9},{9,1},{17,25},{25,17},{2,10},{10... | collective-permute-start | bytes 110600 | tf_op jit(solution)/shard_map/ppermute | solution.py:453
  12.0 1.2 %collective-permute-start.5 = (f32[24,384]{1,0:T(8,128)S(1)}, f32[24,384]{1,0:T(8,128)S(1)}, u32[]{:S(2)}, u32[]{:S(2)}) collective-permute-start(f32[24,384]{1,0:T(8,128)S(1)} %collective-permute-done.3.refs_4_), channel_id=1, source_target_pairs={{0,8},{8,0},{16,24},{24,16},{1,9},{9,1},{17,25},{25,17},{2,10},{10... | collective-permute-start | bytes 110600 | tf_op jit(solution)/shard_map/ppermute | solution.py:453
  12.5 1.2 %collective-permute-start.2 = (f32[24,384]{1,0:T(8,128)S(1)}, f32[24,384]{1,0:T(8,128)S(1)}, u32[]{:S(2)}, u32[]{:S(2)}) collective-permute-start(f32[24,384]{1,0:T(8,128)S(1)} %collective-permute-done.refs_1_), channel_id=1, source_target_pairs={{0,8},{8,0},{16,24},{24,16},{1,9},{9,1},{17,25},{25,17},{2,10},{10... | collective-permute-start | bytes 110600 | tf_op jit(solution)/shard_map/ppermute | solution.py:453
  15.2 5.8 %collective-permute-start.7 = (f32[24,384]{1,0:T(8,128)S(1)}, f32[24,384]{1,0:T(8,128)S(1)}, u32[]{:S(2)}, u32[]{:S(2)}) collective-permute-start(f32[24,384]{1,0:T(8,128)S(1)} %get-tuple-element.19), channel_id=1, source_target_pairs={{0,1},{1,2},{2,3},{3,0},{4,5},{5,6},{6,7},{7,4},{8,9},{9,10},{10,1... | collective-permute-start | bytes 110600 | tf_op jit(solution)/shard_map/ppermute | solution.py:453
  16.8 5.6 %collective-permute-start.8 = (f32[24,384]{1,0:T(8,128)S(1)}, f32[24,384]{1,0:T(8,128)S(1)}, u32[]{:S(2)}, u32[]{:S(2)}) collective-permute-start(f32[24,384]{1,0:T(8,128)S(1)} %get-tuple-element.20), channel_id=1, source_target_pairs={{0,2},{1,3},{2,0},{3,1},{4,6},{5,7},{6,4},{7,5},{8,10},{9,11},{10,... | collective-permute-start | bytes 110600 | tf_op jit(solution)/shard_map/ppermute | solution.py:453
  19.4 4.0 %collective-permute-start.9 = (f32[24,384]{1,0:T(8,128)S(1)}, f32[24,384]{1,0:T(8,128)S(1)}, u32[]{:S(2)}, u32[]{:S(2)}) collective-permute-start(f32[24,384]{1,0:T(8,128)S(1)} %get-tuple-element.21), channel_id=1, source_target_pairs={{0,3},{1,0},{2,1},{3,2},{4,7},{5,4},{6,5},{7,6},{8,11},{9,8},{10,9... | collective-permute-start | bytes 110600 | tf_op jit(solution)/shard_map/ppermute | solution.py:453

commit v7 on v6

--- a/solution.py
+++ b/solution.py
@@ -216,12 +216,10 @@
         weight_y = bspline(y_ref[pl.ds(r, 1), :] + node)
         weight_z = bspline(z_ref[pl.ds(r, 1), :] + node)
         weight_z = jnp.where(slot < counts_ref[p // nby, p % nby, c], weight_z, 0.0)
-        outer = split_rows(
-            jnp.concatenate([weight_y[j : j + 1, :] * weight_x for j in range(8)], axis=0)
-        )
+        outer = jnp.concatenate([weight_y[j : j + 1, :] * weight_x for j in range(8)], axis=0)
         outer_s[r // 2, :, (c % 2) * slots : (c % 2 + 1) * slots] = outer
         along_z_s[r] = weight_z
-        return outer, split_rows(weight_z * charge_ref[pl.ds(r, 1), :])
+        return split_rows(outer), split_rows(weight_z * charge_ref[pl.ds(r, 1), :])
 
     def one_column(p):
         sums = [jnp.zeros((8, LANES), jnp.float32) for _ in range(zp // 8)]
@@ -387,7 +385,7 @@
                 split_rows(column_s[p * zp + 2 * n : p * zp + 2 * n + 8, :]) for n in (c, c + 1)
             ]
             both = jnp.dot(
-                jnp.concatenate(patches, axis=0), outer_s[(p * nbz + c) // 2],
+                jnp.concatenate(patches, axis=0), split_rows(outer_s[(p * nbz + c) // 2]),
                 preferred_element_type=jnp.float32,
             )
             for n in range(2):
@@ -427,7 +425,7 @@
         functools.partial(spread_kernel, plan),
         out_shape=[
             pltpu.VMEM((plan.xp, plan.lanes), f32),
-            pltpu.VMEM((LANES // 2, LANES, 2 * slots), jnp.bfloat16),
+            pltpu.VMEM((LANES // 2, 64, 2 * slots), f32),
             pltpu.VMEM((LANES, 8, slots), f32),
         ]
         + [pltpu.VMEM(t.shape[1:], t.dtype) for t in tables],

time: 25.4 us -> 25.1 us (0.988)
  Pallas kernels: 6.72 us -> 6.46 us
    pallas_call x1, Pallas kernels: 3.44 us -> 3.14 us  [body(): pl.pallas_call(functools.partial(spread_kernel, plan), out_shape=[pltpu.V...]
where the time goes in v7:
time: 25.1 us; the launch traced here: 24.9 us
  starting transfers between devices  10.2 us (41%)
  waiting for transfers between devices  7.63 us (30%)
  Pallas kernels  6.46 us (26%)
  between operations  0.66 us (3%)
    ppermute x10, starting transfers between devices, moved(): return near(lax.ppermute(value, axis, pairs))  10.2 us
    ppermute x10, waiting for transfers between devices, moved(): return near(lax.ppermute(value, axis, pairs))  7.63 us
    pallas_call x1, Pallas kernels, body(): pl.pallas_call(functools.partial(spread_kernel, plan), out_shape=[pltpu.V...  3.14 us
    pallas_call x1, Pallas kernels, body(): pl.pallas_call(functools.partial(gather_kernel, plan), out_shape=[jax.Sha...  1.85 us
    pallas_call x1, Pallas kernels, body(): pl.pallas_call(functools.partial(solve_kernel, plan), out_shape=[pltpu.VM...  1.46 us
  transfers between devices with their start and end apart: 10, of which 8 were waited for; matrix products, arithmetic and copies ran while one was open for 0% of the time, Pallas kernels for 0%

profile of v7, /device:TPU:0, one launch (start us, length us, event | category | flops | bytes accessed | tf_op | source)
XLA Modules:
  0.0 24.9 jit_solution(11351490380866487844)
XLA Ops:
  0.6 3.1 %spread.1 = (f32[24,384]{1,0:T(8,128)S(1)}, f32[64,64,256]{2,1,0:T(8,128)S(1)}, f32[128,8,128]{2,1,0:T(8,128)S(1)}, bf16[192,256]{1,0:T(8,128)(2,1)S(1)}, f32[64...) custom-call(f32[128,128]{1,0:T(8,128)} %bitcast.5, f32[128,128]{1,0:T(8,128)} %bitcast.6, f32[128,128]{1,0:T(8,128)} %bitcast.7, ...), custom_call_target="tpu_custom_call" | custom-call | tf_op jit(solution)/shard_map/spread/pallas_call | solution.py:424
  3.8 4.0 %collective-permute-start.4 = (f32[24,384]{1,0:T(8,128)S(1)}, f32[24,384]{1,0:T(8,128)S(1)}, u32[]{:S(2)}, u32[]{:S(2)}) collective-permute-start(f32[24,384]{1,0:T(8,128)S(1)} %get-tuple-element.14.refs_0_), channel_id=1, source_target_pairs={{0,20},{4,16},{8,28},{12,24},{16,4},{20,0},{24,12},{28,8},{1,21},{... | collective-permute-start | bytes 110600 | tf_op jit(solution)/shard_map/ppermute | solution.py:451
  7.8 0.5 %collective-permute-start.3 = (f32[24,384]{1,0:T(8,128)S(1)}, f32[24,384]{1,0:T(8,128)S(1)}, u32[]{:S(2)}, u32[]{:S(2)}) collective-permute-start(f32[24,384]{1,0:T(8,128)S(1)} %get-tuple-element.14.refs_0_), channel_id=1, source_target_pairs={{0,16},{4,20},{8,24},{12,28},{16,0},{20,4},{24,8},{28,12},{1,17},{... | collective-permute-start | bytes 110600 | tf_op jit(solution)/shard_map/ppermute | solution.py:451
  8.3 0.1 collective-permute-start
  8.4 0.0 collective-permute-start.1
  8.4 1.3 %collective-permute-done.4.refs_5_ = f32[24,384]{1,0:T(8,128)S(1)} collective-permute-done((f32[24,384]{1,0:T(8,128)S(1)}, f32[24,384]{1,0:T(8,128)S(1)}, u32[]{:S(2)}, u32[]{:S(2)}) %collective-permute-start.4) | collective-permute-done | bytes 36896 | tf_op jit(solution)/shard_map/ppermute | solution.py:451
  9.7 0.0 collective-permute-start.6
  9.7 2.0 %collective-permute-done.3.refs_4_ = f32[24,384]{1,0:T(8,128)S(1)} collective-permute-done((f32[24,384]{1,0:T(8,128)S(1)}, f32[24,384]{1,0:T(8,128)S(1)}, u32[]{:S(2)}, u32[]{:S(2)}) %collective-permute-start.3) | collective-permute-done | bytes 36896 | tf_op jit(solution)/shard_map/ppermute | solution.py:451
  11.7 0.0 collective-permute-start.5
  11.7 0.5 %collective-permute-done.refs_1_ = f32[24,384]{1,0:T(8,128)S(1)} collective-permute-done((f32[24,384]{1,0:T(8,128)S(1)}, f32[24,384]{1,0:T(8,128)S(1)}, u32[]{:S(2)}, u32[]{:S(2)}) %collective-permute-start) | collective-permute-done | bytes 36896 | tf_op jit(solution)/shard_map/ppermute | solution.py:451
  12.2 0.0 collective-permute-start.2
  12.2 0.0 collective-permute-done.1.refs_2_
  12.2 0.0 collective-permute-done.6.refs_7_
  12.2 0.7 %collective-permute-done.5.refs_6_ = f32[24,384]{1,0:T(8,128)S(1)} collective-permute-done((f32[24,384]{1,0:T(8,128)S(1)}, f32[24,384]{1,0:T(8,128)S(1)}, u32[]{:S(2)}, u32[]{:S(2)}) %collective-permute-start.5) | collective-permute-done | bytes 36896 | tf_op jit(solution)/shard_map/ppermute | solution.py:451
  12.9 0.5 %collective-permute-done.2.refs_3_ = f32[24,384]{1,0:T(8,128)S(1)} collective-permute-done((f32[24,384]{1,0:T(8,128)S(1)}, f32[24,384]{1,0:T(8,128)S(1)}, u32[]{:S(2)}, u32[]{:S(2)}) %collective-permute-start.2) | collective-permute-done | bytes 36896 | tf_op jit(solution)/shard_map/ppermute | solution.py:451
  13.4 1.5 %solve.1 = (f32[24,384]{1,0:T(8,128)S(1)}, f32[24,384]{1,0:T(8,128)S(1)}, f32[24,384]{1,0:T(8,128)S(1)}, f32[24,384]{1,0:T(8,128)S(1)}) custom-call(f32[24,384]{1,0:T(8,128)S(1)} %get-tuple-element.14.refs_0_, f32[24,384]{1,0:T(8,128)S(1)} %collective-permute-done.refs_1_, f32[24,384]{1,0:T(8,128)S(1)} %collective-permute-done.1.refs_2_, ...), custom_call_target="tpu_custom_call" | custom-call | tf_op jit(solution)/shard_map/solve/pallas_call | solution.py:470
  14.9 1.6 %collective-permute-start.7 = (f32[24,384]{1,0:T(8,128)S(1)}, f32[24,384]{1,0:T(8,128)S(1)}, u32[]{:S(2)}, u32[]{:S(2)}) collective-permute-start(f32[24,384]{1,0:T(8,128)S(1)} %get-tuple-element.19), channel_id=1, source_target_pairs={{0,1},{1,2},{2,3},{3,0},{4,5},{5,6},{6,7},{7,4},{8,9},{9,10},{10,1... | collective-permute-start | bytes 110600 | tf_op jit(solution)/shard_map/ppermute | solution.py:451
  16.5 2.6 %collective-permute-start.8 = (f32[24,384]{1,0:T(8,128)S(1)}, f32[24,384]{1,0:T(8,128)S(1)}, u32[]{:S(2)}, u32[]{:S(2)}) collective-permute-start(f32[24,384]{1,0:T(8,128)S(1)} %get-tuple-element.20), channel_id=1, source_target_pairs={{0,2},{1,3},{2,0},{3,1},{4,6},{5,7},{6,4},{7,5},{8,10},{9,11},{10,... | collective-permute-start | bytes 110600 | tf_op jit(solution)/shard_map/ppermute | solution.py:451
  19.1 1.3 %collective-permute-start.9 = (f32[24,384]{1,0:T(8,128)S(1)}, f32[24,384]{1,0:T(8,128)S(1)}, u32[]{:S(2)}, u32[]{:S(2)}) collective-permute-start(f32[24,384]{1,0:T(8,128)S(1)} %get-tuple-element.21), channel_id=1, source_target_pairs={{0,3},{1,0},{2,1},{3,2},{4,7},{5,4},{6,5},{7,6},{8,11},{9,8},{10,9... | collective-permute-start | bytes 110600 | tf_op jit(solution)/shard_map/ppermute | solution.py:451
  20.5 0.3 %collective-permute-done.7.refs_1_ = f32[24,384]{1,0:T(8,128)S(1)} collective-permute-done((f32[24,384]{1,0:T(8,128)S(1)}, f32[24,384]{1,0:T(8,128)S(1)}, u32[]{:S(2)}, u32[]{:S(2)}) %collective-permute-start.7) | collective-permute-done | bytes 36896 | tf_op jit(solution)/shard_map/ppermute | solution.py:451
  20.7 1.4 %collective-permute-done.8.refs_2_ = f32[24,384]{1,0:T(8,128)S(1)} collective-permute-done((f32[24,384]{1,0:T(8,128)S(1)}, f32[24,384]{1,0:T(8,128)S(1)}, u32[]{:S(2)}, u32[]{:S(2)}) %collective-permute-start.8) | collective-permute-done | bytes 36896 | tf_op jit(solution)/shard_map/ppermute | solution.py:451
  22.1 1.0 %collective-permute-done.9.refs_3_ = f32[24,384]{1,0:T(8,128)S(1)} collective-permute-done((f32[24,384]{1,0:T(8,128)S(1)}, f32[24,384]{1,0:T(8,128)S(1)}, u32[]{:S(2)}, u32[]{:S(2)}) %collective-permute-start.9) | collective-permute-done | bytes 36896 | tf_op jit(solution)/shard_map/ppermute | solution.py:451
  23.1 1.9 %gather.1 = (f32[16,16,16]{2,1,0:T(8,128)}, f32[128,128]{1,0:T(8,128)}) custom-call(f32[24,384]{1,0:T(8,128)S(1)} %get-tuple-element.18.refs_0_, f32[24,384]{1,0:T(8,128)S(1)} %collective-permute-done.7.refs_1_, f32[24,384]{1,0:T(8,128)S(1)} %collective-permute-done.8.refs_2_, f32[24,384]{1,0:T(8,128)S(1)} %collective-permute-done.9.refs_3_, ...), custom_call_target="tpu_custom_call" | custom-call | tf_op jit(solution)/shard_map/gather/pallas_call | solution.py:485
Async XLA Ops:
  3.8 5.9 %collective-permute-start.4 = (f32[24,384]{1,0:T(8,128)S(1)}, f32[24,384]{1,0:T(8,128)S(1)}, u32[]{:S(2)}, u32[]{:S(2)}) collective-permute-start(f32[24,384]{1,0:T(8,128)S(1)} %get-tuple-element.14.refs_0_), channel_id=1, source_target_pairs={{0,20},{4,16},{8,28},{12,24},{16,4},{20,0},{24,12},{28,8},{1,21},{... | collective-permute-start | bytes 110600 | tf_op jit(solution)/shard_map/ppermute | solution.py:451
  7.8 4.0 %collective-permute-start.3 = (f32[24,384]{1,0:T(8,128)S(1)}, f32[24,384]{1,0:T(8,128)S(1)}, u32[]{:S(2)}, u32[]{:S(2)}) collective-permute-start(f32[24,384]{1,0:T(8,128)S(1)} %get-tuple-element.14.refs_0_), channel_id=1, source_target_pairs={{0,16},{4,20},{8,24},{12,28},{16,0},{20,4},{24,8},{28,12},{1,17},{... | collective-permute-start | bytes 110600 | tf_op jit(solution)/shard_map/ppermute | solution.py:451
  8.3 4.0 %collective-permute-start = (f32[24,384]{1,0:T(8,128)S(1)}, f32[24,384]{1,0:T(8,128)S(1)}, u32[]{:S(2)}, u32[]{:S(2)}) collective-permute-start(f32[24,384]{1,0:T(8,128)S(1)} %get-tuple-element.14.refs_0_), channel_id=1, source_target_pairs={{0,4},{4,0},{8,12},{12,8},{16,20},{20,16},{24,28},{28,24},{1,5},{5... | collective-permute-start | bytes 110600 | tf_op jit(solution)/shard_map/ppermute | solution.py:451
  8.4 3.8 %collective-permute-start.1 = (f32[24,384]{1,0:T(8,128)S(1)}, f32[24,384]{1,0:T(8,128)S(1)}, u32[]{:S(2)}, u32[]{:S(2)}) collective-permute-start(f32[24,384]{1,0:T(8,128)S(1)} %get-tuple-element.14.refs_0_), channel_id=1, source_target_pairs={{0,8},{8,0},{16,24},{24,16},{1,9},{9,1},{17,25},{25,17},{2,10},{10... | collective-permute-start | bytes 110600 | tf_op jit(solution)/shard_map/ppermute | solution.py:451
  9.7 2.5 %collective-permute-start.6 = (f32[24,384]{1,0:T(8,128)S(1)}, f32[24,384]{1,0:T(8,128)S(1)}, u32[]{:S(2)}, u32[]{:S(2)}) collective-permute-start(f32[24,384]{1,0:T(8,128)S(1)} %collective-permute-done.4.refs_5_), channel_id=1, source_target_pairs={{0,8},{8,0},{16,24},{24,16},{1,9},{9,1},{17,25},{25,17},{2,10},{10... | collective-permute-start | bytes 110600 | tf_op jit(solution)/shard_map/ppermute | solution.py:451
  11.7 1.2 %collective-permute-start.5 = (f32[24,384]{1,0:T(8,128)S(1)}, f32[24,384]{1,0:T(8,128)S(1)}, u32[]{:S(2)}, u32[]{:S(2)}) collective-permute-start(f32[24,384]{1,0:T(8,128)S(1)} %collective-permute-done.3.refs_4_), channel_id=1, source_target_pairs={{0,8},{8,0},{16,24},{24,16},{1,9},{9,1},{17,25},{25,17},{2,10},{10... | collective-permute-start | bytes 110600 | tf_op jit(solution)/shard_map/ppermute | solution.py:451
  12.2 1.2 %collective-permute-start.2 = (f32[24,384]{1,0:T(8,128)S(1)}, f32[24,384]{1,0:T(8,128)S(1)}, u32[]{:S(2)}, u32[]{:S(2)}) collective-permute-start(f32[24,384]{1,0:T(8,128)S(1)} %collective-permute-done.refs_1_), channel_id=1, source_target_pairs={{0,8},{8,0},{16,24},{24,16},{1,9},{9,1},{17,25},{25,17},{2,10},{10... | collective-permute-start | bytes 110600 | tf_op jit(solution)/shard_map/ppermute | solution.py:451
  14.9 5.8 %collective-permute-start.7 = (f32[24,384]{1,0:T(8,128)S(1)}, f32[24,384]{1,0:T(8,128)S(1)}, u32[]{:S(2)}, u32[]{:S(2)}) collective-permute-start(f32[24,384]{1,0:T(8,128)S(1)} %get-tuple-element.19), channel_id=1, source_target_pairs={{0,1},{1,2},{2,3},{3,0},{4,5},{5,6},{6,7},{7,4},{8,9},{9,10},{10,1... | collective-permute-start | bytes 110600 | tf_op jit(solution)/shard_map/ppermute | solution.py:451
  16.5 5.6 %collective-permute-start.8 = (f32[24,384]{1,0:T(8,128)S(1)}, f32[24,384]{1,0:T(8,128)S(1)}, u32[]{:S(2)}, u32[]{:S(2)}) collective-permute-start(f32[24,384]{1,0:T(8,128)S(1)} %get-tuple-element.20), channel_id=1, source_target_pairs={{0,2},{1,3},{2,0},{3,1},{4,6},{5,7},{6,4},{7,5},{8,10},{9,11},{10,... | collective-permute-start | bytes 110600 | tf_op jit(solution)/shard_map/ppermute | solution.py:451
  19.1 4.0 %collective-permute-start.9 = (f32[24,384]{1,0:T(8,128)S(1)}, f32[24,384]{1,0:T(8,128)S(1)}, u32[]{:S(2)}, u32[]{:S(2)}) collective-permute-start(f32[24,384]{1,0:T(8,128)S(1)} %get-tuple-element.21), channel_id=1, source_target_pairs={{0,3},{1,0},{2,1},{3,2},{4,7},{5,4},{6,5},{7,6},{8,11},{9,8},{10,9... | collective-permute-start | bytes 110600 | tf_op jit(solution)/shard_map/ppermute | solution.py:451

commit v8 on v7

--- a/solution.py
+++ b/solution.py
@@ -13,7 +13,7 @@
 LANES = 128
 TERMS = 5
 SLOT = LANES // TERMS
-PARTS = 4
+PARTS = 2
 RIM = 4
 TAPS = (-0.0625, 0.0, 0.5625, 1.0, 0.5625, 0.0, -0.0625)
 highest = lax.Precision.HIGHEST
@@ -192,7 +192,7 @@
 
 def spread_kernel(plan, *refs):
     hbm, tables, (out_ref, outer_s, along_z_s) = refs[:5], refs[5:8], refs[8:11]
-    tables_out, local, (column_s, turned_s, grid_s, sems) = refs[11:14], refs[14:19], refs[19:]
+    tables_out, local, (column_s, turned_s, grid_s, along_y_s, sems) = refs[11:14], refs[14:19], refs[19:]
     copies = [pltpu.make_async_copy(a, b, sems.at[n]) for n, (a, b) in enumerate(zip(hbm, local))]
     for n, (table, target, axis) in enumerate(zip(tables, tables_out, ("gx", "gy", "gz"))):
         copies.append(pltpu.make_async_copy(table.at[lax.axis_index(axis)], target, sems.at[5 + n]))
@@ -216,7 +216,10 @@
         weight_y = bspline(y_ref[pl.ds(r, 1), :] + node)
         weight_z = bspline(z_ref[pl.ds(r, 1), :] + node)
         weight_z = jnp.where(slot < counts_ref[p // nby, p % nby, c], weight_z, 0.0)
-        outer = jnp.concatenate([weight_y[j : j + 1, :] * weight_x for j in range(8)], axis=0)
+        along_y_s[r * 8 : (r + 1) * 8, :] = weight_y
+        outer = jnp.concatenate(
+            [along_y_s[pl.ds(r * 8 + j, 8, stride=0), :] * weight_x for j in range(8)], axis=0
+        )
         outer_s[r // 2, :, (c % 2) * slots : (c % 2 + 1) * slots] = outer
         along_z_s[r] = weight_z
         return split_rows(outer), split_rows(weight_z * charge_ref[pl.ds(r, 1), :])
@@ -437,6 +440,7 @@
             pltpu.VMEM((plan.columns // 2 * plan.zp, LANES), f32),
             pltpu.VMEM((plan.columns * 64, LANES), f32),
             pltpu.VMEM((plan.width[1] * plan.xp, LANES), f32),
+            pltpu.VMEM((LANES * 8, slots), f32),
             pltpu.SemaphoreType.DMA((8,)),
         ],
         compiler_params=params,

time: 25.1 us -> 25.1 us (level)
  no operation moved by 1% of the time
where the time goes in v8:
time: 25.1 us; the launch traced here: 25 us
  starting transfers between devices  10.2 us (41%)
  waiting for transfers between devices  7.62 us (30%)
  Pallas kernels  6.47 us (26%)
  between operations  0.66 us (3%)
    ppermute x10, starting transfers between devices, moved(): return near(lax.ppermute(value, axis, pairs))  10.2 us
    ppermute x10, waiting for transfers between devices, moved(): return near(lax.ppermute(value, axis, pairs))  7.62 us
    pallas_call x1, Pallas kernels, body(): pl.pallas_call(functools.partial(spread_kernel, plan), out_shape=[pltpu.V...  3.18 us
    pallas_call x1, Pallas kernels, body(): pl.pallas_call(functools.partial(gather_kernel, plan), out_shape=[jax.Sha...  1.84 us
    pallas_call x1, Pallas kernels, body(): pl.pallas_call(functools.partial(solve_kernel, plan), out_shape=[pltpu.VM...  1.46 us
  transfers between devices with their start and end apart: 10, of which 8 were waited for; matrix products, arithmetic and copies ran while one was open for 0% of the time, Pallas kernels for 0%

profile of v8, /device:TPU:0, one launch (start us, length us, event | category | flops | bytes accessed | tf_op | source)
XLA Modules:
  0.0 25.0 jit_solution(16130967410899989029)
XLA Ops:
  0.6 3.2 %spread.1 = (f32[24,384]{1,0:T(8,128)S(1)}, f32[64,64,256]{2,1,0:T(8,128)S(1)}, f32[128,8,128]{2,1,0:T(8,128)S(1)}, bf16[192,256]{1,0:T(8,128)(2,1)S(1)}, f32[64...) custom-call(f32[128,128]{1,0:T(8,128)} %bitcast.5, f32[128,128]{1,0:T(8,128)} %bitcast.6, f32[128,128]{1,0:T(8,128)} %bitcast.7, ...), custom_call_target="tpu_custom_call" | custom-call | tf_op jit(solution)/shard_map/spread/pallas_call | solution.py:427
  3.8 4.0 %collective-permute-start.4 = (f32[24,384]{1,0:T(8,128)S(1)}, f32[24,384]{1,0:T(8,128)S(1)}, u32[]{:S(2)}, u32[]{:S(2)}) collective-permute-start(f32[24,384]{1,0:T(8,128)S(1)} %get-tuple-element.14.refs_0_), channel_id=1, source_target_pairs={{0,20},{4,16},{8,28},{12,24},{16,4},{20,0},{24,12},{28,8},{1,21},{... | collective-permute-start | bytes 110600 | tf_op jit(solution)/shard_map/ppermute | solution.py:455
  7.8 0.5 %collective-permute-start.3 = (f32[24,384]{1,0:T(8,128)S(1)}, f32[24,384]{1,0:T(8,128)S(1)}, u32[]{:S(2)}, u32[]{:S(2)}) collective-permute-start(f32[24,384]{1,0:T(8,128)S(1)} %get-tuple-element.14.refs_0_), channel_id=1, source_target_pairs={{0,16},{4,20},{8,24},{12,28},{16,0},{20,4},{24,8},{28,12},{1,17},{... | collective-permute-start | bytes 110600 | tf_op jit(solution)/shard_map/ppermute | solution.py:455
  8.3 0.1 collective-permute-start
  8.4 0.0 collective-permute-start.1
  8.4 1.3 %collective-permute-done.4.refs_5_ = f32[24,384]{1,0:T(8,128)S(1)} collective-permute-done((f32[24,384]{1,0:T(8,128)S(1)}, f32[24,384]{1,0:T(8,128)S(1)}, u32[]{:S(2)}, u32[]{:S(2)}) %collective-permute-start.4) | collective-permute-done | bytes 36896 | tf_op jit(solution)/shard_map/ppermute | solution.py:455
  9.7 0.0 collective-permute-start.6
  9.7 2.0 %collective-permute-done.3.refs_4_ = f32[24,384]{1,0:T(8,128)S(1)} collective-permute-done((f32[24,384]{1,0:T(8,128)S(1)}, f32[24,384]{1,0:T(8,128)S(1)}, u32[]{:S(2)}, u32[]{:S(2)}) %collective-permute-start.3) | collective-permute-done | bytes 36896 | tf_op jit(solution)/shard_map/ppermute | solution.py:455
  11.8 0.0 collective-permute-start.5
  11.8 0.5 %collective-permute-done.refs_1_ = f32[24,384]{1,0:T(8,128)S(1)} collective-permute-done((f32[24,384]{1,0:T(8,128)S(1)}, f32[24,384]{1,0:T(8,128)S(1)}, u32[]{:S(2)}, u32[]{:S(2)}) %collective-permute-start) | collective-permute-done | bytes 36896 | tf_op jit(solution)/shard_map/ppermute | solution.py:455
  12.3 0.0 collective-permute-start.2
  12.3 0.0 collective-permute-done.1.refs_2_
  12.3 0.0 collective-permute-done.6.refs_7_
  12.3 0.7 %collective-permute-done.5.refs_6_ = f32[24,384]{1,0:T(8,128)S(1)} collective-permute-done((f32[24,384]{1,0:T(8,128)S(1)}, f32[24,384]{1,0:T(8,128)S(1)}, u32[]{:S(2)}, u32[]{:S(2)}) %collective-permute-start.5) | collective-permute-done | bytes 36896 | tf_op jit(solution)/shard_map/ppermute | solution.py:455
  13.0 0.5 %collective-permute-done.2.refs_3_ = f32[24,384]{1,0:T(8,128)S(1)} collective-permute-done((f32[24,384]{1,0:T(8,128)S(1)}, f32[24,384]{1,0:T(8,128)S(1)}, u32[]{:S(2)}, u32[]{:S(2)}) %collective-permute-start.2) | collective-permute-done | bytes 36896 | tf_op jit(solution)/shard_map/ppermute | solution.py:455
  13.5 1.5 %solve.1 = (f32[24,384]{1,0:T(8,128)S(1)}, f32[24,384]{1,0:T(8,128)S(1)}, f32[24,384]{1,0:T(8,128)S(1)}, f32[24,384]{1,0:T(8,128)S(1)}) custom-call(f32[24,384]{1,0:T(8,128)S(1)} %get-tuple-element.14.refs_0_, f32[24,384]{1,0:T(8,128)S(1)} %collective-permute-done.refs_1_, f32[24,384]{1,0:T(8,128)S(1)} %collective-permute-done.1.refs_2_, ...), custom_call_target="tpu_custom_call" | custom-call | tf_op jit(solution)/shard_map/solve/pallas_call | solution.py:474
  14.9 1.6 %collective-permute-start.7 = (f32[24,384]{1,0:T(8,128)S(1)}, f32[24,384]{1,0:T(8,128)S(1)}, u32[]{:S(2)}, u32[]{:S(2)}) collective-permute-start(f32[24,384]{1,0:T(8,128)S(1)} %get-tuple-element.19), channel_id=1, source_target_pairs={{0,1},{1,2},{2,3},{3,0},{4,5},{5,6},{6,7},{7,4},{8,9},{9,10},{10,1... | collective-permute-start | bytes 110600 | tf_op jit(solution)/shard_map/ppermute | solution.py:455
  16.6 2.6 %collective-permute-start.8 = (f32[24,384]{1,0:T(8,128)S(1)}, f32[24,384]{1,0:T(8,128)S(1)}, u32[]{:S(2)}, u32[]{:S(2)}) collective-permute-start(f32[24,384]{1,0:T(8,128)S(1)} %get-tuple-element.20), channel_id=1, source_target_pairs={{0,2},{1,3},{2,0},{3,1},{4,6},{5,7},{6,4},{7,5},{8,10},{9,11},{10,... | collective-permute-start | bytes 110600 | tf_op jit(solution)/shard_map/ppermute | solution.py:455
  19.2 1.3 %collective-permute-start.9 = (f32[24,384]{1,0:T(8,128)S(1)}, f32[24,384]{1,0:T(8,128)S(1)}, u32[]{:S(2)}, u32[]{:S(2)}) collective-permute-start(f32[24,384]{1,0:T(8,128)S(1)} %get-tuple-element.21), channel_id=1, source_target_pairs={{0,3},{1,0},{2,1},{3,2},{4,7},{5,4},{6,5},{7,6},{8,11},{9,8},{10,9... | collective-permute-start | bytes 110600 | tf_op jit(solution)/shard_map/ppermute | solution.py:455
  20.5 0.2 collective-permute-done.7.refs_1_
  20.8 1.4 %collective-permute-done.8.refs_2_ = f32[24,384]{1,0:T(8,128)S(1)} collective-permute-done((f32[24,384]{1,0:T(8,128)S(1)}, f32[24,384]{1,0:T(8,128)S(1)}, u32[]{:S(2)}, u32[]{:S(2)}) %collective-permute-start.8) | collective-permute-done | bytes 36896 | tf_op jit(solution)/shard_map/ppermute | solution.py:455
  22.2 1.0 %collective-permute-done.9.refs_3_ = f32[24,384]{1,0:T(8,128)S(1)} collective-permute-done((f32[24,384]{1,0:T(8,128)S(1)}, f32[24,384]{1,0:T(8,128)S(1)}, u32[]{:S(2)}, u32[]{:S(2)}) %collective-permute-start.9) | collective-permute-done | bytes 36896 | tf_op jit(solution)/shard_map/ppermute | solution.py:455
  23.1 1.8 %gather.1 = (f32[16,16,16]{2,1,0:T(8,128)}, f32[128,128]{1,0:T(8,128)}) custom-call(f32[24,384]{1,0:T(8,128)S(1)} %get-tuple-element.18.refs_0_, f32[24,384]{1,0:T(8,128)S(1)} %collective-permute-done.7.refs_1_, f32[24,384]{1,0:T(8,128)S(1)} %collective-permute-done.8.refs_2_, f32[24,384]{1,0:T(8,128)S(1)} %collective-permute-done.9.refs_3_, ...), custom_call_target="tpu_custom_call" | custom-call | tf_op jit(solution)/shard_map/gather/pallas_call | solution.py:489
Async XLA Ops:
  3.8 5.9 %collective-permute-start.4 = (f32[24,384]{1,0:T(8,128)S(1)}, f32[24,384]{1,0:T(8,128)S(1)}, u32[]{:S(2)}, u32[]{:S(2)}) collective-permute-start(f32[24,384]{1,0:T(8,128)S(1)} %get-tuple-element.14.refs_0_), channel_id=1, source_target_pairs={{0,20},{4,16},{8,28},{12,24},{16,4},{20,0},{24,12},{28,8},{1,21},{... | collective-permute-start | bytes 110600 | tf_op jit(solution)/shard_map/ppermute | solution.py:455
  7.8 4.0 %collective-permute-start.3 = (f32[24,384]{1,0:T(8,128)S(1)}, f32[24,384]{1,0:T(8,128)S(1)}, u32[]{:S(2)}, u32[]{:S(2)}) collective-permute-start(f32[24,384]{1,0:T(8,128)S(1)} %get-tuple-element.14.refs_0_), channel_id=1, source_target_pairs={{0,16},{4,20},{8,24},{12,28},{16,0},{20,4},{24,8},{28,12},{1,17},{... | collective-permute-start | bytes 110600 | tf_op jit(solution)/shard_map/ppermute | solution.py:455
  8.3 4.0 %collective-permute-start = (f32[24,384]{1,0:T(8,128)S(1)}, f32[24,384]{1,0:T(8,128)S(1)}, u32[]{:S(2)}, u32[]{:S(2)}) collective-permute-start(f32[24,384]{1,0:T(8,128)S(1)} %get-tuple-element.14.refs_0_), channel_id=1, source_target_pairs={{0,4},{4,0},{8,12},{12,8},{16,20},{20,16},{24,28},{28,24},{1,5},{5... | collective-permute-start | bytes 110600 | tf_op jit(solution)/shard_map/ppermute | solution.py:455
  8.4 3.8 %collective-permute-start.1 = (f32[24,384]{1,0:T(8,128)S(1)}, f32[24,384]{1,0:T(8,128)S(1)}, u32[]{:S(2)}, u32[]{:S(2)}) collective-permute-start(f32[24,384]{1,0:T(8,128)S(1)} %get-tuple-element.14.refs_0_), channel_id=1, source_target_pairs={{0,8},{8,0},{16,24},{24,16},{1,9},{9,1},{17,25},{25,17},{2,10},{10... | collective-permute-start | bytes 110600 | tf_op jit(solution)/shard_map/ppermute | solution.py:455
  9.7 2.5 %collective-permute-start.6 = (f32[24,384]{1,0:T(8,128)S(1)}, f32[24,384]{1,0:T(8,128)S(1)}, u32[]{:S(2)}, u32[]{:S(2)}) collective-permute-start(f32[24,384]{1,0:T(8,128)S(1)} %collective-permute-done.4.refs_5_), channel_id=1, source_target_pairs={{0,8},{8,0},{16,24},{24,16},{1,9},{9,1},{17,25},{25,17},{2,10},{10... | collective-permute-start | bytes 110600 | tf_op jit(solution)/shard_map/ppermute | solution.py:455
  11.8 1.2 %collective-permute-start.5 = (f32[24,384]{1,0:T(8,128)S(1)}, f32[24,384]{1,0:T(8,128)S(1)}, u32[]{:S(2)}, u32[]{:S(2)}) collective-permute-start(f32[24,384]{1,0:T(8,128)S(1)} %collective-permute-done.3.refs_4_), channel_id=1, source_target_pairs={{0,8},{8,0},{16,24},{24,16},{1,9},{9,1},{17,25},{25,17},{2,10},{10... | collective-permute-start | bytes 110600 | tf_op jit(solution)/shard_map/ppermute | solution.py:455
  12.3 1.2 %collective-permute-start.2 = (f32[24,384]{1,0:T(8,128)S(1)}, f32[24,384]{1,0:T(8,128)S(1)}, u32[]{:S(2)}, u32[]{:S(2)}) collective-permute-start(f32[24,384]{1,0:T(8,128)S(1)} %collective-permute-done.refs_1_), channel_id=1, source_target_pairs={{0,8},{8,0},{16,24},{24,16},{1,9},{9,1},{17,25},{25,17},{2,10},{10... | collective-permute-start | bytes 110600 | tf_op jit(solution)/shard_map/ppermute | solution.py:455
  14.9 5.8 %collective-permute-start.7 = (f32[24,384]{1,0:T(8,128)S(1)}, f32[24,384]{1,0:T(8,128)S(1)}, u32[]{:S(2)}, u32[]{:S(2)}) collective-permute-start(f32[24,384]{1,0:T(8,128)S(1)} %get-tuple-element.19), channel_id=1, source_target_pairs={{0,1},{1,2},{2,3},{3,0},{4,5},{5,6},{6,7},{7,4},{8,9},{9,10},{10,1... | collective-permute-start | bytes 110600 | tf_op jit(solution)/shard_map/ppermute | solution.py:455
  16.6 5.6 %collective-permute-start.8 = (f32[24,384]{1,0:T(8,128)S(1)}, f32[24,384]{1,0:T(8,128)S(1)}, u32[]{:S(2)}, u32[]{:S(2)}) collective-permute-start(f32[24,384]{1,0:T(8,128)S(1)} %get-tuple-element.20), channel_id=1, source_target_pairs={{0,2},{1,3},{2,0},{3,1},{4,6},{5,7},{6,4},{7,5},{8,10},{9,11},{10,... | collective-permute-start | bytes 110600 | tf_op jit(solution)/shard_map/ppermute | solution.py:455
  19.2 4.0 %collective-permute-start.9 = (f32[24,384]{1,0:T(8,128)S(1)}, f32[24,384]{1,0:T(8,128)S(1)}, u32[]{:S(2)}, u32[]{:S(2)}) collective-permute-start(f32[24,384]{1,0:T(8,128)S(1)} %get-tuple-element.21), channel_id=1, source_target_pairs={{0,3},{1,0},{2,1},{3,2},{4,7},{5,4},{6,5},{7,6},{8,11},{9,8},{10,9... | collective-permute-start | bytes 110600 | tf_op jit(solution)/shard_map/ppermute | solution.py:455

commit v9 on v8

--- a/solution.py
+++ b/solution.py
@@ -440,7 +440,7 @@
             pltpu.VMEM((plan.columns // 2 * plan.zp, LANES), f32),
             pltpu.VMEM((plan.columns * 64, LANES), f32),
             pltpu.VMEM((plan.width[1] * plan.xp, LANES), f32),
-            pltpu.VMEM((LANES * 8, slots), f32),
+            pltpu.VMEM((LANES * 8 + 8, slots), f32),
             pltpu.SemaphoreType.DMA((8,)),
         ],
         compiler_params=params,

time: 25.1 us -> 25.1 us (level)
  no operation moved by 1% of the time
where the time goes in v9:
time: 25.1 us; the launch traced here: 25 us
  starting transfers between devices  10.2 us (41%)
  waiting for transfers between devices  7.62 us (30%)
  Pallas kernels  6.48 us (26%)
  between operations  0.66 us (3%)
    ppermute x10, starting transfers between devices, moved(): return near(lax.ppermute(value, axis, pairs))  10.2 us
    ppermute x10, waiting for transfers between devices, moved(): return near(lax.ppermute(value, axis, pairs))  7.62 us
    pallas_call x1, Pallas kernels, body(): pl.pallas_call(functools.partial(spread_kernel, plan), out_shape=[pltpu.V...  3.18 us
    pallas_call x1, Pallas kernels, body(): pl.pallas_call(functools.partial(gather_kernel, plan), out_shape=[jax.Sha...  1.84 us
    pallas_call x1, Pallas kernels, body(): pl.pallas_call(functools.partial(solve_kernel, plan), out_shape=[pltpu.VM...  1.46 us
  transfers between devices with their start and end apart: 10, of which 8 were waited for; matrix products, arithmetic and copies ran while one was open for 0% of the time, Pallas kernels for 0%

profile of v9, /device:TPU:0, one launch (start us, length us, event | category | flops | bytes accessed | tf_op | source)
XLA Modules:
  0.0 25.0 jit_solution(13067034514518977961)
XLA Ops:
  0.6 3.2 %spread.1 = (f32[24,384]{1,0:T(8,128)S(1)}, f32[64,64,256]{2,1,0:T(8,128)S(1)}, f32[128,8,128]{2,1,0:T(8,128)S(1)}, bf16[192,256]{1,0:T(8,128)(2,1)S(1)}, f32[64...) custom-call(f32[128,128]{1,0:T(8,128)} %bitcast.5, f32[128,128]{1,0:T(8,128)} %bitcast.6, f32[128,128]{1,0:T(8,128)} %bitcast.7, ...), custom_call_target="tpu_custom_call" | custom-call | tf_op jit(solution)/shard_map/spread/pallas_call | solution.py:427
  3.8 4.0 %collective-permute-start.4 = (f32[24,384]{1,0:T(8,128)S(1)}, f32[24,384]{1,0:T(8,128)S(1)}, u32[]{:S(2)}, u32[]{:S(2)}) collective-permute-start(f32[24,384]{1,0:T(8,128)S(1)} %get-tuple-element.14.refs_0_), channel_id=1, source_target_pairs={{0,20},{4,16},{8,28},{12,24},{16,4},{20,0},{24,12},{28,8},{1,21},{... | collective-permute-start | bytes 110600 | tf_op jit(solution)/shard_map/ppermute | solution.py:455
  7.8 0.5 %collective-permute-start.3 = (f32[24,384]{1,0:T(8,128)S(1)}, f32[24,384]{1,0:T(8,128)S(1)}, u32[]{:S(2)}, u32[]{:S(2)}) collective-permute-start(f32[24,384]{1,0:T(8,128)S(1)} %get-tuple-element.14.refs_0_), channel_id=1, source_target_pairs={{0,16},{4,20},{8,24},{12,28},{16,0},{20,4},{24,8},{28,12},{1,17},{... | collective-permute-start | bytes 110600 | tf_op jit(solution)/shard_map/ppermute | solution.py:455
  8.3 0.1 collective-permute-start
  8.4 0.0 collective-permute-start.1
  8.4 1.3 %collective-permute-done.4.refs_5_ = f32[24,384]{1,0:T(8,128)S(1)} collective-permute-done((f32[24,384]{1,0:T(8,128)S(1)}, f32[24,384]{1,0:T(8,128)S(1)}, u32[]{:S(2)}, u32[]{:S(2)}) %collective-permute-start.4) | collective-permute-done | bytes 36896 | tf_op jit(solution)/shard_map/ppermute | solution.py:455
  9.7 0.0 collective-permute-start.6
  9.7 2.0 %collective-permute-done.3.refs_4_ = f32[24,384]{1,0:T(8,128)S(1)} collective-permute-done((f32[24,384]{1,0:T(8,128)S(1)}, f32[24,384]{1,0:T(8,128)S(1)}, u32[]{:S(2)}, u32[]{:S(2)}) %collective-permute-start.3) | collective-permute-done | bytes 36896 | tf_op jit(solution)/shard_map/ppermute | solution.py:455
  11.8 0.0 collective-permute-start.5
  11.8 0.5 %collective-permute-done.refs_1_ = f32[24,384]{1,0:T(8,128)S(1)} collective-permute-done((f32[24,384]{1,0:T(8,128)S(1)}, f32[24,384]{1,0:T(8,128)S(1)}, u32[]{:S(2)}, u32[]{:S(2)}) %collective-permute-start) | collective-permute-done | bytes 36896 | tf_op jit(solution)/shard_map/ppermute | solution.py:455
  12.3 0.0 collective-permute-start.2
  12.3 0.0 collective-permute-done.1.refs_2_
  12.3 0.0 collective-permute-done.6.refs_7_
  12.3 0.7 %collective-permute-done.5.refs_6_ = f32[24,384]{1,0:T(8,128)S(1)} collective-permute-done((f32[24,384]{1,0:T(8,128)S(1)}, f32[24,384]{1,0:T(8,128)S(1)}, u32[]{:S(2)}, u32[]{:S(2)}) %collective-permute-start.5) | collective-permute-done | bytes 36896 | tf_op jit(solution)/shard_map/ppermute | solution.py:455
  13.0 0.5 %collective-permute-done.2.refs_3_ = f32[24,384]{1,0:T(8,128)S(1)} collective-permute-done((f32[24,384]{1,0:T(8,128)S(1)}, f32[24,384]{1,0:T(8,128)S(1)}, u32[]{:S(2)}, u32[]{:S(2)}) %collective-permute-start.2) | collective-permute-done | bytes 36896 | tf_op jit(solution)/shard_map/ppermute | solution.py:455
  13.5 1.5 %solve.1 = (f32[24,384]{1,0:T(8,128)S(1)}, f32[24,384]{1,0:T(8,128)S(1)}, f32[24,384]{1,0:T(8,128)S(1)}, f32[24,384]{1,0:T(8,128)S(1)}) custom-call(f32[24,384]{1,0:T(8,128)S(1)} %get-tuple-element.14.refs_0_, f32[24,384]{1,0:T(8,128)S(1)} %collective-permute-done.refs_1_, f32[24,384]{1,0:T(8,128)S(1)} %collective-permute-done.1.refs_2_, ...), custom_call_target="tpu_custom_call" | custom-call | tf_op jit(solution)/shard_map/solve/pallas_call | solution.py:474
  15.0 1.6 %collective-permute-start.7 = (f32[24,384]{1,0:T(8,128)S(1)}, f32[24,384]{1,0:T(8,128)S(1)}, u32[]{:S(2)}, u32[]{:S(2)}) collective-permute-start(f32[24,384]{1,0:T(8,128)S(1)} %get-tuple-element.19), channel_id=1, source_target_pairs={{0,1},{1,2},{2,3},{3,0},{4,5},{5,6},{6,7},{7,4},{8,9},{9,10},{10,1... | collective-permute-start | bytes 110600 | tf_op jit(solution)/shard_map/ppermute | solution.py:455
  16.6 2.6 %collective-permute-start.8 = (f32[24,384]{1,0:T(8,128)S(1)}, f32[24,384]{1,0:T(8,128)S(1)}, u32[]{:S(2)}, u32[]{:S(2)}) collective-permute-start(f32[24,384]{1,0:T(8,128)S(1)} %get-tuple-element.20), channel_id=1, source_target_pairs={{0,2},{1,3},{2,0},{3,1},{4,6},{5,7},{6,4},{7,5},{8,10},{9,11},{10,... | collective-permute-start | bytes 110600 | tf_op jit(solution)/shard_map/ppermute | solution.py:455
  19.2 1.3 %collective-permute-start.9 = (f32[24,384]{1,0:T(8,128)S(1)}, f32[24,384]{1,0:T(8,128)S(1)}, u32[]{:S(2)}, u32[]{:S(2)}) collective-permute-start(f32[24,384]{1,0:T(8,128)S(1)} %get-tuple-element.21), channel_id=1, source_target_pairs={{0,3},{1,0},{2,1},{3,2},{4,7},{5,4},{6,5},{7,6},{8,11},{9,8},{10,9... | collective-permute-start | bytes 110600 | tf_op jit(solution)/shard_map/ppermute | solution.py:455
  20.5 0.2 %collective-permute-done.7.refs_1_ = f32[24,384]{1,0:T(8,128)S(1)} collective-permute-done((f32[24,384]{1,0:T(8,128)S(1)}, f32[24,384]{1,0:T(8,128)S(1)}, u32[]{:S(2)}, u32[]{:S(2)}) %collective-permute-start.7) | collective-permute-done | bytes 36896 | tf_op jit(solution)/shard_map/ppermute | solution.py:455
  20.8 1.4 %collective-permute-done.8.refs_2_ = f32[24,384]{1,0:T(8,128)S(1)} collective-permute-done((f32[24,384]{1,0:T(8,128)S(1)}, f32[24,384]{1,0:T(8,128)S(1)}, u32[]{:S(2)}, u32[]{:S(2)}) %collective-permute-start.8) | collective-permute-done | bytes 36896 | tf_op jit(solution)/shard_map/ppermute | solution.py:455
  22.2 1.0 %collective-permute-done.9.refs_3_ = f32[24,384]{1,0:T(8,128)S(1)} collective-permute-done((f32[24,384]{1,0:T(8,128)S(1)}, f32[24,384]{1,0:T(8,128)S(1)}, u32[]{:S(2)}, u32[]{:S(2)}) %collective-permute-start.9) | collective-permute-done | bytes 36896 | tf_op jit(solution)/shard_map/ppermute | solution.py:455
  23.1 1.8 %gather.1 = (f32[16,16,16]{2,1,0:T(8,128)}, f32[128,128]{1,0:T(8,128)}) custom-call(f32[24,384]{1,0:T(8,128)S(1)} %get-tuple-element.18.refs_0_, f32[24,384]{1,0:T(8,128)S(1)} %collective-permute-done.7.refs_1_, f32[24,384]{1,0:T(8,128)S(1)} %collective-permute-done.8.refs_2_, f32[24,384]{1,0:T(8,128)S(1)} %collective-permute-done.9.refs_3_, ...), custom_call_target="tpu_custom_call" | custom-call | tf_op jit(solution)/shard_map/gather/pallas_call | solution.py:489
Async XLA Ops:
  3.8 5.9 %collective-permute-start.4 = (f32[24,384]{1,0:T(8,128)S(1)}, f32[24,384]{1,0:T(8,128)S(1)}, u32[]{:S(2)}, u32[]{:S(2)}) collective-permute-start(f32[24,384]{1,0:T(8,128)S(1)} %get-tuple-element.14.refs_0_), channel_id=1, source_target_pairs={{0,20},{4,16},{8,28},{12,24},{16,4},{20,0},{24,12},{28,8},{1,21},{... | collective-permute-start | bytes 110600 | tf_op jit(solution)/shard_map/ppermute | solution.py:455
  7.8 4.0 %collective-permute-start.3 = (f32[24,384]{1,0:T(8,128)S(1)}, f32[24,384]{1,0:T(8,128)S(1)}, u32[]{:S(2)}, u32[]{:S(2)}) collective-permute-start(f32[24,384]{1,0:T(8,128)S(1)} %get-tuple-element.14.refs_0_), channel_id=1, source_target_pairs={{0,16},{4,20},{8,24},{12,28},{16,0},{20,4},{24,8},{28,12},{1,17},{... | collective-permute-start | bytes 110600 | tf_op jit(solution)/shard_map/ppermute | solution.py:455
  8.3 4.0 %collective-permute-start = (f32[24,384]{1,0:T(8,128)S(1)}, f32[24,384]{1,0:T(8,128)S(1)}, u32[]{:S(2)}, u32[]{:S(2)}) collective-permute-start(f32[24,384]{1,0:T(8,128)S(1)} %get-tuple-element.14.refs_0_), channel_id=1, source_target_pairs={{0,4},{4,0},{8,12},{12,8},{16,20},{20,16},{24,28},{28,24},{1,5},{5... | collective-permute-start | bytes 110600 | tf_op jit(solution)/shard_map/ppermute | solution.py:455
  8.4 3.8 %collective-permute-start.1 = (f32[24,384]{1,0:T(8,128)S(1)}, f32[24,384]{1,0:T(8,128)S(1)}, u32[]{:S(2)}, u32[]{:S(2)}) collective-permute-start(f32[24,384]{1,0:T(8,128)S(1)} %get-tuple-element.14.refs_0_), channel_id=1, source_target_pairs={{0,8},{8,0},{16,24},{24,16},{1,9},{9,1},{17,25},{25,17},{2,10},{10... | collective-permute-start | bytes 110600 | tf_op jit(solution)/shard_map/ppermute | solution.py:455
  9.7 2.5 %collective-permute-start.6 = (f32[24,384]{1,0:T(8,128)S(1)}, f32[24,384]{1,0:T(8,128)S(1)}, u32[]{:S(2)}, u32[]{:S(2)}) collective-permute-start(f32[24,384]{1,0:T(8,128)S(1)} %collective-permute-done.4.refs_5_), channel_id=1, source_target_pairs={{0,8},{8,0},{16,24},{24,16},{1,9},{9,1},{17,25},{25,17},{2,10},{10... | collective-permute-start | bytes 110600 | tf_op jit(solution)/shard_map/ppermute | solution.py:455
  11.8 1.2 %collective-permute-start.5 = (f32[24,384]{1,0:T(8,128)S(1)}, f32[24,384]{1,0:T(8,128)S(1)}, u32[]{:S(2)}, u32[]{:S(2)}) collective-permute-start(f32[24,384]{1,0:T(8,128)S(1)} %collective-permute-done.3.refs_4_), channel_id=1, source_target_pairs={{0,8},{8,0},{16,24},{24,16},{1,9},{9,1},{17,25},{25,17},{2,10},{10... | collective-permute-start | bytes 110600 | tf_op jit(solution)/shard_map/ppermute | solution.py:455
  12.3 1.2 %collective-permute-start.2 = (f32[24,384]{1,0:T(8,128)S(1)}, f32[24,384]{1,0:T(8,128)S(1)}, u32[]{:S(2)}, u32[]{:S(2)}) collective-permute-start(f32[24,384]{1,0:T(8,128)S(1)} %collective-permute-done.refs_1_), channel_id=1, source_target_pairs={{0,8},{8,0},{16,24},{24,16},{1,9},{9,1},{17,25},{25,17},{2,10},{10... | collective-permute-start | bytes 110600 | tf_op jit(solution)/shard_map/ppermute | solution.py:455
  15.0 5.8 %collective-permute-start.7 = (f32[24,384]{1,0:T(8,128)S(1)}, f32[24,384]{1,0:T(8,128)S(1)}, u32[]{:S(2)}, u32[]{:S(2)}) collective-permute-start(f32[24,384]{1,0:T(8,128)S(1)} %get-tuple-element.19), channel_id=1, source_target_pairs={{0,1},{1,2},{2,3},{3,0},{4,5},{5,6},{6,7},{7,4},{8,9},{9,10},{10,1... | collective-permute-start | bytes 110600 | tf_op jit(solution)/shard_map/ppermute | solution.py:455
  16.6 5.6 %collective-permute-start.8 = (f32[24,384]{1,0:T(8,128)S(1)}, f32[24,384]{1,0:T(8,128)S(1)}, u32[]{:S(2)}, u32[]{:S(2)}) collective-permute-start(f32[24,384]{1,0:T(8,128)S(1)} %get-tuple-element.20), channel_id=1, source_target_pairs={{0,2},{1,3},{2,0},{3,1},{4,6},{5,7},{6,4},{7,5},{8,10},{9,11},{10,... | collective-permute-start | bytes 110600 | tf_op jit(solution)/shard_map/ppermute | solution.py:455
  19.2 4.0 %collective-permute-start.9 = (f32[24,384]{1,0:T(8,128)S(1)}, f32[24,384]{1,0:T(8,128)S(1)}, u32[]{:S(2)}, u32[]{:S(2)}) collective-permute-start(f32[24,384]{1,0:T(8,128)S(1)} %get-tuple-element.21), channel_id=1, source_target_pairs={{0,3},{1,0},{2,1},{3,2},{4,7},{5,4},{6,5},{7,6},{8,11},{9,8},{10,9... | collective-permute-start | bytes 110600 | tf_op jit(solution)/shard_map/ppermute | solution.py:455
